TPU v7x, 512 devices: a whole 4x8x8 slice. The times are simulated.
512 devices in a mesh: scen: 64 (over y, x, core), col: 8 (over z).
Axes of the slice: x: 4, y: 8, z: 8, core: 2. Of those that a mesh axis runs over, the one named last changes fastest.
Arguments:
- adaptive_matrices: bfloat16 [128, 512, 8192], P('scen', None, 'col'), may hold values from -0.0625 to 0.0625
- barrier_ratios: bfloat16 [128, 8192], P('scen', 'col'), may hold values from 0.099609375 to 10
- damping_shift: bfloat16 [128, 512], P('scen'), may hold values from 0.5 to 2
- coupler_matrices: bfloat16 [128, 512, 512], P('scen'), may hold values from -0.25 to 0.25
- constraint_bounds: bfloat16 [128, 512], P('scen'), may hold values from -12 to 12
- leading_main_entries: float32 [512], replicated, may hold values from 1 to 8
- leading_source_vector: float32 [512], replicated, may hold values from -24 to 24
- outcome_tallies: int32 [64], replicated, may hold values from 0 to 2, as said below
Outputs:
- first_dir: float32 [512], replicated
- multiplier_update: float32 [128, 512], P('scen')
- adaptive_update: float32 [128, 8192], P('scen', 'col')
Inputs may be any that keep to these rules, and one draw needn't show every extreme that they name: `outcome_tallies`: in each aligned block of four consecutive groups the counts sum to 2, a group holding 2 is followed by a group holding 0 inside the same block, and some group holds 2.
All inputs are finite; a program needn't handle non-finite values.
Results may differ from a plain program's by a relative error of at most 0.0034.
Values may be sent and summed in bfloat16 or wider, within the bound.
No kernel may reach another device: no remote copies, remote signals or barrier semaphores. Data moves between devices by JAX's collectives and lax.ppermute only.
A program may use at most 64 MiB of HBM per device.

v0:
```python
import jax
import jax.numpy as jnp
from jax import lax
from jax.sharding import PartitionSpec as P

HIGHEST = lax.Precision.HIGHEST


def tri_solve(factor_low, values, transpose_it):
    return lax.linalg.triangular_solve(
        factor_low, values, left_side=True, lower=True, transpose_a=transpose_it
    )


def spd_solve(factor_low, values):
    return tri_solve(factor_low, tri_solve(factor_low, values, False), True)


def gram_part(matrix, scaling):
    scaled = (matrix.astype(jnp.float32) * scaling.astype(jnp.float32)[None, :]).astype(
        jnp.bfloat16
    )
    return lax.dot_general(
        scaled, matrix, (((1,), (1,)), ((), ())), preferred_element_type=jnp.float32
    )


def transposed_dot(left_side, right_side):
    return lax.dot_general(
        left_side,
        right_side,
        (((0,), (0,)), ((), ())),
        precision=HIGHEST,
        preferred_element_type=jnp.float32,
    )


def local(
    adaptive_matrices,
    barrier_ratios,
    damping_shift,
    coupler_matrices,
    constraint_bounds,
    leading_main_entries,
    leading_source_vector,
    outcome_tallies,
):
    position = lax.axis_index("scen")
    held_count = outcome_tallies[position]
    row_count = adaptive_matrices.shape[1]
    col_count = adaptive_matrices.shape[2]
    link_width = coupler_matrices.shape[2]
    own_first_part = (
        adaptive_matrices[0],
        barrier_ratios[0],
        damping_shift[0],
        coupler_matrices[0],
        constraint_bounds[0],
    )

    def gram_live(operand):
        return gram_part(operand[0], operand[1])

    def gram_spare(operand):
        return jnp.zeros((row_count, row_count), jnp.float32)

    pending_items = [
        own_first_part,
        (
            adaptive_matrices[1],
            barrier_ratios[1],
            damping_shift[1],
            coupler_matrices[1],
            constraint_bounds[1],
        ),
    ]
    live_flags = [held_count >= 1, held_count >= 2]
    partials = [
        lax.cond(is_live, gram_live, gram_spare, item_data)
        for item_data, is_live in zip(pending_items, live_flags)
    ]
    stacked_grams = lax.psum(jnp.stack(partials), "col")
    summed_grams = [stacked_grams[0], stacked_grams[1]]
    item_total = len(pending_items)

    def chol_live(operand):
        return jnp.linalg.cholesky(operand[0] + jnp.diag(operand[1].astype(jnp.float32)))

    def chol_spare(operand):
        return jnp.zeros((row_count, row_count), jnp.float32)

    triangle_matrices = [
        lax.cond(
            live_flags[index], chol_live, chol_spare, (summed_grams[index], pending_items[index][2])
        )
        for index in range(item_total)
    ]

    def rhs_part(factor_low, dense_link, target):
        second = spd_solve(factor_low, target.astype(jnp.float32)[:, None])
        return transposed_dot(dense_link, second)[:, 0]

    def whole_live(operand):
        dense_link = operand[1].astype(jnp.float32)
        solved = tri_solve(operand[0], dense_link, False)
        return (transposed_dot(solved, solved), rhs_part(operand[0], dense_link, operand[2]))

    def whole_spare(operand):
        return (
            jnp.zeros((link_width, link_width), jnp.float32),
            jnp.zeros((link_width,), jnp.float32),
        )

    whole_terms = [
        lax.cond(
            live_flags[index],
            whole_live,
            whole_spare,
            (triangle_matrices[index], pending_items[index][3], pending_items[index][4]),
        )
        for index in range(item_total)
    ]
    schur_local = whole_terms[0][0]
    rhs_local = whole_terms[0][1]
    index = 1
    schur_local = schur_local + whole_terms[index][0]
    rhs_local = rhs_local + whole_terms[index][1]
    reduced_matrix_total, rhs_total = lax.psum((schur_local, rhs_local), "scen")
    schur_full = reduced_matrix_total + jnp.diag(leading_main_entries)
    first_dir = spd_solve(
        jnp.linalg.cholesky(schur_full), (leading_source_vector - rhs_total)[:, None]
    )[:, 0]

    def direction_live(operand):
        factor_low, matrix, scaling, coupling, target = operand
        pushed = target.astype(jnp.float32) + jnp.dot(
            coupling.astype(jnp.float32), first_dir, precision=HIGHEST
        )
        dual_vec = spd_solve(factor_low, pushed[:, None])[:, 0]
        primal = scaling.astype(jnp.float32) * jnp.dot(
            dual_vec.astype(jnp.bfloat16), matrix, preferred_element_type=jnp.float32
        )
        return (dual_vec, primal)

    def direction_spare(operand):
        return (jnp.zeros((row_count,), jnp.float32), jnp.zeros((col_count,), jnp.float32))

    results = [
        lax.cond(
            live_flags[index],
            direction_live,
            direction_spare,
            (
                triangle_matrices[index],
                pending_items[index][0],
                pending_items[index][1],
                pending_items[index][3],
                pending_items[index][4],
            ),
        )
        for index in range(item_total)
    ]
    dual_list = [results[0][0], results[1][0]]
    primal_list = [results[0][1], results[1][1]]
    return (first_dir, jnp.stack(dual_list), jnp.stack(primal_list))


def solution(mesh):
    return jax.shard_map(
        local,
        mesh=mesh,
        in_specs=(
            P("scen", None, "col"),
            P("scen", "col"),
            P("scen", None),
            P("scen", None, None),
            P("scen", None),
            P(),
            P(),
            P(),
        ),
        out_specs=(P(), P("scen", None), P("scen", "col")),
        check_vma=False,
    )
```

profile of v0, /device:TPU:2, one launch (start us, length us, event | category | flops | bytes accessed | tf_op | source)
XLA Modules:
  0.0 932.7 jit_solution(16606446807525611188)
XLA Ops:
  10.6 2.7 slice_bitcast_fusion.57
  13.3 2.7 conditional.9
  13.3 2.7 fusion.4
  19.5 90.3 %all-reduce.4.cloned.1.call-done = f32[2,512,512]{1,2,0:T(8,128)} async-done(((f32[2,512,512]{1,2,0:T(8,128)}), f32[2,512,512]{1,2,0:T(8,128)}) %all-reduce.4.cloned.1.call-update) | async-done | bytes 2097168 | tf_op jit(solution)/shard_map/psum | solution.py:82
  109.8 95.0 %conditional.12 = (f32[512,512]{1,0:T(8,128)S(1)}) conditional(s32[]{:T(128)} %bitcast.245, () %tuple.89, (f32[2,512,512]{1,2,0:T(8,128)}, bf16[2,512]{1,0:T(2,128)(2,1)S(1)}) %tuple.264), branch_computations={%region_17.22_spmd, %region_18.23_spmd} | conditional | flops 405931008 | bytes 27012176 | solution.py:93
  110.3 2.5 bitcast_add_fusion.3
  112.8 2.5 copy.12
  117.8 11.7 %cholesky.446 = f32[128,128]{1,0:T(8,128)S(1)} custom-call(f32[128,128]{1,0:T(8,128)S(1)} %cholesky.599), custom_call_target="Cholesky" | custom-call | tf_op jit(solution)/shard_map/cond/branch_1_fun/jit(cholesky)/cholesky | solution.py:87
  129.5 9.8 %custom-call.50 = f32[1,128,128]{1,2,0:T(8,128)S(1)} custom-call(f32[1,128,128]{2,1,0:T(8,128)S(1)} %get-tuple-element.290), custom_call_target="InvertDiagBlocksLowerTriangular" | custom-call | tf_op jit(solution)/shard_map/cond/branch_1_fun/jit(cholesky)/cholesky | solution.py:87
  142.0 11.7 %cholesky.465 = f32[128,128]{1,0:T(8,128)S(1)} custom-call(f32[128,128]{1,0:T(8,128)S(1)} %cholesky.603), custom_call_target="Cholesky" | custom-call | tf_op jit(solution)/shard_map/cond/branch_1_fun/jit(cholesky)/cholesky | solution.py:87
  155.6 9.9 %custom-call.51 = f32[1,128,128]{1,2,0:T(8,128)S(1)} custom-call(f32[1,128,128]{2,1,0:T(8,128)S(1)} %get-tuple-element.287), custom_call_target="InvertDiagBlocksLowerTriangular" | custom-call | tf_op jit(solution)/shard_map/cond/branch_1_fun/jit(cholesky)/cholesky | solution.py:87
  167.1 11.7 %cholesky.486 = f32[128,128]{1,0:T(8,128)S(1)} custom-call(f32[128,128]{1,0:T(8,128)S(1)} %cholesky.608), custom_call_target="Cholesky" | custom-call | tf_op jit(solution)/shard_map/cond/branch_1_fun/jit(cholesky)/cholesky | solution.py:87
  180.0 9.8 %custom-call.52 = f32[1,128,128]{1,2,0:T(8,128)S(1)} custom-call(f32[1,128,128]{2,1,0:T(8,128)S(1)} %get-tuple-element.284), custom_call_target="InvertDiagBlocksLowerTriangular" | custom-call | tf_op jit(solution)/shard_map/cond/branch_1_fun/jit(cholesky)/cholesky | solution.py:87
  191.2 11.7 %cholesky.503 = f32[128,128]{1,0:T(8,128)S(1)} custom-call(f32[128,128]{1,0:T(8,128)S(1)} %convolution_subtract_fusion.8), custom_call_target="Cholesky" | custom-call | tf_op jit(solution)/shard_map/cond/branch_1_fun/jit(cholesky)/cholesky | solution.py:87
  204.8 95.6 %conditional.10 = (f32[512,512]{1,0:T(8,128)S(1)}) conditional(s32[]{:T(128)} %bitcast.242, () %tuple.81, (f32[2,512,512]{1,2,0:T(8,128)}, bf16[2,512]{1,0:T(2,128)(2,1)S(1)}) %tuple.265), branch_computations={%region_5.0_spmd, %region_6.16_spmd} | conditional | flops 405931008 | bytes 14429210 | solution.py:93
  209.3 11.7 %cholesky.374 = f32[128,128]{1,0:T(8,128)S(1)} custom-call(f32[128,128]{1,0:T(8,128)S(1)} %cholesky.586), custom_call_target="Cholesky" | custom-call | tf_op jit(solution)/shard_map/cond/branch_1_fun/jit(cholesky)/cholesky | solution.py:87
  221.1 9.8 %custom-call.44 = f32[1,128,128]{1,2,0:T(8,128)S(1)} custom-call(f32[1,128,128]{2,1,0:T(8,128)S(1)} %get-tuple-element.274), custom_call_target="InvertDiagBlocksLowerTriangular" | custom-call | tf_op jit(solution)/shard_map/cond/branch_1_fun/jit(cholesky)/cholesky | solution.py:87
  233.3 11.7 %cholesky.393 = f32[128,128]{1,0:T(8,128)S(1)} custom-call(f32[128,128]{1,0:T(8,128)S(1)} %cholesky.590), custom_call_target="Cholesky" | custom-call | tf_op jit(solution)/shard_map/cond/branch_1_fun/jit(cholesky)/cholesky | solution.py:87
  247.5 9.9 %custom-call.45 = f32[1,128,128]{1,2,0:T(8,128)S(1)} custom-call(f32[1,128,128]{2,1,0:T(8,128)S(1)} %get-tuple-element.271), custom_call_target="InvertDiagBlocksLowerTriangular" | custom-call | tf_op jit(solution)/shard_map/cond/branch_1_fun/jit(cholesky)/cholesky | solution.py:87
  259.8 11.7 %cholesky.414 = f32[128,128]{1,0:T(8,128)S(1)} custom-call(f32[128,128]{1,0:T(8,128)S(1)} %cholesky.595), custom_call_target="Cholesky" | custom-call | tf_op jit(solution)/shard_map/cond/branch_1_fun/jit(cholesky)/cholesky | solution.py:87
  273.3 9.8 %custom-call.46 = f32[1,128,128]{1,2,0:T(8,128)S(1)} custom-call(f32[1,128,128]{2,1,0:T(8,128)S(1)} %get-tuple-element.268), custom_call_target="InvertDiagBlocksLowerTriangular" | custom-call | tf_op jit(solution)/shard_map/cond/branch_1_fun/jit(cholesky)/cholesky | solution.py:87
  285.4 11.7 %cholesky.431 = f32[128,128]{1,0:T(8,128)S(1)} custom-call(f32[128,128]{1,0:T(8,128)S(1)} %convolution_subtract_fusion.2), custom_call_target="Cholesky" | custom-call | tf_op jit(solution)/shard_map/cond/branch_1_fun/jit(cholesky)/cholesky | solution.py:87
  300.4 73.0 %conditional.13 = (f32[512]{0:T(512)S(1)}, f32[512,512]{0,1:T(8,128)}) conditional(s32[]{:T(128)} %bitcast.245, () %tuple.88, (bf16[512,512]{1,0:T(8,128)(2,1)S(1)}, f32[512,512]{1,0:T(8,128)S(1)}, bf16[512]{0:T(512)(128)(2,1)S(1)}) %tuple.90), branch_computations={%region_19.24_spmd, %region_20.25_spmd} | conditional | flops 2626622208 | bytes 13660397 | solution.py:115
  301.6 14.3 %while.25 = (s32[]{:T(128)}, f32[512,512]{1,0:T(8,128)}, s32[4,2]{0,1:T(2,128)S(1)}, f32[4,128,128]{2,1,0:T(8,128)}, s32[]{:T(128)}) while((s32[]{:T(128)}, f32[512,512]{1,0:T(8,128)}, s32[4,2]{0,1:T(2,128)S(1)}, f32[4,128,128]{2,1,0:T(8,128)}, s32[]{:T(128)}) %tuple.232), condition=%wide.while_cond.clone, body=%wide.while_body.clone.sunk | while | flops 2 | bytes 132205 | solution.py:10
  302.3 2.9 bitcast_dynamic-update-slice_fusion.13
  305.8 2.9 bitcast_dynamic-update-slice_fusion.13
  309.4 2.9 bitcast_dynamic-update-slice_fusion.13
  313.0 2.9 bitcast_dynamic-update-slice_fusion.13
  315.9 40.1 %custom-call.53 = f32[4,128,128]{1,2,0:T(8,128)S(1)} custom-call(f32[4,128,128]{2,1,0:T(8,128)} %get-tuple-element.208), custom_call_target="InvertDiagBlocksLowerTriangular" | custom-call | tf_op jit(solution)/shard_map/cond/branch_1_fun/triangular_solve/custom-call.3 | solution.py:10
  370.6 2.9 fusion.106
  373.5 73.4 %conditional.11 = (f32[512]{0:T(512)S(1)}, f32[512,512]{0,1:T(8,128)}) conditional(s32[]{:T(128)} %bitcast.242, () %tuple.80, (bf16[512,512]{1,0:T(8,128)(2,1)S(1)}, f32[512,512]{1,0:T(8,128)S(1)}, bf16[512]{0:T(512)(128)(2,1)S(1)}) %tuple.87), branch_computations={%region_15.17_spmd, %region_16.21_spmd} | conditional | flops 2626622208 | bytes 13660397 | solution.py:115
  375.0 14.3 %while.24 = (s32[]{:T(128)}, f32[512,512]{1,0:T(8,128)}, s32[4,2]{0,1:T(2,128)S(1)}, f32[4,128,128]{2,1,0:T(8,128)}, s32[]{:T(128)}) while((s32[]{:T(128)}, f32[512,512]{1,0:T(8,128)}, s32[4,2]{0,1:T(2,128)S(1)}, f32[4,128,128]{2,1,0:T(8,128)}, s32[]{:T(128)}) %tuple.235), condition=%wide.while_cond, body=%wide.while_body.sunk | while | flops 2 | bytes 132205 | solution.py:10
  375.7 2.9 bitcast_dynamic-update-slice_fusion.14
  379.2 2.9 bitcast_dynamic-update-slice_fusion.14
  382.8 2.9 bitcast_dynamic-update-slice_fusion.14
  386.4 2.9 bitcast_dynamic-update-slice_fusion.14
  389.3 40.1 %custom-call.47 = f32[4,128,128]{1,2,0:T(8,128)S(1)} custom-call(f32[4,128,128]{2,1,0:T(8,128)} %get-tuple-element.205), custom_call_target="InvertDiagBlocksLowerTriangular" | custom-call | tf_op jit(solution)/shard_map/cond/branch_1_fun/triangular_solve/custom-call.3 | solution.py:10
  444.0 2.9 fusion.24
  446.9 2.8 add.64
  449.7 118.8 %psum.23 = f32[512]{0:T(512)S(1)} all-reduce(f32[512]{0:T(512)S(1)} %add.66), channel_id=1, replica_groups=mesh['scen'=64,'col'=8] {'scen'}, use_global_device_ids=true, to_apply=%region_22.27 | all-reduce | flops 512 | bytes 4096 | tf_op jit(solution)/shard_map/psum | solution.py:128
  568.6 76.5 %all-reduce.6.cloned.1.call-done = f32[512,512]{0,1:T(8,128)} async-done(((f32[512,512]{0,1:T(8,128)}), f32[512,512]{0,1:T(8,128)}) %all-reduce.6.cloned.1.call-update) | async-done | bytes 1048592 | tf_op jit(solution)/shard_map/psum | solution.py:128
  645.0 2.3 select_add_fusion
  647.4 2.6 copy.17
  652.7 11.7 %cholesky.518 = f32[128,128]{1,0:T(8,128)S(1)} custom-call(f32[128,128]{1,0:T(8,128)S(1)} %cholesky.612), custom_call_target="Cholesky" | custom-call | tf_op jit(solution)/shard_map/jit(cholesky)/cholesky | solution.py:131
  664.5 9.8 %custom-call.60 = f32[1,128,128]{1,2,0:T(8,128)S(1)} custom-call(f32[1,128,128]{2,1,0:T(8,128)S(1)} %get-tuple-element.316), custom_call_target="InvertDiagBlocksLowerTriangular" | custom-call | tf_op jit(solution)/shard_map/jit(cholesky)/cholesky | solution.py:131
  678.7 11.7 %cholesky.537 = f32[128,128]{1,0:T(8,128)S(1)} custom-call(f32[128,128]{1,0:T(8,128)S(1)} %cholesky.616), custom_call_target="Cholesky" | custom-call | tf_op jit(solution)/shard_map/jit(cholesky)/cholesky | solution.py:131
  691.1 10.0 %custom-call.61 = f32[1,128,128]{1,2,0:T(8,128)S(1)} custom-call(f32[1,128,128]{2,1,0:T(8,128)S(1)} %get-tuple-element.313), custom_call_target="InvertDiagBlocksLowerTriangular" | custom-call | tf_op jit(solution)/shard_map/jit(cholesky)/cholesky | solution.py:131
  703.5 11.7 %cholesky.558 = f32[128,128]{1,0:T(8,128)S(1)} custom-call(f32[128,128]{1,0:T(8,128)S(1)} %cholesky.621), custom_call_target="Cholesky" | custom-call | tf_op jit(solution)/shard_map/jit(cholesky)/cholesky | solution.py:131
  716.4 9.8 %custom-call.62 = f32[1,128,128]{1,2,0:T(8,128)S(1)} custom-call(f32[1,128,128]{2,1,0:T(8,128)S(1)} %get-tuple-element.310), custom_call_target="InvertDiagBlocksLowerTriangular" | custom-call | tf_op jit(solution)/shard_map/jit(cholesky)/cholesky | solution.py:131
  728.5 11.7 %cholesky.575 = f32[128,128]{1,0:T(8,128)S(1)} custom-call(f32[128,128]{1,0:T(8,128)S(1)} %convolution_subtract_fusion.14), custom_call_target="Cholesky" | custom-call | tf_op jit(solution)/shard_map/jit(cholesky)/cholesky | solution.py:131
  745.1 2.4 select_select_fusion.2
  747.5 14.1 %while.28 = (s32[]{:T(128)}, f32[512,512]{1,0:T(8,128)}, s32[4,2]{0,1:T(2,128)S(1)}, f32[4,128,128]{2,1,0:T(8,128)}, s32[]{:T(128)}) while((s32[]{:T(128)}, f32[512,512]{1,0:T(8,128)}, s32[4,2]{0,1:T(2,128)S(1)}, f32[4,128,128]{2,1,0:T(8,128)}, s32[]{:T(128)}) %tuple.246), condition=%wide.while_cond.2.clone.3, body=%wide.while_body.2.clone.3.sunk | while | flops 2 | bytes 132205 | solution.py:10
  748.2 2.9 bitcast_dynamic-update-slice_fusion.10
  751.7 2.9 bitcast_dynamic-update-slice_fusion.10
  755.2 2.9 bitcast_dynamic-update-slice_fusion.10
  758.8 2.8 bitcast_dynamic-update-slice_fusion.10
  761.6 40.1 %custom-call.64 = f32[4,128,128]{1,2,0:T(8,128)S(1)} custom-call(f32[4,128,128]{2,1,0:T(8,128)} %get-tuple-element.216), custom_call_target="InvertDiagBlocksLowerTriangular" | custom-call | tf_op jit(solution)/shard_map/triangular_solve/custom-call.9 | solution.py:10
  810.0 62.8 %conditional.15 = (f32[1,512]{1,0:T(1,128)S(1)}, f32[1,1024]{1,0:T(1,128)S(1)}) conditional(s32[]{:T(128)} %bitcast.245, () %tuple.93, (bf16[512]{0:T(512)(128)(2,1)S(1)}, bf16[512,512]{1,0:T(8,128)(2,1)S(1)}, f32[512]{0:T(512)S(1)}, f32[512,512]{1,0:T(8,128)S(1)}, bf16[1024]{0:T(1024)(128)(2,1)S(1)}, ...), branch_computations={%region_25.30_spmd, %region_26.31_spmd} | conditional | flops 8662278 | bytes 5162229 | solution.py:149
  811.7 12.0 %while.27 = (s32[]{:T(128)}, f32[512,512]{1,0:T(8,128)}, s32[4,2]{0,1:T(2,128)S(1)}, f32[4,128,128]{2,1,0:T(8,128)S(1)}, s32[]{:T(128)}) while((s32[]{:T(128)}, f32[512,512]{1,0:T(8,128)}, s32[4,2]{0,1:T(2,128)S(1)}, f32[4,128,128]{2,1,0:T(8,128)S(1)}, s32[]{:T(128)}) %tuple.226), condition=%wide.while_cond.2.clone.2, body=%wide.while_body.2.clone.2.sunk | while | flops 2 | bytes 131189 | solution.py:10
  812.3 2.3 bitcast_dynamic-update-slice_fusion.11
  823.7 39.3 %custom-call.59 = f32[4,128,128]{1,2,0:T(8,128)S(1)} custom-call(f32[4,128,128]{2,1,0:T(8,128)S(1)} %get-tuple-element.214), custom_call_target="InvertDiagBlocksLowerTriangular" | custom-call | tf_op jit(solution)/shard_map/cond/branch_1_fun/triangular_solve/custom-call.9 | solution.py:10
  872.8 51.4 %conditional.14 = (f32[1,512]{1,0:T(1,128)S(1)}, f32[1,1024]{1,0:T(1,128)S(1)}) conditional(s32[]{:T(128)} %bitcast.242, () %tuple.91, (bf16[512]{0:T(512)(128)(2,1)S(1)}, bf16[512,512]{1,0:T(8,128)(2,1)S(1)}, f32[512]{0:T(512)S(1)}, f32[512,512]{1,0:T(8,128)S(1)}, bf16[1024]{0:T(1024)(128)(2,1)S(1)}, ...), branch_computations={%region_23.28_spmd, %region_24.29_spmd} | conditional | flops 8662278 | bytes 9356561 | solution.py:149
  873.5 8.2 while.26
  881.6 39.3 %custom-call.57 = f32[4,128,128]{1,2,0:T(8,128)S(1)} custom-call(f32[4,128,128]{2,1,0:T(8,128)S(1)} %get-tuple-element.212), custom_call_target="InvertDiagBlocksLowerTriangular" | custom-call | tf_op jit(solution)/shard_map/cond/branch_1_fun/triangular_solve/custom-call.9 | solution.py:10
  (266 shorter events, 130.9 us)
Async XLA Ops:
  7.2 102.7 %all-reduce.4.cloned.1.call-start = ((), (), s32[]{:S(2)}) async-start(), calls=%async_computation | async-start | bytes 4194304 | tf_op jit(solution)/shard_map/psum | solution.py:82
  13.3 2.7 copy-start.1
  18.2 0.7 copy-start.7
  18.2 1.2 copy-start.5
  18.2 91.6 %copy-start.8 = (bf16[2,512]{1,0:T(2,128)(2,1)S(1)}, bf16[2,512]{1,0:T(2,128)(2,1)}, u32[]{:S(2)}) copy-start(bf16[2,512]{1,0:T(2,128)(2,1)} %param.33) | copy-start | bytes 6148
  18.3 626.8 %all-reduce.6.cloned.1.call-start = ((), (), s32[]{:S(2)}) async-start(), calls=%async_computation.1 | async-start | bytes 2097152 | tf_op jit(solution)/shard_map/psum | solution.py:128
  110.3 5.0 copy-start
  116.8 1.0 copy-start.3
  446.9 121.7 %copy-start.10 = (f32[512]{0:T(512)S(1)}, f32[512]{0:T(512)}, u32[]{:S(2)}) copy-start(f32[512]{0:T(512)} %param.37) | copy-start | bytes 6148
  446.9 198.2 %copy-start.9 = (f32[512]{0:T(512)S(1)}, f32[512]{0:T(512)}, u32[]{:S(2)}) copy-start(f32[512]{0:T(512)} %param.36) | copy-start | bytes 6148
  651.7 1.0 copy-start.4
  810.0 62.8 %copy-start.6 = (f32[512,1]{0,1:T(1,128)}, f32[512,1]{0,1:T(1,128)S(1)}, u32[]{:S(2)}) copy-start(f32[512,1]{0,1:T(1,128)S(1)} %pad_maximum_fusion.7) | copy-start | bytes 6148
  872.9 50.9 %copy-start.2 = (bf16[512,1024]{1,0:T(8,128)(2,1)S(1)}, bf16[512,1024]{1,0:T(8,128)(2,1)}, u32[]{:S(2)}) copy-start(bf16[512,1024]{1,0:T(8,128)(2,1)} %get-tuple-element.101) | copy-start | bytes 3145732 | tf_op jit(solution)/shard_map/cond
Sparse Core Ops, SparseCore 0:
  18.4 91.3 all-reduce.3
  449.8 195.1 all-reduce.5
where the time goes:
time: 937 us; the launch traced here: 933 us
  other arithmetic  463 us (49%)
  waiting for transfers between devices  167 us (18%)
  blocking collectives  119 us (13%)
  local copies, waits for them, and re-layouts  79.5 us (8%)
  matrix products  79.3 us (8%)
  between operations  18.6 us (2%)
    another operation x21, other arithmetic, tri_solve(): lax.linalg.triangular_solve(factor_low, values, left_side=True, lower=Tru...  205 us
    another operation x28, other arithmetic, chol_live(): jnp.linalg.cholesky(operand[0] + jnp.diag(operand[1].astype(jnp.float32)))  159 us
    psum x1, blocking collectives, local(): reduced_matrix_total, rhs_total = lax.psum((schur_local, rhs_local), 'scen')  119 us
    psum x1, waiting for transfers between devices, local(): stacked_grams = lax.psum(jnp.stack(partials), 'col')  90.3 us
    another operation x14, other arithmetic, local(): jnp.linalg.cholesky(schur_full)  80.7 us
    psum x1, waiting for transfers between devices, local(): reduced_matrix_total, rhs_total = lax.psum((schur_local, rhs_local), 'scen')  76.5 us
    another operation x65, local copies, waits for them, and re-layouts, tri_solve(): lax.linalg.triangular_solve(factor_low, values, left_side=True, lower=Tru...  62.6 us
    another operation x84, matrix products, tri_solve(): lax.linalg.triangular_solve(factor_low, values, left_side=True, lower=Tru...  47.4 us
  transfers between devices with their start and end apart: 2, of which 2 were waited for; matrix products, arithmetic and copies ran while one was open for 0% of the time, Pallas kernels for 0%

commit v1 on v0

v1 whole, which is shorter than its diff:
```python
import functools

import jax
import jax.numpy as jnp
from jax import lax
from jax.experimental import pallas as pl
from jax.experimental.pallas import tpu as pltpu
from jax.sharding import PartitionSpec as P

F32 = jnp.float32
BF16 = jnp.bfloat16
B = 128
TOL2 = 1e-12
MAX_STEPS = 4096


def blocks_of(rows):
    n = rows // B
    return [(i, j) for i in range(n) for j in range(i + 1)]


def mm(a, b):
    return lax.dot_general(a, b, (((1,), (0,)), ((), ())), preferred_element_type=F32)


def split3(x):
    hi = x.astype(BF16)
    rest = x - hi.astype(F32)
    mid = rest.astype(BF16)
    low = (rest - mid.astype(F32)).astype(BF16)
    return hi, mid, low


def eye_mask():
    return lax.broadcasted_iota(jnp.int32, (B, B), 0) == lax.broadcasted_iota(
        jnp.int32, (B, B), 1
    )


def gram_kernel(slot, parts, w_ref, d_ref, out_ref, scaled_ref, g_ref):
    rows = w_ref.shape[1]
    scale = d_ref[...].astype(F32)[slot : slot + 1]
    for i in range(rows // B):
        at = slice(i * B, (i + 1) * B)
        scaled_ref[at, :] = (w_ref[0, at, :].astype(F32) * scale).astype(BF16)
    for i in range(rows // B):
        at = slice(i * B, (i + 1) * B)
        g_ref[at, :] = lax.dot_general(
            scaled_ref[at, :], w_ref[0], (((1,), (1,)), ((), ())), preferred_element_type=F32
        )
    step = B // parts
    for b, (i, j) in enumerate(blocks_of(rows)):
        blk = g_ref[i * B : (i + 1) * B, j * B : (j + 1) * B]
        if i != j:
            blk = 0.5 * (blk + g_ref[j * B : (j + 1) * B, i * B : (i + 1) * B].T)
        for z in range(parts):
            out_ref[z, b * step : (b + 1) * step, :] = blk[z * step : (z + 1) * step, :]


def gram(slot, parts, matrices, ratios):
    _, rows, cols = matrices.shape
    height = len(blocks_of(rows)) * B // parts
    return pl.pallas_call(
        functools.partial(gram_kernel, slot, parts),
        grid=(1,),
        in_specs=[
            pl.BlockSpec((1, rows, cols), lambda i: (slot, 0, 0)),
            pl.BlockSpec(ratios.shape, lambda i: (0, 0)),
        ],
        out_specs=pl.BlockSpec((parts, height, B), lambda i: (0, 0, 0)),
        out_shape=jax.ShapeDtypeStruct((parts, height, B), F32),
        scratch_shapes=[pltpu.VMEM((rows, cols), BF16), pltpu.VMEM((rows, rows), F32)],
        name=f"gram{slot}",
    )(matrices, ratios)


def cg_block(parts_of_matrix, x_ref, r_ref, p_ref, rr_ref, bb_ref):
    hi, mid, low = parts_of_matrix
    n = x_ref.shape[1]

    def apply(p):
        ph, pm, plow = split3(p)
        a = mm(hi[...], jnp.concatenate([ph, pm, plow], axis=1))
        c = mm(mid[...], jnp.concatenate([ph, pm], axis=1))
        e = mm(low[...], ph)
        small = a[:, 2 * n :] + c[:, n:] + e
        return a[:, :n] + ((a[:, n : 2 * n] + c[:, :n]) + small)

    def body(carry):
        k, _ = carry
        p = p_ref[...]
        q = apply(p)
        rr = rr_ref[...]
        pq = jnp.sum(p * q, axis=0, keepdims=True)
        alpha = jnp.where(pq > 0.0, rr / jnp.where(pq > 0.0, pq, 1.0), 0.0)
        x_ref[...] += alpha * p
        r = r_ref[...] - alpha * q
        r_ref[...] = r
        new = jnp.sum(r * r, axis=0, keepdims=True)
        beta = jnp.where(rr > 0.0, new / jnp.where(rr > 0.0, rr, 1.0), 0.0)
        p_ref[...] = r + beta * p
        rr_ref[...] = new
        return k + 1, jnp.max(new - TOL2 * bb_ref[...])

    rhs = r_ref[...]
    x_ref[...] = jnp.zeros_like(rhs)
    p_ref[...] = rhs
    first = jnp.sum(rhs * rhs, axis=0, keepdims=True)
    rr_ref[...] = first
    bb_ref[...] = first
    lax.while_loop(
        lambda c: (c[0] < MAX_STEPS) & (c[1] > 0.0), body, (jnp.int32(0), jnp.max(first))
    )


def solve_kernel(
    recv_ref, reg_ref, rhs_ref, link_ref, g_ref, out_ref,
    hi_ref, mid_ref, low_ref, x_ref, r_ref, p_ref, rr_ref, bb_ref,
):
    parts = recv_ref.shape[0]
    rows = g_ref.shape[0]
    step = B // parts
    eye = eye_mask()
    for b, (i, j) in enumerate(blocks_of(rows)):
        ri, rj = slice(i * B, (i + 1) * B), slice(j * B, (j + 1) * B)
        for z in range(parts):
            g_ref[i * B + z * step : i * B + (z + 1) * step, rj] = recv_ref[
                z, b * step : (b + 1) * step, :
            ]
        blk = g_ref[ri, rj]
        if i == j:
            g_ref[ri, rj] = 0.5 * (blk + blk.T) + jnp.where(eye, reg_ref[:, rj], 0.0)
        else:
            g_ref[rj, ri] = blk.T
    for i in range(rows // B):
        at = slice(i * B, (i + 1) * B)
        hi_ref[at, :], mid_ref[at, :], low_ref[at, :] = split3(g_ref[at, :])
    r_ref[...] = rhs_ref[...].astype(F32)
    cg_block((hi_ref, mid_ref, low_ref), x_ref, r_ref, p_ref, rr_ref, bb_ref)
    n = x_ref.shape[1]
    pieces = jnp.concatenate(split3(x_ref[...]), axis=1)
    y = lax.dot_general(
        link_ref[...], pieces, (((0,), (0,)), ((), ())), preferred_element_type=F32
    )
    out_ref[...] = y[:, :n] + (y[:, n : 2 * n] + y[:, 2 * n :])


def solve(received, reg_row, rhs, link):
    rows, width = rhs.shape
    n0 = link.shape[1]
    return pl.pallas_call(
        solve_kernel,
        out_shape=(
            jax.ShapeDtypeStruct((rows, rows), F32),
            jax.ShapeDtypeStruct((n0, width), F32),
        ),
        scratch_shapes=[pltpu.VMEM((rows, rows), BF16)] * 3
        + [pltpu.VMEM((rows, width), F32)] * 3
        + [pltpu.VMEM((1, width), F32)] * 2,
        name="solve",
    )(received, reg_row, rhs, link)


def as_row(col, eye):
    return jnp.sum(jnp.where(eye, col, 0.0), axis=0, keepdims=True)


def times_row(mat_ref, row, eye):
    rows, cols = mat_ref.shape[0], row.shape[1]
    out = []
    for i in range(rows // B):
        part = mat_ref[i * B : (i + 1) * B, :cols].astype(F32) * row
        out.append(as_row(jnp.sum(part, axis=1, keepdims=True), eye))
    return jnp.concatenate(out, axis=1)


def cg_row(mat_ref, rhs, x_ref, r_ref, p_ref, eye):
    def body(carry):
        k, rr, stop = carry
        p = p_ref[...]
        q = times_row(mat_ref, p, eye)
        pq = jnp.sum(p * q)
        alpha = jnp.where(pq > 0.0, rr / jnp.where(pq > 0.0, pq, 1.0), 0.0)
        x_ref[...] += alpha * p
        r = r_ref[...] - alpha * q
        r_ref[...] = r
        new = jnp.sum(r * r)
        beta = jnp.where(rr > 0.0, new / jnp.where(rr > 0.0, rr, 1.0), 0.0)
        p_ref[...] = r + beta * p
        return k + 1, new, stop

    x_ref[...] = jnp.zeros_like(rhs)
    r_ref[...] = rhs
    p_ref[...] = rhs
    first = jnp.sum(rhs * rhs)
    lax.while_loop(
        lambda c: (c[0] < MAX_STEPS) & (c[1] > c[2]), body, (jnp.int32(0), first, TOL2 * first)
    )
    return x_ref[...]


def main_kernel(
    recv_ref, q_ref, c_ref, g_ref, link_ref, b_ref, first_ref, dual_ref,
    s_ref, x_ref, r_ref, p_ref,
):
    pair, count, each, _ = recv_ref.shape
    n0 = q_ref.shape[1]
    eye = eye_mask()
    for i in range(count):
        for k in range(pair):
            at = (i * pair + k) * each
            s_ref[at : at + each, :] = recv_ref[k, i]
    rho = []
    for i in range(n0 // B):
        at = slice(i * B, (i + 1) * B)
        rho.append(as_row(s_ref[at, n0 : n0 + 1], eye))
        s_ref[at, at] += jnp.where(eye, q_ref[:, at], 0.0)
    rhs = c_ref[...] - jnp.concatenate(rho, axis=1)
    first = cg_row(s_ref.at[:, :n0], rhs, x_ref, r_ref, p_ref, eye)
    first_ref[...] = first
    pushed = b_ref[...] + times_row(link_ref, first, eye)
    dual_ref[...] = cg_row(g_ref, pushed, x_ref, r_ref, p_ref, eye)


def main_solve(received, q_row, c_row, g, link, b_row):
    n0, rows = q_row.shape[1], b_row.shape[1]
    return pl.pallas_call(
        main_kernel,
        out_shape=(
            jax.ShapeDtypeStruct((1, n0), F32),
            jax.ShapeDtypeStruct((1, rows), F32),
        ),
        scratch_shapes=[pltpu.VMEM((n0, received.shape[-1]), F32)]
        + [pltpu.VMEM((1, n0), F32)] * 3,
        name="main_solve",
    )(received, q_row, c_row, g, link, b_row)


def primal_kernel(w_ref, d_ref, dual_ref, out_ref):
    for slot in range(w_ref.shape[0]):
        low = dual_ref[slot : slot + 1, :].astype(BF16)
        out_ref[slot : slot + 1, :] = d_ref[...].astype(F32)[slot : slot + 1] * mm(
            low, w_ref[slot]
        )


def primal(matrices, ratios, duals):
    return pl.pallas_call(
        primal_kernel,
        out_shape=jax.ShapeDtypeStruct(ratios.shape, F32),
        name="primal",
    )(matrices, ratios, duals)


def local(
    scen_size, col_size, matrices, ratios, damping, coupler, bounds, q_diag, c_vec, tallies
):
    n_s, n_z = scen_size, col_size
    rows = matrices.shape[1]
    n0 = coupler.shape[2]
    pos = lax.axis_index("scen")
    zpos = lax.axis_index("col")
    held = tallies[pos]
    before = tallies[jnp.maximum(pos - 1, 0)]
    own = held >= 1
    live = own | ((pos % 4 != 0) & (before == 2))
    forth = [(4 * b + i, 4 * b + i + 1) for b in range(n_s // 4) for i in range(3)]
    back = [(j, i) for i, j in forth]

    def everyone(x, axis, count, **kw):
        return lax.all_to_all(
            jnp.broadcast_to(x[None], (count,) + x.shape), axis, 0, 0, **kw
        )

    sides = [
        jnp.concatenate([coupler[k], damping[k : k + 1], bounds[k : k + 1]], axis=0)
        for k in range(2)
    ]
    side_moved = lax.ppermute(sides[1], "scen", forth)
    gram1 = gram(1, n_z, matrices, ratios)
    gram_moved = lax.ppermute(gram1, "scen", forth)
    gram0 = gram(0, n_z, matrices, ratios)
    side = jnp.where(own, sides[0], side_moved)
    link = side[:rows]
    reg_row = side[rows : rows + 1].astype(F32)
    b_row = side[rows + 1 : rows + 2].astype(F32)
    share = n0 // n_z
    width = -(-(share + 1) // B) * B
    rhs = jnp.concatenate(
        [
            lax.dynamic_slice(link, (0, zpos * share), (rows, share)),
            side[rows + 1][:, None],
            jnp.zeros((rows, width - share - 1), BF16),
        ],
        axis=1,
    )
    rhs = jnp.where(live, rhs, jnp.zeros_like(rhs))

    partial = jnp.where(own, gram0, gram_moved)
    shard = jnp.sum(lax.all_to_all(partial, "col", 0, 0), axis=0)
    g, terms = solve(everyone(shard, "col", n_z), reg_row, rhs, link)

    each = n0 // n_s
    mine = jnp.sum(lax.all_to_all(terms.reshape(n_s, each, width), "scen", 0, 0), axis=0)
    wide = everyone(mine, "col", n_z)
    flat = jnp.concatenate(
        [wide[k, :, :share] for k in range(n_z)] + [wide[0, :, share : share + B]], axis=1
    )
    if flat.shape[1] < n0 + B:
        flat = jnp.pad(flat, ((0, 0), (0, n0 + B - flat.shape[1])))
    same = [[2 * i + k for i in range(n_s // 2)] for k in range(2)]
    cores = [[2 * i, 2 * i + 1] for i in range(n_s // 2)]
    half = everyone(flat, "scen", n_s // 2, axis_index_groups=same)
    full = everyone(half, "scen", 2, axis_index_groups=cores)
    first, dual = main_solve(full, q_diag[None], c_vec[None], g, link, b_row)

    returned = lax.ppermute(dual, "scen", back)
    duals = jnp.concatenate(
        [
            jnp.where(own, dual, jnp.zeros_like(dual)),
            jnp.where(held >= 2, returned, jnp.zeros_like(dual)),
        ],
        axis=0,
    )
    return first[0], duals, primal(matrices, ratios, duals)


def solution(mesh):
    body = functools.partial(local, mesh.shape["scen"], mesh.shape["col"])
    return jax.shard_map(
        body,
        mesh=mesh,
        in_specs=(
            P("scen", None, "col"),
            P("scen", "col"),
            P("scen", None),
            P("scen", None, None),
            P("scen", None),
            P(),
            P(),
            P(),
        ),
        out_specs=(P(), P("scen", None), P("scen", "col")),
        check_vma=False,
    )
```

time: 937 us -> 174 us (0.19)
  the two profiles are of different devices: /device:TPU:2 before, /device:TPU:1 now
where the time goes in v1:
time: 174 us
  waiting for transfers between devices  53.2 us (31%)
  Pallas kernels  41.1 us (24%)
  blocking collectives  40.8 us (23%)
  starting transfers between devices  28.9 us (17%)
  local copies, waits for them, and re-layouts  3.97 us (2%)
  other arithmetic  3.25 us (2%)
  between operations  2.77 us (2%)
    all_to_all x2, waiting for transfers between devices, everyone(): lax.all_to_all(jnp.broadcast_to(x[None], (count,) + x.shape), axis, 0, 0,...  33.9 us
    all_to_all x1, blocking collectives, local(): lax.all_to_all(terms.reshape(n_s, each, width), 'scen', 0, 0)  22.8 us
    all_to_all x2, blocking collectives, everyone(): lax.all_to_all(jnp.broadcast_to(x[None], (count,) + x.shape), axis, 0, 0,...  18 us
    pallas_call x1, Pallas kernels, main_solve(): pl.pallas_call(main_kernel, out_shape=(jax.ShapeDtypeStruct((1, n0), F32)...  16.3 us
    pallas_call x1, Pallas kernels, solve(): pl.pallas_call(solve_kernel, out_shape=(jax.ShapeDtypeStruct((rows, rows)...  15 us
    all_to_all x1, waiting for transfers between devices, local(): shard = jnp.sum(lax.all_to_all(partial, 'col', 0, 0), axis=0)  13.5 us
    all_to_all x1, starting transfers between devices, local(): shard = jnp.sum(lax.all_to_all(partial, 'col', 0, 0), axis=0)  10.2 us
    all_to_all x2, starting transfers between devices, everyone(): lax.all_to_all(jnp.broadcast_to(x[None], (count,) + x.shape), axis, 0, 0,...  7.44 us
  transfers between devices with their start and end apart: 6, of which 5 were waited for; matrix products, arithmetic and copies ran while one was open for 2% of the time, Pallas kernels for 2%

profile of v1, /device:TPU:1, one launch (start us, length us, event | category | flops | bytes accessed | tf_op | source)
XLA Modules:
  0.0 174.0 jit_solution(2238875712985857617)
XLA Ops:
  0.6 3.6 %gram1.1 = f32[8,160,128]{2,1,0:T(8,128)} custom-call(bf16[2,512,1024]{2,1,0:T(8,128)(2,1)} %w_ref.5, bf16[2,1024]{1,0:T(2,128)(2,1)} %d_ref.5), custom_call_target="tpu_custom_call" | custom-call | tf_op jit(solution)/shard_map/gram1/pallas_call | solution.py:63
  4.2 4.5 %collective-permute-start = (f32[8,160,128]{2,1,0:T(8,128)}, f32[8,160,128]{2,1,0:T(8,128)S(1)}, u32[]{:S(2)}, u32[]{:S(2)}) collective-permute-start(f32[8,160,128]{2,1,0:T(8,128)} %gram1.1), channel_id=1, source_target_pairs={{0,8},{8,16},{16,24},{32,40},{40,48},{48,56},{64,72},{72,80},{80,8... | collective-permute-start | bytes 1966088 | tf_op jit(solution)/shard_map/ppermute | solution.py:281
  8.7 0.0 copy-start.5
  8.7 3.6 %gram0.1 = f32[8,160,128]{2,1,0:T(8,128)} custom-call(bf16[2,512,1024]{2,1,0:T(8,128)(2,1)} %w_ref.5, bf16[2,1024]{1,0:T(2,128)(2,1)} %d_ref.5), custom_call_target="tpu_custom_call" | custom-call | tf_op jit(solution)/shard_map/gram0/pallas_call | solution.py:63
  12.3 0.0 copy-done.5
  12.3 0.6 fusion.2
  13.6 3.0 %collective-permute-done = f32[8,160,128]{2,1,0:T(8,128)S(1)} collective-permute-done((f32[8,160,128]{2,1,0:T(8,128)}, f32[8,160,128]{2,1,0:T(8,128)S(1)}, u32[]{:S(2)}, u32[]{:S(2)}) %collective-permute-start) | collective-permute-done | bytes 655392 | tf_op jit(solution)/shard_map/ppermute | solution.py:281
  16.6 0.9 broadcast_select_fusion
  17.5 0.0 copy-start.3
  17.5 0.0 copy-start.4
  17.5 0.0 copy-start.2
  17.5 10.2 %all-to-all-start = ((f32[8,160,128]{2,1,0:T(8,128)}), f32[8,160,128]{2,1,0:T(8,128)S(1)}, u32[]{:S(2)}, u32[]{:S(2)}) async-start(f32[8,160,128]{2,1,0:T(8,128)} %broadcast_select_fusion), calls=%async_computation | async-start | bytes 1310720 | tf_op jit(solution)/shard_map/all_to_all | solution.py:300
  27.6 0.0 copy-done.3
  27.7 0.0 copy-done.4
  27.7 0.0 copy-done.2
  27.7 0.1 slice_bitcast_fusion.1
  27.8 4.6 %collective-permute-start.1 = (bf16[514,512]{1,0:T(8,128)(2,1)S(1)}, bf16[514,512]{1,0:T(8,128)(2,1)S(1)}, u32[]{:S(2)}, u32[]{:S(2)}) collective-permute-start(bf16[514,512]{1,0:T(8,128)(2,1)S(1)} %pad_maximum_fusion), channel_id=1, source_target_pairs={{0,8},{8,16},{16,24},{32,40},{40,48},{48,56},{64,72},{72,80},{80,8... | collective-permute-start | bytes 1579016 | tf_op jit(solution)/shard_map/ppermute | solution.py:279
  32.4 13.5 %all-to-all-done = f32[8,160,128]{2,1,0:T(8,128)S(1)} async-done(((f32[8,160,128]{2,1,0:T(8,128)}), f32[8,160,128]{2,1,0:T(8,128)S(1)}, u32[]{:S(2)}, u32[]{:S(2)}) %all-to-all-start) | async-done | bytes 655392 | tf_op jit(solution)/shard_map/all_to_all | solution.py:300
  45.9 0.9 broadcast_in_dim.16
  46.8 3.5 %all-to-all-start.1 = ((f32[8,160,128]{2,1,0:T(8,128)}), f32[8,160,128]{2,1,0:T(8,128)S(1)}, u32[]{:S(2)}, u32[]{:S(2)}) async-start(f32[8,160,128]{2,1,0:T(8,128)} %broadcast_in_dim.16), calls=%async_computation.1 | async-start | bytes 1310720 | tf_op jit(solution)/shard_map/all_to_all | solution.py:271
  51.0 0.1 pad.9.clone
  51.1 0.0 collective-permute-done.1
  51.1 0.1 maximum_select_fusion
  51.3 0.0 copy-start
  51.3 0.6 slice_convert_fusion.1
  51.9 0.2 copy.11
  52.1 0.1 constant_dynamic-slice_fusion
  52.2 0.8 maximum_select_fusion.1.rhs_ref
  53.0 17.0 %all-to-all-done.1.recv_ref = f32[8,160,128]{2,1,0:T(8,128)S(1)} async-done(((f32[8,160,128]{2,1,0:T(8,128)}), f32[8,160,128]{2,1,0:T(8,128)S(1)}, u32[]{:S(2)}, u32[]{:S(2)}) %all-to-all-start.1) | async-done | bytes 655392 | tf_op jit(solution)/shard_map/all_to_all | solution.py:271
  70.1 0.0 copy-start.1
  70.1 0.0 copy-done
  70.1 0.8 copy-done.1
  70.9 15.0 %solve.1 = (f32[512,512]{1,0:T(8,128)}, f32[512,128]{1,0:T(8,128)}) custom-call(f32[8,160,128]{2,1,0:T(8,128)} %copy-done.1, f32[1,512]{1,0:T(1,128)} %get-tuple-element.15.reg_ref, bf16[512,128]{1,0:T(8,128)(2,1)} %maximum_select_fusion.1.rhs_ref, bf16[512,512]{1,0:T(8,128)(2,1)} %copy-done), custom_call_target="tpu_custom_call" | custom-call | tf_op jit(solution)/shard_map/solve/pallas_call | solution.py:151
  85.9 22.8 %all_to_all.30 = f32[64,8,128]{2,1,0:T(8,128)S(1)} all-to-all(f32[64,8,128]{2,1,0:T(8,128)} %bitcast.31), channel_id=1, replica_groups=mesh['scen'=64,'col'=8] {'scen'}, dimensions={0} | all-to-all | bytes 524288 | tf_op jit(solution)/shard_map/all_to_all | solution.py:304
  108.7 0.1 reduce_sum.19
  108.8 9.2 %all_to_all.31 = f32[8,8,128]{2,1,0:T(8,128)S(1)} all-to-all(f32[8,8,128]{2,1,0:T(8,128)S(1)} %broadcast_in_dim.19), channel_id=1, replica_groups=mesh['scen'=64,'col'=8] {'col'}, dimensions={0} | all-to-all | bytes 65536 | tf_op jit(solution)/shard_map/all_to_all | solution.py:271
  118.0 0.1 slice_bitcast_fusion.2
  118.1 0.1 concatenate.18
  118.2 0.9 broadcast_in_dim.40
  119.1 3.9 %all-to-all-start.4 = ((f32[32,8,640]{2,1,0:T(8,128)}), f32[32,8,640]{2,1,0:T(8,128)S(1)}, u32[]{:S(2)}, u32[]{:S(2)}) async-start(f32[32,8,640]{2,1,0:T(8,128)} %broadcast_in_dim.40), calls=%async_computation.4 | async-start | bytes 1310720 | tf_op jit(solution)/shard_map/all_to_all | solution.py:271
  123.7 16.9 %all-to-all-done.4 = f32[32,8,640]{2,1,0:T(8,128)S(1)} async-done(((f32[32,8,640]{2,1,0:T(8,128)}), f32[32,8,640]{2,1,0:T(8,128)S(1)}, u32[]{:S(2)}, u32[]{:S(2)}) %all-to-all-start.4) | async-done | bytes 655392 | tf_op jit(solution)/shard_map/all_to_all | solution.py:271
  140.6 0.1 broadcast_in_dim.41
  140.6 8.8 %all_to_all.32.recv_ref = f32[2,32,8,640]{3,2,1,0:T(8,128)} all-to-all(f32[2,32,8,640]{3,2,1,0:T(8,128)S(1)} %broadcast_in_dim.41), channel_id=1, replica_groups={{0,8},{16,24},{32,40},{48,56},{64,72},{80,88},{96,104},{112,120},{128,1..., dimensions={0} | all-to-all | bytes 2621440 | tf_op jit(solution)/shard_map/all_to_all | solution.py:271
  149.4 16.3 %main_solve.1 = (f32[1,512]{1,0:T(1,128)}, f32[1,512]{1,0:T(1,128)}) custom-call(f32[2,32,8,640]{3,2,1,0:T(8,128)} %all_to_all.32.recv_ref, f32[1,512]{1,0:T(1,128)} %bitcast.32, f32[1,512]{1,0:T(1,128)} %bitcast.33, f32[512,512]{1,0:T(8,128)} %get-tuple-element.8.g_ref, bf16[512,512]{1,0:T(8,128)(2,1)} %copy-done, f32[1,512]{1,0:T(1,128)} %get-tuple-element.13.b_ref), custom_call_target="tpu_custom_call" | custom-call | tf_op jit(solution)/shard_map/main_solve/pallas_call | solution.py:227
  165.7 2.3 %collective-permute-start.2 = (f32[1,512]{1,0:T(1,128)}, f32[1,512]{1,0:T(1,128)S(1)}, u32[]{:S(2)}, u32[]{:S(2)}) collective-permute-start(f32[1,512]{1,0:T(1,128)} %get-tuple-element.10), channel_id=1, source_target_pairs={{8,0},{16,8},{24,16},{40,32},{48,40},{56,48},{72,64},{80,72},{88,8... | collective-permute-start | bytes 6152 | tf_op jit(solution)/shard_map/ppermute | solution.py:317
  168.0 2.8 %collective-permute-done.2 = f32[1,512]{1,0:T(1,128)S(1)} collective-permute-done((f32[1,512]{1,0:T(1,128)}, f32[1,512]{1,0:T(1,128)S(1)}, u32[]{:S(2)}, u32[]{:S(2)}) %collective-permute-start.2) | collective-permute-done | bytes 2080 | tf_op jit(solution)/shard_map/ppermute | solution.py:317
  170.8 0.6 pad_maximum_fusion.1.dual_ref
  171.4 2.6 %primal.1 = f32[2,1024]{1,0:T(2,128)} custom-call(bf16[2,512,1024]{2,1,0:T(8,128)(2,1)} %w_ref.5, bf16[2,1024]{1,0:T(2,128)(2,1)} %d_ref.5, f32[2,512]{1,0:T(2,128)} %pad_maximum_fusion.1.dual_ref), custom_call_target="tpu_custom_call" | custom-call | tf_op jit(solution)/shard_map/primal/pallas_call | solution.py:248
  (9 shorter events, 0.2 us)
Async XLA Ops:
  4.2 12.3 %collective-permute-start = (f32[8,160,128]{2,1,0:T(8,128)}, f32[8,160,128]{2,1,0:T(8,128)S(1)}, u32[]{:S(2)}, u32[]{:S(2)}) collective-permute-start(f32[8,160,128]{2,1,0:T(8,128)} %gram1.1), channel_id=1, source_target_pairs={{0,8},{8,16},{16,24},{32,40},{40,48},{48,56},{64,72},{72,80},{80,8... | collective-permute-start | bytes 1966088 | tf_op jit(solution)/shard_map/ppermute | solution.py:281
  8.7 3.6 %copy-start.5 = (s32[64]{0:T(128)S(1)}, s32[64]{0:T(128)}, u32[]{:S(2)}) copy-start(s32[64]{0:T(128)} %param.15) | copy-start | bytes 772
  17.5 10.2 %copy-start.3 = (bf16[2,512]{1,0:T(2,128)(2,1)S(1)}, bf16[2,512]{1,0:T(2,128)(2,1)}, u32[]{:S(2)}) copy-start(bf16[2,512]{1,0:T(2,128)(2,1)} %param.10) | copy-start | bytes 6148
  17.5 10.2 %copy-start.4 = (bf16[2,512]{1,0:T(2,128)(2,1)S(1)}, bf16[2,512]{1,0:T(2,128)(2,1)}, u32[]{:S(2)}) copy-start(bf16[2,512]{1,0:T(2,128)(2,1)} %param.12) | copy-start | bytes 6148
  17.5 10.2 %copy-start.2 = (bf16[2,512,512]{2,1,0:T(8,128)(2,1)S(1)}, bf16[2,512,512]{2,1,0:T(8,128)(2,1)}, u32[]{:S(2)}) copy-start(bf16[2,512,512]{2,1,0:T(8,128)(2,1)} %param.11) | copy-start | bytes 3145732
  17.5 28.4 %all-to-all-start = ((f32[8,160,128]{2,1,0:T(8,128)}), f32[8,160,128]{2,1,0:T(8,128)S(1)}, u32[]{:S(2)}, u32[]{:S(2)}) async-start(f32[8,160,128]{2,1,0:T(8,128)} %broadcast_select_fusion), calls=%async_computation | async-start | bytes 1310720 | tf_op jit(solution)/shard_map/all_to_all | solution.py:300
  27.8 23.3 %collective-permute-start.1 = (bf16[514,512]{1,0:T(8,128)(2,1)S(1)}, bf16[514,512]{1,0:T(8,128)(2,1)S(1)}, u32[]{:S(2)}, u32[]{:S(2)}) collective-permute-start(bf16[514,512]{1,0:T(8,128)(2,1)S(1)} %pad_maximum_fusion), channel_id=1, source_target_pairs={{0,8},{8,16},{16,24},{32,40},{40,48},{48,56},{64,72},{72,80},{80,8... | collective-permute-start | bytes 1579016 | tf_op jit(solution)/shard_map/ppermute | solution.py:279
  46.8 23.3 %all-to-all-start.1 = ((f32[8,160,128]{2,1,0:T(8,128)}), f32[8,160,128]{2,1,0:T(8,128)S(1)}, u32[]{:S(2)}, u32[]{:S(2)}) async-start(f32[8,160,128]{2,1,0:T(8,128)} %broadcast_in_dim.16), calls=%async_computation.1 | async-start | bytes 1310720 | tf_op jit(solution)/shard_map/all_to_all | solution.py:271
  51.3 18.8 %copy-start = (bf16[512,512]{1,0:T(8,128)(2,1)}, bf16[512,512]{1,0:T(8,128)(2,1)S(1)}, u32[]{:S(2)}) copy-start(bf16[512,512]{1,0:T(8,128)(2,1)S(1)} %slice.74.link_ref) | copy-start | bytes 1572868
  70.1 0.8 copy-start.1
  119.1 21.5 %all-to-all-start.4 = ((f32[32,8,640]{2,1,0:T(8,128)}), f32[32,8,640]{2,1,0:T(8,128)S(1)}, u32[]{:S(2)}, u32[]{:S(2)}) async-start(f32[32,8,640]{2,1,0:T(8,128)} %broadcast_in_dim.40), calls=%async_computation.4 | async-start | bytes 1310720 | tf_op jit(solution)/shard_map/all_to_all | solution.py:271
  165.7 5.1 %collective-permute-start.2 = (f32[1,512]{1,0:T(1,128)}, f32[1,512]{1,0:T(1,128)S(1)}, u32[]{:S(2)}, u32[]{:S(2)}) collective-permute-start(f32[1,512]{1,0:T(1,128)} %get-tuple-element.10), channel_id=1, source_target_pairs={{8,0},{16,8},{24,16},{40,32},{48,40},{56,48},{72,64},{80,72},{88,8... | collective-permute-start | bytes 6152 | tf_op jit(solution)/shard_map/ppermute | solution.py:317

commit v2 on v1

v2 whole, which is shorter than its diff:
```python
import functools

import jax
import jax.numpy as jnp
from jax import lax
from jax.experimental import pallas as pl
from jax.experimental.pallas import tpu as pltpu
from jax.sharding import PartitionSpec as P

F32 = jnp.float32
BF16 = jnp.bfloat16
B = 128
TOL2 = 1e-12
MAX_STEPS = 4096
VMEM = 20 * 2**20


def blocks_of(rows):
    n = rows // B
    return [(i, j) for i in range(n) for j in range(i + 1)]


def mm(a, b):
    return lax.dot_general(a, b, (((1,), (0,)), ((), ())), preferred_element_type=F32)


def split3(x):
    hi = x.astype(BF16)
    rest = x - hi.astype(F32)
    mid = rest.astype(BF16)
    low = (rest - mid.astype(F32)).astype(BF16)
    return hi, mid, low


def eye_mask():
    return lax.broadcasted_iota(jnp.int32, (B, B), 0) == lax.broadcasted_iota(
        jnp.int32, (B, B), 1
    )


def gram_kernel(slot, parts, w_ref, d_ref, out_ref, scaled_ref, g_ref):
    rows = w_ref.shape[1]
    scale = d_ref[...].astype(F32)[slot : slot + 1]
    for i in range(rows // B):
        at = slice(i * B, (i + 1) * B)
        scaled_ref[at, :] = (w_ref[0, at, :].astype(F32) * scale).astype(BF16)
    for i in range(rows // B):
        at = slice(i * B, (i + 1) * B)
        g_ref[at, :] = lax.dot_general(
            scaled_ref[at, :], w_ref[0], (((1,), (1,)), ((), ())), preferred_element_type=F32
        )
    step = B // parts
    for b, (i, j) in enumerate(blocks_of(rows)):
        blk = g_ref[i * B : (i + 1) * B, j * B : (j + 1) * B]
        if i != j:
            blk = 0.5 * (blk + g_ref[j * B : (j + 1) * B, i * B : (i + 1) * B].T)
        for z in range(parts):
            out_ref[z, b * step : (b + 1) * step, :] = blk[z * step : (z + 1) * step, :]


def gram(slot, parts, matrices, ratios):
    _, rows, cols = matrices.shape
    height = len(blocks_of(rows)) * B // parts
    return pl.pallas_call(
        functools.partial(gram_kernel, slot, parts),
        grid=(1,),
        in_specs=[
            pl.BlockSpec((1, rows, cols), lambda i: (slot, 0, 0)),
            pl.BlockSpec(ratios.shape, lambda i: (0, 0)),
        ],
        out_specs=pl.BlockSpec((parts, height, B), lambda i: (0, 0, 0)),
        out_shape=jax.ShapeDtypeStruct((parts, height, B), F32),
        scratch_shapes=[pltpu.VMEM((rows, cols), BF16), pltpu.VMEM((rows, rows), F32)],
        compiler_params=pltpu.CompilerParams(vmem_limit_bytes=VMEM),
        name=f"gram{slot}",
    )(matrices, ratios)


def ratio(a, b):
    ok = b > 0.0
    return jnp.where(ok, a / jnp.where(ok, b, 1.0), 0.0)


def low_lanes(shape):
    return lax.broadcasted_iota(jnp.int32, shape, len(shape) - 1) < B // 2


def cg_block(pieces, x_ref, r_ref, p_ref, s_ref, rb_ref, sc_ref):
    hi, mid = pieces
    rows = x_ref.shape[0]
    tiles = [slice(i * B, (i + 1) * B) for i in range(rows // B)]

    def body(carry):
        k, _ = carry
        rb = rb_ref[...]
        gamma, old, was, bound = (sc_ref[i : i + 1, :] for i in range(4))
        delta = jnp.zeros_like(gamma)
        for at in tiles:
            w = mm(hi[at, :], rb) + mm(mid[at, :], rb)
            x_ref[at, :] += was * p_ref[at, :]
            p_ref[at, :] = rb_ref[at, :].astype(F32) + ratio(gamma, old) * p_ref[at, :]
            s_ref[at, :] = w + ratio(gamma, old) * s_ref[at, :]
            delta += jnp.sum(p_ref[at, :] * s_ref[at, :], axis=0, keepdims=True)
        alpha = ratio(gamma, delta)
        new = jnp.zeros_like(gamma)
        size = jnp.zeros_like(gamma)
        for at in tiles:
            r = r_ref[at, :] - alpha * s_ref[at, :]
            r_ref[at, :] = r
            rounded = r.astype(BF16)
            rb_ref[at, :] = rounded
            new += jnp.sum(r * rounded.astype(F32), axis=0, keepdims=True)
        sc_ref[0:1, :] = new
        sc_ref[1:2, :] = gamma
        sc_ref[2:3, :] = alpha
        return k + 1, jnp.max(new - bound)

    rhs = r_ref[...]
    x_ref[...] = jnp.zeros_like(rhs)
    p_ref[...] = jnp.zeros_like(rhs)
    s_ref[...] = jnp.zeros_like(rhs)
    rounded = rhs.astype(BF16)
    rb_ref[...] = rounded
    first = jnp.sum(rhs * rounded.astype(F32), axis=0, keepdims=True)
    sc_ref[0:1, :] = first
    sc_ref[1:3, :] = jnp.zeros((2,) + first.shape[1:], F32)
    sc_ref[3:4, :] = TOL2 * first
    lax.while_loop(
        lambda c: (c[0] < MAX_STEPS) & (c[1] > 0.0), body, (jnp.int32(0), jnp.max(first))
    )
    for at in tiles:
        x_ref[at, :] += sc_ref[2:3, :] * p_ref[at, :]


def solve_kernel(
    recv_ref, reg_ref, rhs_ref, link_ref, g_ref, out_ref,
    hi_ref, mid_ref, x_ref, r_ref, p_ref, s_ref, rb_ref, sc_ref,
):
    parts = recv_ref.shape[0]
    rows = g_ref.shape[0]
    step = B // parts
    eye = eye_mask()
    for b, (i, j) in enumerate(blocks_of(rows)):
        ri, rj = slice(i * B, (i + 1) * B), slice(j * B, (j + 1) * B)
        blk = jnp.concatenate(
            [recv_ref[z, b * step : (b + 1) * step, :] for z in range(parts)], axis=0
        )
        other = blk.T
        if i == j:
            blk = 0.5 * (blk + other) + jnp.where(eye, reg_ref[:, rj], 0.0)
        g_ref[ri, rj] = blk
        hi_ref[ri, rj], mid_ref[ri, rj] = split3(blk)[:2]
        if i != j:
            g_ref[rj, ri] = other
            hi_ref[rj, ri], mid_ref[rj, ri] = split3(other)[:2]
    r_ref[...] = rhs_ref[...].astype(F32)
    cg_block((hi_ref, mid_ref), x_ref, r_ref, p_ref, s_ref, rb_ref, sc_ref)
    n = x_ref.shape[1]
    pieces = jnp.concatenate(split3(x_ref[...]), axis=1)
    y = lax.dot_general(
        link_ref[...], pieces, (((0,), (0,)), ((), ())), preferred_element_type=F32
    )
    y = y[:, :n] + (y[:, n : 2 * n] + y[:, 2 * n :])
    half, quarter = B // 2, B // 4
    after = lax.rem(lax.axis_index("col") + 1, n0_blocks(rows))
    row = lax.broadcasted_iota(jnp.int32, y.shape, 0)
    lane = lax.broadcasted_iota(jnp.int32, y.shape, 1)
    start = after * half
    here = (row >= start) & (row < start + half) & (lane == 0)
    x_ref[...] = jnp.where(here, pltpu.roll(y, half, 1), y)
    low = low_lanes((quarter, B))
    for t in range(rows // B):
        for c in range(2):
            at = t * B + c * quarter
            up = pltpu.roll(x_ref[at + half : at + half + quarter, :], half, 1)
            out_ref[c, :, t, :] = jnp.where(low, x_ref[at : at + quarter, :], up)


def n0_blocks(rows):
    return rows // (B // 2)


def solve(received, reg_row, rhs, link):
    rows, width = rhs.shape
    return pl.pallas_call(
        solve_kernel,
        out_shape=(
            jax.ShapeDtypeStruct((rows, rows), F32),
            jax.ShapeDtypeStruct((2, B // 4, rows // B, B), F32),
        ),
        scratch_shapes=[pltpu.VMEM((rows, rows), BF16)] * 2
        + [pltpu.VMEM((rows, width), F32)] * 4
        + [pltpu.VMEM((rows, width), BF16), pltpu.VMEM((8, width), F32)],
        compiler_params=pltpu.CompilerParams(vmem_limit_bytes=VMEM),
        name="solve",
    )(received, reg_row, rhs, link)


def as_row(col, eye):
    return jnp.sum(jnp.where(eye, col, 0.0), axis=0, keepdims=True)


def as_col(row, eye):
    return jnp.sum(jnp.where(eye, row, 0.0), axis=1, keepdims=True)


def times_row(mat_ref, row, eye):
    rows = mat_ref.shape[0]
    out = []
    for i in range(rows // B):
        part = mat_ref[i * B : (i + 1) * B, :].astype(F32) * row
        out.append(as_row(jnp.sum(part, axis=1, keepdims=True), eye))
    return jnp.concatenate(out, axis=1)


def sym_times_row(mat_ref, row, eye):
    total = None
    for i in range(mat_ref.shape[0] // B):
        at = slice(i * B, (i + 1) * B)
        part = jnp.sum(mat_ref[at, :] * as_col(row[:, at], eye), axis=0, keepdims=True)
        total = part if total is None else total + part
    return total


def lane_sum(row):
    return jnp.sum(row, axis=1, keepdims=True)


def cg_row(mat_ref, rhs, x_ref, r_ref, p_ref, s_ref, sc_ref, eye):
    def body(carry):
        k, _ = carry
        gamma, old, bound = (sc_ref[i : i + 1, 0:1] for i in range(3))
        r = r_ref[...]
        w = sym_times_row(mat_ref, r, eye)
        beta = ratio(gamma, old)
        p = r + beta * p_ref[...]
        s = w + beta * s_ref[...]
        alpha = ratio(gamma, lane_sum(p * s))
        p_ref[...] = p
        s_ref[...] = s
        x_ref[...] += alpha * p
        r = r - alpha * s
        r_ref[...] = r
        new = lane_sum(r * r)
        sc_ref[0:1, 0:1] = new
        sc_ref[1:2, 0:1] = gamma
        return k + 1, jnp.max(new - bound)

    zero = jnp.zeros_like(rhs)
    x_ref[...] = zero
    p_ref[...] = zero
    s_ref[...] = zero
    r_ref[...] = rhs
    first = lane_sum(rhs * rhs)
    sc_ref[0:1, 0:1] = first
    sc_ref[1:2, 0:1] = jnp.zeros_like(first)
    sc_ref[2:3, 0:1] = TOL2 * first
    lax.while_loop(
        lambda c: (c[0] < MAX_STEPS) & (c[1] > 0.0), body, (jnp.int32(0), jnp.max(first))
    )
    return x_ref[...]


def main_kernel(
    mine_ref, other_ref, q_ref, c_ref, g_ref, link_ref, b_ref, first_ref, dual_ref,
    m_ref, x_ref, r_ref, p_ref, s_ref, sc_ref,
):
    quarter, shards, tiles, _ = mine_ref.shape
    half = 2 * quarter
    eye = eye_mask()
    core = lax.rem(lax.axis_index("scen"), 2)
    low = low_lanes((quarter, B))
    for src, which in ((mine_ref, core), (other_ref, 1 - core)):
        for t in range(tiles):
            top = pl.multiple_of(which * quarter + t * B, quarter)
            for m in range(shards // 2):
                v0, v1 = src[:, 2 * m, t, :], src[:, 2 * m + 1, t, :]
                at = slice(m * B, (m + 1) * B)
                m_ref[pl.ds(top, quarter), at] = jnp.where(low, v0, pltpu.roll(v1, half, 1))
                m_ref[pl.ds(top + half, quarter), at] = jnp.where(
                    low, pltpu.roll(v0, half, 1), v1
                )
    row = lax.broadcasted_iota(jnp.int32, (B, B), 0)
    lane = lax.broadcasted_iota(jnp.int32, (B, B), 1)
    rho = []
    for t in range(tiles):
        at = slice(t * B, (t + 1) * B)
        e = (t + tiles - 1) % tiles
        before = slice(e * B, (e + 1) * B)
        near, far = m_ref[at, at], m_ref[at, before]
        rho.append(as_row(jnp.where(row[:, :1] < half, far[:, half : half + 1], near[:, :1]), eye))
        give = jnp.where(
            lane[:1] < half,
            m_ref[e * B + half : e * B + half + 1, at],
            m_ref[t * B : t * B + 1, at],
        )
        give = as_col(give, eye)
        m_ref[at, at] = jnp.where((row >= half) & (lane == 0), give, near) + jnp.where(
            eye, q_ref[:, at], 0.0
        )
        m_ref[at, before] = jnp.where((row < half) & (lane == half), give, far)
    rhs = c_ref[...] - jnp.concatenate(rho, axis=1)
    refs = (x_ref, r_ref, p_ref, s_ref, sc_ref)
    first = cg_row(m_ref, rhs, *refs, eye)
    first_ref[...] = first
    pushed = b_ref[...] + times_row(link_ref, first, eye)
    dual_ref[...] = cg_row(g_ref, pushed, *refs, eye)


def main_solve(mine, other, q_row, c_row, g, link, b_row):
    n0, rows = q_row.shape[1], b_row.shape[1]
    return pl.pallas_call(
        main_kernel,
        out_shape=(
            jax.ShapeDtypeStruct((1, n0), F32),
            jax.ShapeDtypeStruct((1, rows), F32),
        ),
        scratch_shapes=[pltpu.VMEM((n0, n0), F32)]
        + [pltpu.VMEM((1, n0), F32)] * 4
        + [pltpu.VMEM((8, B), F32)],
        compiler_params=pltpu.CompilerParams(vmem_limit_bytes=VMEM),
        name="main_solve",
    )(mine, other, q_row, c_row, g, link, b_row)


def primal_kernel(tallies_ref, w_ref, d_ref, dual_ref, back_ref, y_ref, out_ref):
    held = tallies_ref[lax.axis_index("scen")]
    scale = d_ref[...].astype(F32)
    for slot, source in enumerate((dual_ref, back_ref)):
        dual = source[...]
        dual = jnp.where(held > slot, dual, jnp.zeros_like(dual))
        y_ref[slot : slot + 1, :] = dual
        out_ref[slot : slot + 1, :] = scale[slot : slot + 1] * mm(
            dual.astype(BF16), w_ref[slot]
        )


def primal(tallies, matrices, ratios, dual, back):
    return pl.pallas_call(
        primal_kernel,
        in_specs=[pl.BlockSpec(memory_space=pltpu.SMEM)]
        + [pl.BlockSpec(memory_space=pltpu.VMEM)] * 4,
        out_shape=(
            jax.ShapeDtypeStruct((2, dual.shape[1]), F32),
            jax.ShapeDtypeStruct(ratios.shape, F32),
        ),
        compiler_params=pltpu.CompilerParams(vmem_limit_bytes=VMEM),
        name="primal",
    )(tallies, matrices, ratios, dual, back)


def local(
    scen_size, col_size, matrices, ratios, damping, coupler, bounds, q_diag, c_vec, tallies
):
    n_s, n_z = scen_size, col_size
    rows = matrices.shape[1]
    n0 = coupler.shape[2]
    pos = lax.axis_index("scen")
    zpos = lax.axis_index("col")
    held = tallies[pos]
    before = tallies[jnp.maximum(pos - 1, 0)]
    own = held >= 1
    live = own | ((pos % 4 != 0) & (before == 2))
    forth = [(4 * b + i, 4 * b + i + 1) for b in range(n_s // 4) for i in range(3)]
    back = [(j, i) for i, j in forth]

    def everyone(x, axis, count, **kw):
        return lax.all_to_all(
            jnp.broadcast_to(x[None], (count,) + x.shape), axis, 0, 0, **kw
        )

    sides = [
        jnp.concatenate([coupler[k], damping[k : k + 1], bounds[k : k + 1]], axis=0)
        for k in range(2)
    ]
    side_moved = lax.ppermute(sides[1], "scen", forth)
    gram1 = gram(1, n_z, matrices, ratios)
    gram_moved = lax.ppermute(gram1, "scen", forth)
    gram0 = gram(0, n_z, matrices, ratios)
    side = jnp.where(own, sides[0], side_moved)
    link = side[:rows]
    reg_row = side[rows : rows + 1].astype(F32)
    b_row = side[rows + 1 : rows + 2].astype(F32)
    share = n0 // n_z
    width = -(-(share + 1) // B) * B
    rhs = jnp.concatenate(
        [
            lax.dynamic_slice(link, (0, zpos * share), (rows, share)),
            side[rows + 1][:, None],
            jnp.zeros((rows, width - share - 1), BF16),
        ],
        axis=1,
    )
    rhs = jnp.where(live, rhs, jnp.zeros_like(rhs))

    partial = jnp.where(own, gram0, gram_moved)
    shard = jnp.sum(lax.all_to_all(partial, "col", 0, 0), axis=0)
    g, terms = solve(everyone(shard, "col", n_z), reg_row, rhs, link)

    count = n_s // 2
    same = [[2 * i + k for i in range(count)] for k in range(2)]
    terms = terms.reshape((n_s,) + terms.shape[2:])
    mine = lax.all_to_all(terms, "scen", 0, 0, axis_index_groups=[same[0] + same[1]])
    wide = everyone(jnp.sum(mine, axis=0), "col", n_z)
    half = everyone(wide, "scen", count, axis_index_groups=same)
    other = lax.ppermute(half, "scen", [(i, i ^ 1) for i in range(n_s)])
    first, dual = main_solve(half, other, q_diag[None], c_vec[None], g, link, b_row)

    returned = lax.ppermute(dual, "scen", back)
    duals, primals = primal(tallies, matrices, ratios, dual, returned)
    return first[0], duals, primals


def solution(mesh):
    body = functools.partial(local, mesh.shape["scen"], mesh.shape["col"])
    return jax.shard_map(
        body,
        mesh=mesh,
        in_specs=(
            P("scen", None, "col"),
            P("scen", "col"),
            P("scen", None),
            P("scen", None, None),
            P("scen", None),
            P(),
            P(),
            P(),
        ),
        out_specs=(P(), P("scen", None), P("scen", "col")),
        check_vma=False,
    )
```

time: 174 us -> 151 us (0.87)
  Pallas kernels: 41.1 us -> 21.5 us
  waiting for transfers between devices: 53.2 us -> 35.1 us
  blocking collectives: 40.8 us -> 56.8 us
  other arithmetic: 3.25 us -> 1.35 us
    all_to_all x2 -> x1, waiting for transfers between devices: 33.9 us -> 15.4 us  [everyone(): lax.all_to_all(jnp.broadcast_to(x[None], (count,) + x.shape), axis, 0, 0,...]
    pallas_call x1, Pallas kernels: 15 us -> 1.04 us  [solve(): pl.pallas_call(solve_kernel, out_shape=(jax.ShapeDtypeStruct((rows, rows)...]
    all_to_all x2, blocking collectives: 18 us -> 27.6 us  [everyone(): lax.all_to_all(jnp.broadcast_to(x[None], (count,) + x.shape), axis, 0, 0,...]
    all_to_all x1, blocking collectives: 22.8 us -> 29.2 us  [local(): lax.all_to_all(terms, 'scen', 0, 0, axis_index_groups=[same[0] + same[1]])]
    ppermute x0 -> x1, starting transfers between devices: none -> 5.53 us  [local(): other = lax.ppermute(half, 'scen', [(i, i ^ 1) for i in range(n_s)])]
    pallas_call x2, Pallas kernels: 7.2 us -> 3 us  [gram(): pl.pallas_call(functools.partial(gram_kernel, slot, parts), grid=(1,), in...]
    all_to_all x2 -> x1, starting transfers between devices: 7.44 us -> 3.54 us  [everyone(): lax.all_to_all(jnp.broadcast_to(x[None], (count,) + x.shape), axis, 0, 0,...]
    all_to_all x1, waiting for transfers between devices: 13.5 us -> 10.5 us  [local(): shard = jnp.sum(lax.all_to_all(partial, 'col', 0, 0), axis=0)]
  transfers between devices with their start and end apart: 6 -> 6, of which waited for: 5 -> 5; matrix products, arithmetic and copies ran while one was open for 2% -> 2% of each run, Pallas kernels for 2% -> 1%
where the time goes in v2:
time: 151 us; the launch traced here: 152 us
  blocking collectives  56.8 us (38%)
  waiting for transfers between devices  35.1 us (23%)
  starting transfers between devices  30.3 us (20%)
  Pallas kernels  21.5 us (14%)
  local copies, waits for them, and re-layouts  4.4 us (3%)
  between operations  2.18 us (1%)
    all_to_all x1, blocking collectives, local(): lax.all_to_all(terms, 'scen', 0, 0, axis_index_groups=[same[0] + same[1]])  29.2 us
    all_to_all x2, blocking collectives, everyone(): lax.all_to_all(jnp.broadcast_to(x[None], (count,) + x.shape), axis, 0, 0,...  27.6 us
    pallas_call x1, Pallas kernels, main_solve(): pl.pallas_call(main_kernel, out_shape=(jax.ShapeDtypeStruct((1, n0), F32)...  15.9 us
    all_to_all x1, waiting for transfers between devices, everyone(): lax.all_to_all(jnp.broadcast_to(x[None], (count,) + x.shape), axis, 0, 0,...  15.4 us
    all_to_all x1, waiting for transfers between devices, local(): shard = jnp.sum(lax.all_to_all(partial, 'col', 0, 0), axis=0)  10.5 us
    all_to_all x1, starting transfers between devices, local(): shard = jnp.sum(lax.all_to_all(partial, 'col', 0, 0), axis=0)  10.2 us
    ppermute x1, starting transfers between devices, local(): other = lax.ppermute(half, 'scen', [(i, i ^ 1) for i in range(n_s)])  5.53 us
    ppermute x1, waiting for transfers between devices, local(): gram_moved = lax.ppermute(gram1, 'scen', forth)  4.72 us
  transfers between devices with their start and end apart: 6, of which 5 were waited for; matrix products, arithmetic and copies ran while one was open for 2% of the time, Pallas kernels for 1%

profile of v2, /device:TPU:1, one launch (start us, length us, event | category | flops | bytes accessed | tf_op | source)
XLA Modules:
  0.0 151.7 jit_solution(6036246780196972178)
XLA Ops:
  0.6 0.0 copy-start
  0.6 1.6 %copy-done = bf16[2,512,1024]{2,1,0:T(8,128)(2,1)S(1)} copy-done((bf16[2,512,1024]{2,1,0:T(8,128)(2,1)S(1)}, bf16[2,512,1024]{2,1,0:T(8,128)(2,1)}, u32[]{:S(2)}) %copy-start) | copy-done | bytes 2097176
  2.2 0.0 copy-start.2
  2.2 0.7 copy-done.2
  2.9 1.5 gram1.1
  4.4 4.5 %collective-permute-start = (f32[8,160,128]{2,1,0:T(8,128)S(1)}, f32[8,160,128]{2,1,0:T(8,128)S(1)}, u32[]{:S(2)}, u32[]{:S(2)}) collective-permute-start(f32[8,160,128]{2,1,0:T(8,128)S(1)} %gram1.1), channel_id=1, source_target_pairs={{0,8},{8,16},{16,24},{32,40},{40,48},{48,56},{64,72},{72,80},{80,8... | collective-permute-start | bytes 1966088 | tf_op jit(solution)/shard_map/ppermute | solution.py:378
  8.9 0.0 copy-start.4
  8.9 1.5 gram0.1
  10.5 0.0 copy-done.4
  10.5 0.6 fusion.2
  11.7 4.7 %collective-permute-done = f32[8,160,128]{2,1,0:T(8,128)S(1)} collective-permute-done((f32[8,160,128]{2,1,0:T(8,128)S(1)}, f32[8,160,128]{2,1,0:T(8,128)S(1)}, u32[]{:S(2)}, u32[]{:S(2)}) %collective-permute-start) | collective-permute-done | bytes 655392 | tf_op jit(solution)/shard_map/ppermute | solution.py:378
  16.4 0.9 broadcast_select_fusion
  17.4 0.0 copy-start.8
  17.4 0.0 copy-start.9
  17.4 0.0 copy-start.7
  17.4 10.2 %all-to-all-start = ((f32[8,160,128]{2,1,0:T(8,128)}), f32[8,160,128]{2,1,0:T(8,128)S(1)}, u32[]{:S(2)}, u32[]{:S(2)}) async-start(f32[8,160,128]{2,1,0:T(8,128)} %broadcast_select_fusion), calls=%async_computation | async-start | bytes 1310720 | tf_op jit(solution)/shard_map/all_to_all | solution.py:397
  27.5 0.0 copy-done.8
  27.5 0.0 copy-done.9
  27.6 0.0 copy-done.7
  27.6 0.1 slice_bitcast_fusion.1
  27.7 4.7 %collective-permute-start.1 = (bf16[514,512]{1,0:T(8,128)(2,1)S(1)}, bf16[514,512]{1,0:T(8,128)(2,1)S(1)}, u32[]{:S(2)}, u32[]{:S(2)}) collective-permute-start(bf16[514,512]{1,0:T(8,128)(2,1)S(1)} %pad_maximum_fusion), channel_id=1, source_target_pairs={{0,8},{8,16},{16,24},{32,40},{40,48},{48,56},{64,72},{72,80},{80,8... | collective-permute-start | bytes 1579016 | tf_op jit(solution)/shard_map/ppermute | solution.py:376
  32.4 10.5 %all-to-all-done = f32[8,160,128]{2,1,0:T(8,128)S(1)} async-done(((f32[8,160,128]{2,1,0:T(8,128)}), f32[8,160,128]{2,1,0:T(8,128)S(1)}, u32[]{:S(2)}, u32[]{:S(2)}) %all-to-all-start) | async-done | bytes 655392 | tf_op jit(solution)/shard_map/all_to_all | solution.py:397
  43.0 0.9 broadcast_in_dim.14
  43.8 3.5 %all-to-all-start.1 = ((f32[8,160,128]{2,1,0:T(8,128)}), f32[8,160,128]{2,1,0:T(8,128)S(1)}, u32[]{:S(2)}, u32[]{:S(2)}) async-start(f32[8,160,128]{2,1,0:T(8,128)} %broadcast_in_dim.14), calls=%async_computation.1 | async-start | bytes 1310720 | tf_op jit(solution)/shard_map/all_to_all | solution.py:368
  48.1 0.1 pad.2.clone
  48.2 0.0 collective-permute-done.1
  48.2 0.1 maximum_select_fusion
  48.4 0.2 copy.11
  48.6 0.1 constant_dynamic-slice_fusion
  48.7 0.1 maximum_select_fusion.1.rhs_ref
  48.8 15.4 %all-to-all-done.1.recv_ref = f32[8,160,128]{2,1,0:T(8,128)S(1)} async-done(((f32[8,160,128]{2,1,0:T(8,128)}), f32[8,160,128]{2,1,0:T(8,128)S(1)}, u32[]{:S(2)}, u32[]{:S(2)}) %all-to-all-start.1) | async-done | bytes 655392 | tf_op jit(solution)/shard_map/all_to_all | solution.py:368
  64.2 1.0 solve.1
  65.2 0.0 copy-start.5
  65.2 0.0 copy-start.6
  65.2 29.2 %all_to_all.25 = f32[64,4,128]{2,1,0:T(4,128)S(1)} all-to-all(f32[64,4,128]{2,1,0:T(4,128)S(1)} %bitcast.12), channel_id=1, replica_groups={{0,16,32,48,64,80,96,112,128,144,160,176,192,208,224,240,256,272,288,30..., dimensions={0} | all-to-all | bytes 262144 | tf_op jit(solution)/shard_map/all_to_all | solution.py:403
  94.5 0.1 reduce_sum.19
  94.6 9.0 %all_to_all.26 = f32[8,4,128]{2,1,0:T(4,128)S(1)} all-to-all(f32[8,4,128]{2,1,0:T(4,128)S(1)} %broadcast_in_dim.33), channel_id=1, replica_groups=mesh['scen'=64,'col'=8] {'col'}, dimensions={0} | all-to-all | bytes 32768 | tf_op jit(solution)/shard_map/all_to_all | solution.py:368
  103.6 0.1 broadcast_in_dim.34
  103.7 18.6 %all_to_all.27.mine_ref = f32[32,8,4,128]{3,2,1,0:T(4,128)S(1)} all-to-all(f32[32,8,4,128]{3,2,1,0:T(4,128)S(1)} %broadcast_in_dim.34), channel_id=1, replica_groups={{0,16,32,48,64,80,96,112,128,144,160,176,192,208,224,240,256,272,288,30..., dimensions={0} | all-to-all | bytes 1048576 | tf_op jit(solution)/shard_map/all_to_all | solution.py:368
  122.3 5.5 %collective-permute-start.2 = (f32[32,8,4,128]{3,2,1,0:T(4,128)S(1)}, f32[32,8,4,128]{3,2,1,0:T(4,128)S(1)}, u32[]{:S(2)}, u32[]{:S(2)}) collective-permute-start(f32[32,8,4,128]{3,2,1,0:T(4,128)S(1)} %all_to_all.27.mine_ref), channel_id=1, source_target_pairs={{0,8},{8,0},{16,24},{24,16},{32,40},{40,32},{48,56},{56,48},{64,72... | collective-permute-start | bytes 1572872 | tf_op jit(solution)/shard_map/ppermute | solution.py:406
  127.8 1.5 collective-permute-done.2.other_ref
  129.3 0.0 copy-done.5
  129.3 0.0 copy-done.6
  129.3 0.0 copy-start.1
  129.3 0.0 copy-start.3
  129.3 15.9 %main_solve.1 = (f32[1,512]{1,0:T(1,128)}, f32[1,512]{1,0:T(1,128)S(1)}) custom-call(f32[32,8,4,128]{3,2,1,0:T(4,128)S(1)} %all_to_all.27.mine_ref, f32[32,8,4,128]{3,2,1,0:T(4,128)S(1)} %collective-permute-done.2.other_ref, f32[1,512]{1,0:T(1,128)S(1)} %bitcast.13, f32[1,512]{1,0:T(1,128)S(1)} %bitcast.14, f32[512,512]{1,0:T(8,128)S(1)} %get-tuple-element.10.g_ref, ...), custom_call_target="tpu_custom_call" | custom-call | tf_op jit(solution)/shard_map/main_solve/pallas_call | solution.py:312
  145.3 1.9 %collective-permute-start.3 = (f32[1,512]{1,0:T(1,128)S(1)}, f32[1,512]{1,0:T(1,128)S(1)}, u32[]{:S(2)}, u32[]{:S(2)}) collective-permute-start(f32[1,512]{1,0:T(1,128)S(1)} %get-tuple-element.12.dual_ref), channel_id=1, source_target_pairs={{8,0},{16,8},{24,16},{40,32},{48,40},{56,48},{72,64},{80,72},{88,8... | collective-permute-start | bytes 6152 | tf_op jit(solution)/shard_map/ppermute | solution.py:409
  147.2 3.0 %collective-permute-done.3.back_ref = f32[1,512]{1,0:T(1,128)S(1)} collective-permute-done((f32[1,512]{1,0:T(1,128)S(1)}, f32[1,512]{1,0:T(1,128)S(1)}, u32[]{:S(2)}, u32[]{:S(2)}) %collective-permute-start.3) | collective-permute-done | bytes 2080 | tf_op jit(solution)/shard_map/ppermute | solution.py:409
  150.2 0.0 copy-done.1
  150.2 0.0 copy-done.3
  150.2 1.5 %primal.1 = (f32[2,512]{1,0:T(2,128)}, f32[2,1024]{1,0:T(2,128)}) custom-call(s32[64]{0:T(128)S(1)} %copy-done.4, bf16[2,512,1024]{2,1,0:T(8,128)(2,1)S(1)} %copy-done.1, bf16[2,1024]{1,0:T(2,128)(2,1)S(1)} %copy-done.3, f32[1,512]{1,0:T(1,128)S(1)} %get-tuple-element.12.dual_ref, f32[1,512]{1,0:T(1,128)S(1)} %collective-permute-done.3.back_ref), custom_call_target="tpu_custom_call" | custom-call | tf_op jit(solution)/shard_map/primal/pallas_call | solution.py:339
  (7 shorter events, 0.1 us)
Async XLA Ops:
  0.6 1.6 %copy-start = (bf16[2,512,1024]{2,1,0:T(8,128)(2,1)S(1)}, bf16[2,512,1024]{2,1,0:T(8,128)(2,1)}, u32[]{:S(2)}) copy-start(bf16[2,512,1024]{2,1,0:T(8,128)(2,1)} %w_ref.5) | copy-start | bytes 6291460
  2.2 0.7 copy-start.2
  4.4 12.0 %collective-permute-start = (f32[8,160,128]{2,1,0:T(8,128)S(1)}, f32[8,160,128]{2,1,0:T(8,128)S(1)}, u32[]{:S(2)}, u32[]{:S(2)}) collective-permute-start(f32[8,160,128]{2,1,0:T(8,128)S(1)} %gram1.1), channel_id=1, source_target_pairs={{0,8},{8,16},{16,24},{32,40},{40,48},{48,56},{64,72},{72,80},{80,8... | collective-permute-start | bytes 1966088 | tf_op jit(solution)/shard_map/ppermute | solution.py:378
  8.9 1.5 %copy-start.4 = (s32[64]{0:T(128)S(1)}, s32[64]{0:T(128)}, u32[]{:S(2)}) copy-start(s32[64]{0:T(128)} %tallies_ref.1) | copy-start | bytes 772
  17.4 10.2 %copy-start.8 = (bf16[2,512]{1,0:T(2,128)(2,1)S(1)}, bf16[2,512]{1,0:T(2,128)(2,1)}, u32[]{:S(2)}) copy-start(bf16[2,512]{1,0:T(2,128)(2,1)} %param.10) | copy-start | bytes 6148
  17.4 10.2 %copy-start.9 = (bf16[2,512]{1,0:T(2,128)(2,1)S(1)}, bf16[2,512]{1,0:T(2,128)(2,1)}, u32[]{:S(2)}) copy-start(bf16[2,512]{1,0:T(2,128)(2,1)} %param.12) | copy-start | bytes 6148
  17.4 10.2 %copy-start.7 = (bf16[2,512,512]{2,1,0:T(8,128)(2,1)S(1)}, bf16[2,512,512]{2,1,0:T(8,128)(2,1)}, u32[]{:S(2)}) copy-start(bf16[2,512,512]{2,1,0:T(8,128)(2,1)} %param.11) | copy-start | bytes 3145732
  17.4 25.5 %all-to-all-start = ((f32[8,160,128]{2,1,0:T(8,128)}), f32[8,160,128]{2,1,0:T(8,128)S(1)}, u32[]{:S(2)}, u32[]{:S(2)}) async-start(f32[8,160,128]{2,1,0:T(8,128)} %broadcast_select_fusion), calls=%async_computation | async-start | bytes 1310720 | tf_op jit(solution)/shard_map/all_to_all | solution.py:397
  27.7 20.5 %collective-permute-start.1 = (bf16[514,512]{1,0:T(8,128)(2,1)S(1)}, bf16[514,512]{1,0:T(8,128)(2,1)S(1)}, u32[]{:S(2)}, u32[]{:S(2)}) collective-permute-start(bf16[514,512]{1,0:T(8,128)(2,1)S(1)} %pad_maximum_fusion), channel_id=1, source_target_pairs={{0,8},{8,16},{16,24},{32,40},{40,48},{48,56},{64,72},{72,80},{80,8... | collective-permute-start | bytes 1579016 | tf_op jit(solution)/shard_map/ppermute | solution.py:376
  43.8 20.3 %all-to-all-start.1 = ((f32[8,160,128]{2,1,0:T(8,128)}), f32[8,160,128]{2,1,0:T(8,128)S(1)}, u32[]{:S(2)}, u32[]{:S(2)}) async-start(f32[8,160,128]{2,1,0:T(8,128)} %broadcast_in_dim.14), calls=%async_computation.1 | async-start | bytes 1310720 | tf_op jit(solution)/shard_map/all_to_all | solution.py:368
  65.2 64.1 %copy-start.5 = (f32[512]{0:T(512)S(1)}, f32[512]{0:T(512)}, u32[]{:S(2)}) copy-start(f32[512]{0:T(512)} %param.13) | copy-start | bytes 6148
  65.2 64.1 %copy-start.6 = (f32[512]{0:T(512)S(1)}, f32[512]{0:T(512)}, u32[]{:S(2)}) copy-start(f32[512]{0:T(512)} %param.14) | copy-start | bytes 6148
  122.3 7.0 %collective-permute-start.2 = (f32[32,8,4,128]{3,2,1,0:T(4,128)S(1)}, f32[32,8,4,128]{3,2,1,0:T(4,128)S(1)}, u32[]{:S(2)}, u32[]{:S(2)}) collective-permute-start(f32[32,8,4,128]{3,2,1,0:T(4,128)S(1)} %all_to_all.27.mine_ref), channel_id=1, source_target_pairs={{0,8},{8,0},{16,24},{24,16},{32,40},{40,32},{48,56},{56,48},{64,72... | collective-permute-start | bytes 1572872 | tf_op jit(solution)/shard_map/ppermute | solution.py:406
  129.3 20.8 %copy-start.1 = (bf16[2,512,1024]{2,1,0:T(8,128)(2,1)S(1)}, bf16[2,512,1024]{2,1,0:T(8,128)(2,1)}, u32[]{:S(2)}) copy-start(bf16[2,512,1024]{2,1,0:T(8,128)(2,1)} %w_ref.5) | copy-start | bytes 6291460
  129.3 20.8 %copy-start.3 = (bf16[2,1024]{1,0:T(2,128)(2,1)S(1)}, bf16[2,1024]{1,0:T(2,128)(2,1)}, u32[]{:S(2)}) copy-start(bf16[2,1024]{1,0:T(2,128)(2,1)} %d_ref.5) | copy-start | bytes 12292
  145.3 4.9 %collective-permute-start.3 = (f32[1,512]{1,0:T(1,128)S(1)}, f32[1,512]{1,0:T(1,128)S(1)}, u32[]{:S(2)}, u32[]{:S(2)}) collective-permute-start(f32[1,512]{1,0:T(1,128)S(1)} %get-tuple-element.12.dual_ref), channel_id=1, source_target_pairs={{8,0},{16,8},{24,16},{40,32},{48,40},{56,48},{72,64},{80,72},{88,8... | collective-permute-start | bytes 6152 | tf_op jit(solution)/shard_map/ppermute | solution.py:409

commit v3 on v2

--- a/solution.py
+++ b/solution.py
@@ -10,7 +10,7 @@
 F32 = jnp.float32
 BF16 = jnp.bfloat16
 B = 128
-TOL2 = 1e-12
+TOL2 = 1e-11
 MAX_STEPS = 4096
 VMEM = 20 * 2**20
 
@@ -38,22 +38,31 @@
     )
 
 
-def gram_kernel(slot, parts, w_ref, d_ref, out_ref, scaled_ref, g_ref):
-    rows = w_ref.shape[1]
+def gram_kernel(slot, parts, w_hbm, d_hbm, out_ref, w_ref, d_ref, scaled_ref, g_ref, sem):
+    rows = w_ref.shape[0]
+    tiles = [slice(i * B, (i + 1) * B) for i in range(rows // B)]
+    scale_copy = pltpu.make_async_copy(d_hbm, d_ref, sem.at[len(tiles)])
+    copies = [
+        pltpu.make_async_copy(w_hbm.at[slot, at, :], w_ref.at[at, :], sem.at[i])
+        for i, at in enumerate(tiles)
+    ]
+    scale_copy.start()
+    for copy in copies:
+        copy.start()
+    scale_copy.wait()
     scale = d_ref[...].astype(F32)[slot : slot + 1]
-    for i in range(rows // B):
-        at = slice(i * B, (i + 1) * B)
-        scaled_ref[at, :] = (w_ref[0, at, :].astype(F32) * scale).astype(BF16)
-    for i in range(rows // B):
-        at = slice(i * B, (i + 1) * B)
+    for at, copy in zip(tiles, copies):
+        copy.wait()
+        scaled_ref[at, :] = (w_ref[at, :].astype(F32) * scale).astype(BF16)
+    for at in tiles:
         g_ref[at, :] = lax.dot_general(
-            scaled_ref[at, :], w_ref[0], (((1,), (1,)), ((), ())), preferred_element_type=F32
+            scaled_ref[at, :], w_ref[...], (((1,), (1,)), ((), ())), preferred_element_type=F32
         )
     step = B // parts
     for b, (i, j) in enumerate(blocks_of(rows)):
-        blk = g_ref[i * B : (i + 1) * B, j * B : (j + 1) * B]
+        blk = g_ref[tiles[i], tiles[j]]
         if i != j:
-            blk = 0.5 * (blk + g_ref[j * B : (j + 1) * B, i * B : (i + 1) * B].T)
+            blk = 0.5 * (blk + g_ref[tiles[j], tiles[i]].T)
         for z in range(parts):
             out_ref[z, b * step : (b + 1) * step, :] = blk[z * step : (z + 1) * step, :]
 
@@ -63,14 +72,15 @@
     height = len(blocks_of(rows)) * B // parts
     return pl.pallas_call(
         functools.partial(gram_kernel, slot, parts),
-        grid=(1,),
-        in_specs=[
-            pl.BlockSpec((1, rows, cols), lambda i: (slot, 0, 0)),
-            pl.BlockSpec(ratios.shape, lambda i: (0, 0)),
+        in_specs=[pl.BlockSpec(memory_space=pl.ANY)] * 2,
+        out_shape=jax.ShapeDtypeStruct((parts, height, B), F32),
+        scratch_shapes=[
+            pltpu.VMEM((rows, cols), BF16),
+            pltpu.VMEM(ratios.shape, BF16),
+            pltpu.VMEM((rows, cols), BF16),
+            pltpu.VMEM((rows, rows), F32),
+            pltpu.SemaphoreType.DMA((rows // B + 1,)),
         ],
-        out_specs=pl.BlockSpec((parts, height, B), lambda i: (0, 0, 0)),
-        out_shape=jax.ShapeDtypeStruct((parts, height, B), F32),
-        scratch_shapes=[pltpu.VMEM((rows, cols), BF16), pltpu.VMEM((rows, rows), F32)],
         compiler_params=pltpu.CompilerParams(vmem_limit_bytes=VMEM),
         name=f"gram{slot}",
     )(matrices, ratios)
@@ -113,7 +123,7 @@
         sc_ref[0:1, :] = new
         sc_ref[1:2, :] = gamma
         sc_ref[2:3, :] = alpha
-        return k + 1, jnp.max(new - bound)
+        return k + 1, jnp.max(gamma - bound)
 
     rhs = r_ref[...]
     x_ref[...] = jnp.zeros_like(rhs)
@@ -229,22 +239,22 @@
 def cg_row(mat_ref, rhs, x_ref, r_ref, p_ref, s_ref, sc_ref, eye):
     def body(carry):
         k, _ = carry
-        gamma, old, bound = (sc_ref[i : i + 1, 0:1] for i in range(3))
+        old, bound, scale = (sc_ref[i : i + 1, 0:1] for i in range(3))
         r = r_ref[...]
+        gamma = lane_sum(r * r)
         w = sym_times_row(mat_ref, r, eye)
+        delta = lane_sum(r * w)
         beta = ratio(gamma, old)
+        alpha = ratio(gamma, delta - beta * gamma * scale)
         p = r + beta * p_ref[...]
         s = w + beta * s_ref[...]
-        alpha = ratio(gamma, lane_sum(p * s))
         p_ref[...] = p
         s_ref[...] = s
         x_ref[...] += alpha * p
-        r = r - alpha * s
-        r_ref[...] = r
-        new = lane_sum(r * r)
-        sc_ref[0:1, 0:1] = new
-        sc_ref[1:2, 0:1] = gamma
-        return k + 1, jnp.max(new - bound)
+        r_ref[...] = r - alpha * s
+        sc_ref[0:1, 0:1] = gamma
+        sc_ref[2:3, 0:1] = ratio(jnp.ones_like(alpha), alpha)
+        return k + 1, jnp.max(gamma - bound)
 
     zero = jnp.zeros_like(rhs)
     x_ref[...] = zero
@@ -252,9 +262,9 @@
     s_ref[...] = zero
     r_ref[...] = rhs
     first = lane_sum(rhs * rhs)
-    sc_ref[0:1, 0:1] = first
-    sc_ref[1:2, 0:1] = jnp.zeros_like(first)
-    sc_ref[2:3, 0:1] = TOL2 * first
+    sc_ref[0:1, 0:1] = jnp.zeros_like(first)
+    sc_ref[1:2, 0:1] = TOL2 * first
+    sc_ref[2:3, 0:1] = jnp.zeros_like(first)
     lax.while_loop(
         lambda c: (c[0] < MAX_STEPS) & (c[1] > 0.0), body, (jnp.int32(0), jnp.max(first))
     )
@@ -358,11 +368,9 @@
     pos = lax.axis_index("scen")
     zpos = lax.axis_index("col")
     held = tallies[pos]
-    before = tallies[jnp.maximum(pos - 1, 0)]
     own = held >= 1
-    live = own | ((pos % 4 != 0) & (before == 2))
-    forth = [(4 * b + i, 4 * b + i + 1) for b in range(n_s // 4) for i in range(3)]
-    back = [(j, i) for i, j in forth]
+    live = own | (tallies[pos ^ 1] == 2)
+    partner = [(i, i ^ 1) for i in range(n_s)]
 
     def everyone(x, axis, count, **kw):
         return lax.all_to_all(
@@ -373,9 +381,9 @@
         jnp.concatenate([coupler[k], damping[k : k + 1], bounds[k : k + 1]], axis=0)
         for k in range(2)
     ]
-    side_moved = lax.ppermute(sides[1], "scen", forth)
+    side_moved = lax.ppermute(sides[1], "scen", partner)
     gram1 = gram(1, n_z, matrices, ratios)
-    gram_moved = lax.ppermute(gram1, "scen", forth)
+    gram_moved = lax.ppermute(gram1, "scen", partner)
     gram0 = gram(0, n_z, matrices, ratios)
     side = jnp.where(own, sides[0], side_moved)
     link = side[:rows]
@@ -403,10 +411,10 @@
     mine = lax.all_to_all(terms, "scen", 0, 0, axis_index_groups=[same[0] + same[1]])
     wide = everyone(jnp.sum(mine, axis=0), "col", n_z)
     half = everyone(wide, "scen", count, axis_index_groups=same)
-    other = lax.ppermute(half, "scen", [(i, i ^ 1) for i in range(n_s)])
+    other = lax.ppermute(half, "scen", partner)
     first, dual = main_solve(half, other, q_diag[None], c_vec[None], g, link, b_row)
 
-    returned = lax.ppermute(dual, "scen", back)
+    returned = lax.ppermute(dual, "scen", partner)
     duals, primals = primal(tallies, matrices, ratios, dual, returned)
     return first[0], duals, primals
 

time: 151 us -> 150 us (level); the launches traced: 152 us -> 149 us
  blocking collectives: 56.8 us -> 48.9 us
  local copies, waits for them, and re-layouts: 4.4 us -> 7.08 us
  Pallas kernels: 21.5 us -> 23.8 us
  starting transfers between devices: 30.3 us -> 28.2 us
  other arithmetic: 1.35 us -> 2.89 us
    all_to_all x1, blocking collectives: 29.2 us -> 21.1 us  [local(): lax.all_to_all(terms, 'scen', 0, 0, axis_index_groups=[same[0] + same[1]])]
    ppermute x4, waiting for transfers between devices: 9.21 us -> 2.32 us  [the longest x1 1.51 us: local(): other = lax.ppermute(half, 'scen', partner)]
    pallas_call x1, Pallas kernels: 1.04 us -> 7.24 us  [solve(): pl.pallas_call(solve_kernel, out_shape=(jax.ShapeDtypeStruct((rows, rows)...]
    all_to_all x1, starting transfers between devices: 10.2 us -> 4.83 us  [local(): shard = jnp.sum(lax.all_to_all(partial, 'col', 0, 0), axis=0)]
    all_to_all x1, waiting for transfers between devices: 10.5 us -> 15.3 us  [local(): shard = jnp.sum(lax.all_to_all(partial, 'col', 0, 0), axis=0)]
    pallas_call x1, Pallas kernels: 15.9 us -> 11.5 us  [main_solve(): pl.pallas_call(main_kernel, out_shape=(jax.ShapeDtypeStruct((1, n0), F32)...]
    ppermute x4, starting transfers between devices: 16.6 us -> 19.8 us  [the longest x1 8.75 us: local(): gram_moved = lax.ppermute(gram1, 'scen', partner)]
    all_to_all x1, waiting for transfers between devices: 15.4 us -> 18.1 us  [everyone(): lax.all_to_all(jnp.broadcast_to(x[None], (count,) + x.shape), axis, 0, 0,...]
  transfers between devices with their start and end apart: 6 -> 6, of which waited for: 5 -> 4; matrix products, arithmetic and copies ran while one was open for 2% -> 4% of each run, Pallas kernels for 1% -> 1%
where the time goes in v3:
time: 150 us; the launch traced here: 149 us
  blocking collectives  48.9 us (33%)
  waiting for transfers between devices  35.8 us (24%)
  starting transfers between devices  28.2 us (19%)
  Pallas kernels  23.8 us (16%)
  local copies, waits for them, and re-layouts  7.08 us (5%)
  other arithmetic  2.89 us (2%)
  between operations  2.17 us (1%)
    all_to_all x2, blocking collectives, everyone(): lax.all_to_all(jnp.broadcast_to(x[None], (count,) + x.shape), axis, 0, 0,...  27.7 us
    all_to_all x1, blocking collectives, local(): lax.all_to_all(terms, 'scen', 0, 0, axis_index_groups=[same[0] + same[1]])  21.1 us
    all_to_all x1, waiting for transfers between devices, everyone(): lax.all_to_all(jnp.broadcast_to(x[None], (count,) + x.shape), axis, 0, 0,...  18.1 us
    all_to_all x1, waiting for transfers between devices, local(): shard = jnp.sum(lax.all_to_all(partial, 'col', 0, 0), axis=0)  15.3 us
    pallas_call x1, Pallas kernels, main_solve(): pl.pallas_call(main_kernel, out_shape=(jax.ShapeDtypeStruct((1, n0), F32)...  11.5 us
    ppermute x1, starting transfers between devices, local(): gram_moved = lax.ppermute(gram1, 'scen', partner)  8.75 us
    pallas_call x1, Pallas kernels, solve(): pl.pallas_call(solve_kernel, out_shape=(jax.ShapeDtypeStruct((rows, rows)...  7.24 us
    ppermute x1, starting transfers between devices, local(): other = lax.ppermute(half, 'scen', partner)  5.53 us
  transfers between devices with their start and end apart: 6, of which 4 were waited for; matrix products, arithmetic and copies ran while one was open for 4% of the time, Pallas kernels for 1%

profile of v3, /device:TPU:1, one launch (start us, length us, event | category | flops | bytes accessed | tf_op | source)
XLA Modules:
  0.0 148.8 jit_solution(10281814844916876663)
XLA Ops:
  0.6 0.0 copy-start
  0.6 1.6 %copy-done = bf16[2,512,1024]{2,1,0:T(8,128)(2,1)S(1)} copy-done((bf16[2,512,1024]{2,1,0:T(8,128)(2,1)S(1)}, bf16[2,512,1024]{2,1,0:T(8,128)(2,1)}, u32[]{:S(2)}) %copy-start) | copy-done | bytes 2097176
  2.2 0.0 copy-start.4
  2.2 0.7 copy-done.4
  2.9 0.0 copy-start.1
  2.9 0.0 copy-start.5
  2.9 1.8 %gram1.1 = f32[8,160,128]{2,1,0:T(8,128)S(1)} custom-call(bf16[2,512,1024]{2,1,0:T(8,128)(2,1)S(1)} %copy-done, bf16[2,1024]{1,0:T(2,128)(2,1)S(1)} %copy-done.4), custom_call_target="tpu_custom_call" | custom-call | tf_op jit(solution)/shard_map/gram1/pallas_call | solution.py:73
  4.7 8.7 %collective-permute-start = (f32[8,160,128]{2,1,0:T(8,128)S(1)}, f32[8,160,128]{2,1,0:T(8,128)}, u32[]{:S(2)}, u32[]{:S(2)}) collective-permute-start(f32[8,160,128]{2,1,0:T(8,128)S(1)} %gram1.1), channel_id=1, source_target_pairs={{0,8},{8,0},{16,24},{24,16},{32,40},{40,32},{48,56},{56,48},{64,72... | collective-permute-start | bytes 1966088 | tf_op jit(solution)/shard_map/ppermute | solution.py:386
  13.5 0.0 copy-done.1
  13.5 0.0 copy-done.5
  13.5 0.0 copy-start.6
  13.5 1.8 %gram0.1 = f32[8,160,128]{2,1,0:T(8,128)S(1)} custom-call(bf16[2,512,1024]{2,1,0:T(8,128)(2,1)S(1)} %copy-done.1, bf16[2,1024]{1,0:T(2,128)(2,1)S(1)} %copy-done.5), custom_call_target="tpu_custom_call" | custom-call | tf_op jit(solution)/shard_map/gram0/pallas_call | solution.py:73
  15.3 0.0 copy-done.6
  15.4 0.6 fusion.2
  16.6 0.0 collective-permute-done
  16.6 1.0 broadcast_select_fusion
  17.6 0.0 copy-start.9
  17.6 0.0 copy-start.10
  17.6 4.8 %all-to-all-start = ((f32[8,160,128]{2,1,0:T(8,128)}), f32[8,160,128]{2,1,0:T(8,128)S(1)}, u32[]{:S(2)}, u32[]{:S(2)}) async-start(f32[8,160,128]{2,1,0:T(8,128)} %broadcast_select_fusion), calls=%async_computation | async-start | bytes 1310720 | tf_op jit(solution)/shard_map/all_to_all | solution.py:405
  22.4 0.0 copy-done.9
  22.4 0.0 copy-done.10
  22.5 1.3 slice_bitcast_fusion.1
  23.7 0.9 pad_maximum_fusion
  24.6 3.3 %collective-permute-start.1 = (bf16[514,512]{1,0:T(8,128)(2,1)}, bf16[514,512]{1,0:T(8,128)(2,1)}, u32[]{:S(2)}, u32[]{:S(2)}) collective-permute-start(bf16[514,512]{1,0:T(8,128)(2,1)} %pad_maximum_fusion), channel_id=1, source_target_pairs={{0,8},{8,0},{16,24},{24,16},{32,40},{40,32},{48,56},{56,48},{64,72... | collective-permute-start | bytes 1579016 | tf_op jit(solution)/shard_map/ppermute | solution.py:384
  27.9 15.3 %all-to-all-done = f32[8,160,128]{2,1,0:T(8,128)S(1)} async-done(((f32[8,160,128]{2,1,0:T(8,128)}), f32[8,160,128]{2,1,0:T(8,128)S(1)}, u32[]{:S(2)}, u32[]{:S(2)}) %all-to-all-start) | async-done | bytes 655392 | tf_op jit(solution)/shard_map/all_to_all | solution.py:405
  43.2 0.9 broadcast_in_dim.14
  44.1 3.5 %all-to-all-start.1 = ((f32[8,160,128]{2,1,0:T(8,128)}), f32[8,160,128]{2,1,0:T(8,128)S(1)}, u32[]{:S(2)}, u32[]{:S(2)}) async-start(f32[8,160,128]{2,1,0:T(8,128)} %broadcast_in_dim.14), calls=%async_computation.1 | async-start | bytes 1310720 | tf_op jit(solution)/shard_map/all_to_all | solution.py:376
  48.3 0.6 pad.2.clone
  48.9 0.0 collective-permute-done.1
  48.9 0.1 maximum_select_fusion
  49.1 0.2 copy.11
  49.3 0.1 constant_dynamic-slice_fusion
  49.4 0.8 maximum_select_fusion.1.rhs_ref
  50.2 18.1 %all-to-all-done.1.recv_ref = f32[8,160,128]{2,1,0:T(8,128)S(1)} async-done(((f32[8,160,128]{2,1,0:T(8,128)}), f32[8,160,128]{2,1,0:T(8,128)S(1)}, u32[]{:S(2)}, u32[]{:S(2)}) %all-to-all-start.1) | async-done | bytes 655392 | tf_op jit(solution)/shard_map/all_to_all | solution.py:376
  68.4 7.2 %solve.1 = (f32[512,512]{1,0:T(8,128)S(1)}, f32[2,32,4,128]{3,2,1,0:T(4,128)S(1)}) custom-call(f32[8,160,128]{2,1,0:T(8,128)S(1)} %all-to-all-done.1.recv_ref, f32[1,512]{1,0:T(1,128)S(1)} %get-tuple-element.19.reg_ref, bf16[512,128]{1,0:T(8,128)(2,1)S(1)} %maximum_select_fusion.1.rhs_ref, bf16[512,512]{1,0:T(8,128)(2,1)S(1)} %slice.38.link_ref), custom_call_target="tpu_custom_call" | custom-call | tf_op jit(solution)/shard_map/solve/pallas_call | solution.py:195
  75.6 0.0 copy-start.2
  75.6 1.0 copy-done.2
  76.6 0.0 copy-start.7
  76.6 0.0 copy-start.8
  76.6 21.1 %all_to_all.25 = f32[64,4,128]{2,1,0:T(4,128)S(1)} all-to-all(f32[64,4,128]{2,1,0:T(4,128)S(1)} %bitcast.12), channel_id=1, replica_groups={{0,16,32,48,64,80,96,112,128,144,160,176,192,208,224,240,256,272,288,30..., dimensions={0} | all-to-all | bytes 262144 | tf_op jit(solution)/shard_map/all_to_all | solution.py:411
  97.7 0.1 reduce_sum.19
  97.8 0.0 copy-start.3
  97.8 9.1 %all_to_all.26 = f32[8,4,128]{2,1,0:T(4,128)S(1)} all-to-all(f32[8,4,128]{2,1,0:T(4,128)S(1)} %broadcast_in_dim.33), channel_id=1, replica_groups=mesh['scen'=64,'col'=8] {'col'}, dimensions={0} | all-to-all | bytes 32768 | tf_op jit(solution)/shard_map/all_to_all | solution.py:376
  106.9 0.1 broadcast_in_dim.34
  107.1 18.6 %all_to_all.27.mine_ref = f32[32,8,4,128]{3,2,1,0:T(4,128)S(1)} all-to-all(f32[32,8,4,128]{3,2,1,0:T(4,128)S(1)} %broadcast_in_dim.34), channel_id=1, replica_groups={{0,16,32,48,64,80,96,112,128,144,160,176,192,208,224,240,256,272,288,30..., dimensions={0} | all-to-all | bytes 1048576 | tf_op jit(solution)/shard_map/all_to_all | solution.py:376
  125.7 5.5 %collective-permute-start.2 = (f32[32,8,4,128]{3,2,1,0:T(4,128)S(1)}, f32[32,8,4,128]{3,2,1,0:T(4,128)S(1)}, u32[]{:S(2)}, u32[]{:S(2)}) collective-permute-start(f32[32,8,4,128]{3,2,1,0:T(4,128)S(1)} %all_to_all.27.mine_ref), channel_id=1, source_target_pairs={{0,8},{8,0},{16,24},{24,16},{32,40},{40,32},{48,56},{56,48},{64,72... | collective-permute-start | bytes 1572872 | tf_op jit(solution)/shard_map/ppermute | solution.py:414
  131.2 1.5 %collective-permute-done.2.other_ref = f32[32,8,4,128]{3,2,1,0:T(4,128)S(1)} collective-permute-done((f32[32,8,4,128]{3,2,1,0:T(4,128)S(1)}, f32[32,8,4,128]{3,2,1,0:T(4,128)S(1)}, u32[]{:S(2)}, u32[]{:S(2)}) %collective-permute-start.2) | collective-permute-done | bytes 524320 | tf_op jit(solution)/shard_map/ppermute | solution.py:414
  132.7 0.0 copy-done.7
  132.7 0.0 copy-done.8
  132.7 0.0 copy-done.3
  132.7 11.5 %main_solve.1 = (f32[1,512]{1,0:T(1,128)}, f32[1,512]{1,0:T(1,128)S(1)}) custom-call(f32[32,8,4,128]{3,2,1,0:T(4,128)S(1)} %all_to_all.27.mine_ref, f32[32,8,4,128]{3,2,1,0:T(4,128)S(1)} %collective-permute-done.2.other_ref, f32[1,512]{1,0:T(1,128)S(1)} %bitcast.13, f32[1,512]{1,0:T(1,128)S(1)} %bitcast.14, f32[512,512]{1,0:T(8,128)S(1)} %copy-done.3, ...), custom_call_target="tpu_custom_call" | custom-call | tf_op jit(solution)/shard_map/main_solve/pallas_call | solution.py:322
  144.2 2.3 %collective-permute-start.3 = (f32[1,512]{1,0:T(1,128)S(1)}, f32[1,512]{1,0:T(1,128)S(1)}, u32[]{:S(2)}, u32[]{:S(2)}) collective-permute-start(f32[1,512]{1,0:T(1,128)S(1)} %get-tuple-element.12.dual_ref), channel_id=1, source_target_pairs={{0,8},{8,0},{16,24},{24,16},{32,40},{40,32},{48,56},{56,48},{64,72... | collective-permute-start | bytes 6152 | tf_op jit(solution)/shard_map/ppermute | solution.py:417
  146.5 0.8 collective-permute-done.3.back_ref
  147.3 1.5 %primal.1 = (f32[2,512]{1,0:T(2,128)}, f32[2,1024]{1,0:T(2,128)}) custom-call(s32[64]{0:T(128)S(1)} %copy-done.6, bf16[2,512,1024]{2,1,0:T(8,128)(2,1)S(1)} %copy-done.1, bf16[2,1024]{1,0:T(2,128)(2,1)S(1)} %copy-done.5, f32[1,512]{1,0:T(1,128)S(1)} %get-tuple-element.12.dual_ref, f32[1,512]{1,0:T(1,128)S(1)} %collective-permute-done.3.back_ref), custom_call_target="tpu_custom_call" | custom-call | tf_op jit(solution)/shard_map/primal/pallas_call | solution.py:349
  (6 shorter events, 0.1 us)
Async XLA Ops:
  0.6 1.6 %copy-start = (bf16[2,512,1024]{2,1,0:T(8,128)(2,1)S(1)}, bf16[2,512,1024]{2,1,0:T(8,128)(2,1)}, u32[]{:S(2)}) copy-start(bf16[2,512,1024]{2,1,0:T(8,128)(2,1)} %w_ref.1) | copy-start | bytes 6291460
  2.2 0.7 copy-start.4
  2.9 10.6 %copy-start.1 = (bf16[2,512,1024]{2,1,0:T(8,128)(2,1)S(1)}, bf16[2,512,1024]{2,1,0:T(8,128)(2,1)}, u32[]{:S(2)}) copy-start(bf16[2,512,1024]{2,1,0:T(8,128)(2,1)} %w_ref.1) | copy-start | bytes 6291460
  2.9 10.6 %copy-start.5 = (bf16[2,1024]{1,0:T(2,128)(2,1)S(1)}, bf16[2,1024]{1,0:T(2,128)(2,1)}, u32[]{:S(2)}) copy-start(bf16[2,1024]{1,0:T(2,128)(2,1)} %d_ref.1) | copy-start | bytes 12292
  4.7 11.9 %collective-permute-start = (f32[8,160,128]{2,1,0:T(8,128)S(1)}, f32[8,160,128]{2,1,0:T(8,128)}, u32[]{:S(2)}, u32[]{:S(2)}) collective-permute-start(f32[8,160,128]{2,1,0:T(8,128)S(1)} %gram1.1), channel_id=1, source_target_pairs={{0,8},{8,0},{16,24},{24,16},{32,40},{40,32},{48,56},{56,48},{64,72... | collective-permute-start | bytes 1966088 | tf_op jit(solution)/shard_map/ppermute | solution.py:386
  13.5 1.8 %copy-start.6 = (s32[64]{0:T(128)S(1)}, s32[64]{0:T(128)}, u32[]{:S(2)}) copy-start(s32[64]{0:T(128)} %tallies_ref.1) | copy-start | bytes 772
  17.6 4.8 %copy-start.9 = (bf16[2,512]{1,0:T(2,128)(2,1)S(1)}, bf16[2,512]{1,0:T(2,128)(2,1)}, u32[]{:S(2)}) copy-start(bf16[2,512]{1,0:T(2,128)(2,1)} %param.10) | copy-start | bytes 6148
  17.6 4.8 %copy-start.10 = (bf16[2,512]{1,0:T(2,128)(2,1)S(1)}, bf16[2,512]{1,0:T(2,128)(2,1)}, u32[]{:S(2)}) copy-start(bf16[2,512]{1,0:T(2,128)(2,1)} %param.12) | copy-start | bytes 6148
  17.6 25.6 %all-to-all-start = ((f32[8,160,128]{2,1,0:T(8,128)}), f32[8,160,128]{2,1,0:T(8,128)S(1)}, u32[]{:S(2)}, u32[]{:S(2)}) async-start(f32[8,160,128]{2,1,0:T(8,128)} %broadcast_select_fusion), calls=%async_computation | async-start | bytes 1310720 | tf_op jit(solution)/shard_map/all_to_all | solution.py:405
  24.6 24.3 %collective-permute-start.1 = (bf16[514,512]{1,0:T(8,128)(2,1)}, bf16[514,512]{1,0:T(8,128)(2,1)}, u32[]{:S(2)}, u32[]{:S(2)}) collective-permute-start(bf16[514,512]{1,0:T(8,128)(2,1)} %pad_maximum_fusion), channel_id=1, source_target_pairs={{0,8},{8,0},{16,24},{24,16},{32,40},{40,32},{48,56},{56,48},{64,72... | collective-permute-start | bytes 1579016 | tf_op jit(solution)/shard_map/ppermute | solution.py:384
  44.1 24.2 %all-to-all-start.1 = ((f32[8,160,128]{2,1,0:T(8,128)}), f32[8,160,128]{2,1,0:T(8,128)S(1)}, u32[]{:S(2)}, u32[]{:S(2)}) async-start(f32[8,160,128]{2,1,0:T(8,128)} %broadcast_in_dim.14), calls=%async_computation.1 | async-start | bytes 1310720 | tf_op jit(solution)/shard_map/all_to_all | solution.py:376
  75.6 1.0 copy-start.2
  76.6 56.1 %copy-start.7 = (f32[512]{0:T(512)S(1)}, f32[512]{0:T(512)}, u32[]{:S(2)}) copy-start(f32[512]{0:T(512)} %param.13) | copy-start | bytes 6148
  76.6 56.1 %copy-start.8 = (f32[512]{0:T(512)S(1)}, f32[512]{0:T(512)}, u32[]{:S(2)}) copy-start(f32[512]{0:T(512)} %param.14) | copy-start | bytes 6148
  97.8 34.9 %copy-start.3 = (f32[512,512]{1,0:T(8,128)S(1)}, f32[512,512]{1,0:T(8,128)}, u32[]{:S(2)}) copy-start(f32[512,512]{1,0:T(8,128)} %copy-done.2) | copy-start | bytes 3145732
  125.7 7.0 %collective-permute-start.2 = (f32[32,8,4,128]{3,2,1,0:T(4,128)S(1)}, f32[32,8,4,128]{3,2,1,0:T(4,128)S(1)}, u32[]{:S(2)}, u32[]{:S(2)}) collective-permute-start(f32[32,8,4,128]{3,2,1,0:T(4,128)S(1)} %all_to_all.27.mine_ref), channel_id=1, source_target_pairs={{0,8},{8,0},{16,24},{24,16},{32,40},{40,32},{48,56},{56,48},{64,72... | collective-permute-start | bytes 1572872 | tf_op jit(solution)/shard_map/ppermute | solution.py:414
  144.2 3.1 %collective-permute-start.3 = (f32[1,512]{1,0:T(1,128)S(1)}, f32[1,512]{1,0:T(1,128)S(1)}, u32[]{:S(2)}, u32[]{:S(2)}) collective-permute-start(f32[1,512]{1,0:T(1,128)S(1)} %get-tuple-element.12.dual_ref), channel_id=1, source_target_pairs={{0,8},{8,0},{16,24},{24,16},{32,40},{40,32},{48,56},{56,48},{64,72... | collective-permute-start | bytes 6152 | tf_op jit(solution)/shard_map/ppermute | solution.py:417

commit v4 on v3

--- a/solution.py
+++ b/solution.py
@@ -13,6 +13,7 @@
 TOL2 = 1e-11
 MAX_STEPS = 4096
 VMEM = 20 * 2**20
+STAGGER_NS = 6000
 
 
 def blocks_of(rows):
@@ -38,21 +39,11 @@
     )
 
 
-def gram_kernel(slot, parts, w_hbm, d_hbm, out_ref, w_ref, d_ref, scaled_ref, g_ref, sem):
+def gram_kernel(slot, parts, w_ref, d_ref, out_ref, scaled_ref, g_ref):
     rows = w_ref.shape[0]
     tiles = [slice(i * B, (i + 1) * B) for i in range(rows // B)]
-    scale_copy = pltpu.make_async_copy(d_hbm, d_ref, sem.at[len(tiles)])
-    copies = [
-        pltpu.make_async_copy(w_hbm.at[slot, at, :], w_ref.at[at, :], sem.at[i])
-        for i, at in enumerate(tiles)
-    ]
-    scale_copy.start()
-    for copy in copies:
-        copy.start()
-    scale_copy.wait()
     scale = d_ref[...].astype(F32)[slot : slot + 1]
-    for at, copy in zip(tiles, copies):
-        copy.wait()
+    for at in tiles:
         scaled_ref[at, :] = (w_ref[at, :].astype(F32) * scale).astype(BF16)
     for at in tiles:
         g_ref[at, :] = lax.dot_general(
@@ -67,23 +58,61 @@
             out_ref[z, b * step : (b + 1) * step, :] = blk[z * step : (z + 1) * step, :]
 
 
-def gram(slot, parts, matrices, ratios):
-    _, rows, cols = matrices.shape
+def gram(slot, parts, matrix, ratios):
+    rows, cols = matrix.shape
     height = len(blocks_of(rows)) * B // parts
     return pl.pallas_call(
         functools.partial(gram_kernel, slot, parts),
-        in_specs=[pl.BlockSpec(memory_space=pl.ANY)] * 2,
         out_shape=jax.ShapeDtypeStruct((parts, height, B), F32),
-        scratch_shapes=[
-            pltpu.VMEM((rows, cols), BF16),
-            pltpu.VMEM(ratios.shape, BF16),
-            pltpu.VMEM((rows, cols), BF16),
-            pltpu.VMEM((rows, rows), F32),
-            pltpu.SemaphoreType.DMA((rows // B + 1,)),
-        ],
+        scratch_shapes=[pltpu.VMEM((rows, cols), BF16), pltpu.VMEM((rows, rows), F32)],
         compiler_params=pltpu.CompilerParams(vmem_limit_bytes=VMEM),
         name=f"gram{slot}",
-    )(matrices, ratios)
+    )(matrix, ratios)
+
+
+def choose_kernel(tallies_ref, own_ref, moved_ref, out_ref):
+    group = lax.axis_index("scen")
+    held = tallies_ref[group]
+
+    @pl.when(lax.rem(group, 2) == 1)
+    def _():
+        pl.delay(STAGGER_NS)
+
+    @pl.when(held >= 1)
+    def _():
+        out_ref[...] = own_ref[...]
+
+    @pl.when(held < 1)
+    def _():
+        out_ref[...] = moved_ref[...]
+
+
+def choose(tallies, own, moved):
+    return pl.pallas_call(
+        choose_kernel,
+        in_specs=[pl.BlockSpec(memory_space=pltpu.SMEM)]
+        + [pl.BlockSpec(memory_space=pltpu.VMEM)] * 2,
+        out_shape=jax.ShapeDtypeStruct(own.shape, F32),
+        compiler_params=pltpu.CompilerParams(vmem_limit_bytes=VMEM),
+        name="choose",
+    )(tallies, own, moved)
+
+
+def spread_kernel(recv_ref, out_ref):
+    total = recv_ref[0]
+    for z in range(1, recv_ref.shape[0]):
+        total = total + recv_ref[z]
+    for z in range(recv_ref.shape[0]):
+        out_ref[z] = total
+
+
+def spread(received):
+    return pl.pallas_call(
+        spread_kernel,
+        out_shape=jax.ShapeDtypeStruct(received.shape, F32),
+        compiler_params=pltpu.CompilerParams(vmem_limit_bytes=VMEM),
+        name="spread",
+    )(received)
 
 
 def ratio(a, b):
@@ -382,9 +411,10 @@
         for k in range(2)
     ]
     side_moved = lax.ppermute(sides[1], "scen", partner)
-    gram1 = gram(1, n_z, matrices, ratios)
+    gram1 = gram(1, n_z, matrices[1], ratios)
+    later, gram1 = lax.optimization_barrier((matrices, gram1))
     gram_moved = lax.ppermute(gram1, "scen", partner)
-    gram0 = gram(0, n_z, matrices, ratios)
+    gram0 = gram(0, n_z, later[0], ratios)
     side = jnp.where(own, sides[0], side_moved)
     link = side[:rows]
     reg_row = side[rows : rows + 1].astype(F32)
@@ -401,9 +431,9 @@
     )
     rhs = jnp.where(live, rhs, jnp.zeros_like(rhs))
 
-    partial = jnp.where(own, gram0, gram_moved)
-    shard = jnp.sum(lax.all_to_all(partial, "col", 0, 0), axis=0)
-    g, terms = solve(everyone(shard, "col", n_z), reg_row, rhs, link)
+    partial = choose(tallies, gram0, gram_moved)
+    shards = spread(lax.all_to_all(partial, "col", 0, 0))
+    g, terms = solve(lax.all_to_all(shards, "col", 0, 0), reg_row, rhs, link)
 
     count = n_s // 2
     same = [[2 * i + k for i in range(count)] for k in range(2)]

time: 150 us -> 145 us (0.967)
  waiting for transfers between devices: 35.8 us -> 27.4 us
  Pallas kernels: 23.8 us -> 31.6 us
  local copies, waits for them, and re-layouts: 7.08 us -> 5.43 us
    all_to_all x2, waiting for transfers between devices: 33.4 us -> 25 us  [the longest x1 13.4 us: local(): g, terms = solve(lax.all_to_all(shards, 'col', 0, 0), reg_row, rhs, link)]
    pallas_call x2 -> x4, Pallas kernels: 3.61 us -> 11.4 us  [the longest x1 7.46 us: choose(): pl.pallas_call(choose_kernel, in_specs=[pl.BlockSpec(memory_space=pltpu.S...]
    unnamed x22 -> x18, local copies, waits for them, and re-layouts: 3.29 us -> 1.01 us
    squeeze x0 -> x2, local copies, waits for them, and re-layouts: none -> 1.51 us  [the longest x1 1.44 us: local(): gram1 = gram(1, n_z, matrices[1], ratios)]
  transfers between devices with their start and end apart: 6 -> 6, of which waited for: 4 -> 5; matrix products, arithmetic and copies ran while one was open for 4% -> 3% of each run, Pallas kernels for 1% -> 2%
where the time goes in v4:
time: 145 us; the launch traced here: 144 us
  blocking collectives  48.7 us (34%)
  Pallas kernels  31.6 us (22%)
  waiting for transfers between devices  27.4 us (19%)
  starting transfers between devices  26.8 us (18%)
  local copies, waits for them, and re-layouts  5.43 us (4%)
  between operations  2.16 us (1%)
  other arithmetic  1.86 us (1%)
    all_to_all x2, blocking collectives, everyone(): lax.all_to_all(jnp.broadcast_to(x[None], (count,) + x.shape), axis, 0, 0,...  27.7 us
    all_to_all x1, blocking collectives, local(): lax.all_to_all(terms, 'scen', 0, 0, axis_index_groups=[same[0] + same[1]])  21 us
    all_to_all x1, waiting for transfers between devices, local(): g, terms = solve(lax.all_to_all(shards, 'col', 0, 0), reg_row, rhs, link)  13.4 us
    all_to_all x1, waiting for transfers between devices, local(): shards = spread(lax.all_to_all(partial, 'col', 0, 0))  11.6 us
    pallas_call x1, Pallas kernels, main_solve(): pl.pallas_call(main_kernel, out_shape=(jax.ShapeDtypeStruct((1, n0), F32)...  11.5 us
    ppermute x1, starting transfers between devices, local(): gram_moved = lax.ppermute(gram1, 'scen', partner)  8.75 us
    pallas_call x1, Pallas kernels, choose(): pl.pallas_call(choose_kernel, in_specs=[pl.BlockSpec(memory_space=pltpu.S...  7.46 us
    pallas_call x1, Pallas kernels, solve(): pl.pallas_call(solve_kernel, out_shape=(jax.ShapeDtypeStruct((rows, rows)...  7.24 us
  transfers between devices with their start and end apart: 6, of which 5 were waited for; matrix products, arithmetic and copies ran while one was open for 3% of the time, Pallas kernels for 2%

profile of v4, /device:TPU:1, one launch (start us, length us, event | category | flops | bytes accessed | tf_op | source)
XLA Modules:
  0.0 144.0 jit_solution(15769870330548437773)
XLA Ops:
  0.6 0.0 copy-start.3
  0.6 0.0 copy-start
  0.6 1.4 %slice_bitcast_fusion.1.w_ref = bf16[512,1024]{1,0:T(8,128)(2,1)S(1)} fusion(bf16[2,512,1024]{2,1,0:T(8,128)(2,1)} %w_ref.1), kind=kLoop, calls=%fused_computation.1 | loop fusion | bytes 2097152 | tf_op jit(solution)/shard_map/squeeze | solution.py:414
  2.1 0.0 copy-done.3
  2.1 1.5 %gram1.1 = f32[8,160,128]{2,1,0:T(8,128)S(1)} custom-call(bf16[512,1024]{1,0:T(8,128)(2,1)S(1)} %slice_bitcast_fusion.1.w_ref, bf16[2,1024]{1,0:T(2,128)(2,1)S(1)} %copy-done.3), custom_call_target="tpu_custom_call" | custom-call | tf_op jit(solution)/shard_map/gram1/pallas_call | solution.py:64
  3.6 8.7 %collective-permute-start = (f32[8,160,128]{2,1,0:T(8,128)S(1)}, f32[8,160,128]{2,1,0:T(8,128)S(1)}, u32[]{:S(2)}, u32[]{:S(2)}) collective-permute-start(f32[8,160,128]{2,1,0:T(8,128)S(1)} %gram1.1), channel_id=1, source_target_pairs={{0,8},{8,0},{16,24},{24,16},{32,40},{40,32},{48,56},{56,48},{64,72... | collective-permute-start | bytes 1966088 | tf_op jit(solution)/shard_map/ppermute | solution.py:416
  12.4 0.0 copy-done
  12.4 0.1 slice_bitcast_fusion.w_ref
  12.5 0.0 copy-start.4
  12.5 1.5 %gram0.1.own_ref = f32[8,160,128]{2,1,0:T(8,128)S(1)} custom-call(bf16[512,1024]{1,0:T(8,128)(2,1)S(1)} %slice_bitcast_fusion.w_ref, bf16[2,1024]{1,0:T(2,128)(2,1)S(1)} %copy-done.3), custom_call_target="tpu_custom_call" | custom-call | tf_op jit(solution)/shard_map/gram0/pallas_call | solution.py:64
  14.0 0.1 collective-permute-done.moved_ref
  14.1 0.0 copy-done.4
  14.1 7.5 %choose.1 = f32[8,160,128]{2,1,0:T(8,128)} custom-call(s32[64]{0:T(128)S(1)} %copy-done.4, f32[8,160,128]{2,1,0:T(8,128)S(1)} %gram0.1.own_ref, f32[8,160,128]{2,1,0:T(8,128)S(1)} %collective-permute-done.moved_ref), custom_call_target="tpu_custom_call" | custom-call | tf_op jit(solution)/shard_map/choose/pallas_call | solution.py:91
  21.5 0.0 copy-start.7
  21.5 0.0 copy-start.8
  21.5 4.8 %all-to-all-start = ((f32[8,160,128]{2,1,0:T(8,128)}), f32[8,160,128]{2,1,0:T(8,128)S(1)}, u32[]{:S(2)}, u32[]{:S(2)}) async-start(f32[8,160,128]{2,1,0:T(8,128)} %choose.1), calls=%async_computation | async-start | bytes 1310720 | tf_op jit(solution)/shard_map/all_to_all | solution.py:435
  26.4 0.0 copy-done.7
  26.4 0.0 copy-done.8
  26.4 1.3 slice_bitcast_fusion.3
  27.7 0.9 pad_maximum_fusion
  28.5 1.9 %collective-permute-start.1 = (bf16[514,512]{1,0:T(8,128)(2,1)}, bf16[514,512]{1,0:T(8,128)(2,1)}, u32[]{:S(2)}, u32[]{:S(2)}) collective-permute-start(bf16[514,512]{1,0:T(8,128)(2,1)} %pad_maximum_fusion), channel_id=1, source_target_pairs={{0,8},{8,0},{16,24},{24,16},{32,40},{40,32},{48,56},{56,48},{64,72... | collective-permute-start | bytes 1579016 | tf_op jit(solution)/shard_map/ppermute | solution.py:413
  30.4 11.6 %all-to-all-done.recv_ref = f32[8,160,128]{2,1,0:T(8,128)S(1)} async-done(((f32[8,160,128]{2,1,0:T(8,128)}), f32[8,160,128]{2,1,0:T(8,128)S(1)}, u32[]{:S(2)}, u32[]{:S(2)}) %all-to-all-start) | async-done | bytes 655392 | tf_op jit(solution)/shard_map/all_to_all | solution.py:435
  42.1 0.9 spread.1
  43.0 3.5 %all-to-all-start.1 = ((f32[8,160,128]{2,1,0:T(8,128)}), f32[8,160,128]{2,1,0:T(8,128)S(1)}, u32[]{:S(2)}, u32[]{:S(2)}) async-start(f32[8,160,128]{2,1,0:T(8,128)} %spread.1), calls=%async_computation.1 | async-start | bytes 1310720 | tf_op jit(solution)/shard_map/all_to_all | solution.py:436
  46.5 0.6 fusion.2
  48.4 0.6 pad.2.clone
  49.0 0.0 collective-permute-done.1
  49.0 0.1 maximum_select_fusion
  49.2 0.2 copy.11
  49.4 0.1 constant_dynamic-slice_fusion
  49.5 0.8 maximum_select_fusion.1.rhs_ref
  50.3 13.4 %all-to-all-done.1.recv_ref = f32[8,160,128]{2,1,0:T(8,128)S(1)} async-done(((f32[8,160,128]{2,1,0:T(8,128)}), f32[8,160,128]{2,1,0:T(8,128)S(1)}, u32[]{:S(2)}, u32[]{:S(2)}) %all-to-all-start.1) | async-done | bytes 655392 | tf_op jit(solution)/shard_map/all_to_all | solution.py:436
  63.7 7.2 %solve.1 = (f32[512,512]{1,0:T(8,128)S(1)}, f32[2,32,4,128]{3,2,1,0:T(4,128)S(1)}) custom-call(f32[8,160,128]{2,1,0:T(8,128)S(1)} %all-to-all-done.1.recv_ref, f32[1,512]{1,0:T(1,128)S(1)} %get-tuple-element.23.reg_ref, bf16[512,128]{1,0:T(8,128)(2,1)S(1)} %maximum_select_fusion.1.rhs_ref, bf16[512,512]{1,0:T(8,128)(2,1)S(1)} %slice.46.link_ref), custom_call_target="tpu_custom_call" | custom-call | tf_op jit(solution)/shard_map/solve/pallas_call | solution.py:224
  71.0 0.0 copy-start.1
  71.0 1.0 copy-done.1
  71.9 0.0 copy-start.5
  72.0 0.0 copy-start.6
  72.0 21.0 %all_to_all.25 = f32[64,4,128]{2,1,0:T(4,128)S(1)} all-to-all(f32[64,4,128]{2,1,0:T(4,128)S(1)} %bitcast.16), channel_id=1, replica_groups={{0,16,32,48,64,80,96,112,128,144,160,176,192,208,224,240,256,272,288,30..., dimensions={0} | all-to-all | bytes 262144 | tf_op jit(solution)/shard_map/all_to_all | solution.py:441
  92.9 0.1 reduce_sum.9
  93.0 0.0 copy-start.2
  93.0 9.1 %all_to_all.26 = f32[8,4,128]{2,1,0:T(4,128)S(1)} all-to-all(f32[8,4,128]{2,1,0:T(4,128)S(1)} %broadcast_in_dim.26), channel_id=1, replica_groups=mesh['scen'=64,'col'=8] {'col'}, dimensions={0} | all-to-all | bytes 32768 | tf_op jit(solution)/shard_map/all_to_all | solution.py:405
  102.1 0.1 broadcast_in_dim.27
  102.3 18.6 %all_to_all.27.mine_ref = f32[32,8,4,128]{3,2,1,0:T(4,128)S(1)} all-to-all(f32[32,8,4,128]{3,2,1,0:T(4,128)S(1)} %broadcast_in_dim.27), channel_id=1, replica_groups={{0,16,32,48,64,80,96,112,128,144,160,176,192,208,224,240,256,272,288,30..., dimensions={0} | all-to-all | bytes 1048576 | tf_op jit(solution)/shard_map/all_to_all | solution.py:405
  120.9 5.5 %collective-permute-start.2 = (f32[32,8,4,128]{3,2,1,0:T(4,128)S(1)}, f32[32,8,4,128]{3,2,1,0:T(4,128)S(1)}, u32[]{:S(2)}, u32[]{:S(2)}) collective-permute-start(f32[32,8,4,128]{3,2,1,0:T(4,128)S(1)} %all_to_all.27.mine_ref), channel_id=1, source_target_pairs={{0,8},{8,0},{16,24},{24,16},{32,40},{40,32},{48,56},{56,48},{64,72... | collective-permute-start | bytes 1572872 | tf_op jit(solution)/shard_map/ppermute | solution.py:444
  126.4 1.5 %collective-permute-done.2.other_ref = f32[32,8,4,128]{3,2,1,0:T(4,128)S(1)} collective-permute-done((f32[32,8,4,128]{3,2,1,0:T(4,128)S(1)}, f32[32,8,4,128]{3,2,1,0:T(4,128)S(1)}, u32[]{:S(2)}, u32[]{:S(2)}) %collective-permute-start.2) | collective-permute-done | bytes 524320 | tf_op jit(solution)/shard_map/ppermute | solution.py:444
  127.9 0.0 copy-done.5
  127.9 0.0 copy-done.6
  127.9 0.0 copy-done.2
  127.9 11.5 %main_solve.1 = (f32[1,512]{1,0:T(1,128)}, f32[1,512]{1,0:T(1,128)S(1)}) custom-call(f32[32,8,4,128]{3,2,1,0:T(4,128)S(1)} %all_to_all.27.mine_ref, f32[32,8,4,128]{3,2,1,0:T(4,128)S(1)} %collective-permute-done.2.other_ref, f32[1,512]{1,0:T(1,128)S(1)} %bitcast.17, f32[1,512]{1,0:T(1,128)S(1)} %bitcast.18, f32[512,512]{1,0:T(8,128)S(1)} %copy-done.2, ...), custom_call_target="tpu_custom_call" | custom-call | tf_op jit(solution)/shard_map/main_solve/pallas_call | solution.py:351
  139.4 2.3 %collective-permute-start.3 = (f32[1,512]{1,0:T(1,128)S(1)}, f32[1,512]{1,0:T(1,128)S(1)}, u32[]{:S(2)}, u32[]{:S(2)}) collective-permute-start(f32[1,512]{1,0:T(1,128)S(1)} %get-tuple-element.16.dual_ref), channel_id=1, source_target_pairs={{0,8},{8,0},{16,24},{24,16},{32,40},{40,32},{48,56},{56,48},{64,72... | collective-permute-start | bytes 6152 | tf_op jit(solution)/shard_map/ppermute | solution.py:447
  141.7 0.8 collective-permute-done.3.back_ref
  142.5 1.5 %primal.1 = (f32[2,512]{1,0:T(2,128)}, f32[2,1024]{1,0:T(2,128)}) custom-call(s32[64]{0:T(128)S(1)} %copy-done.4, bf16[2,512,1024]{2,1,0:T(8,128)(2,1)S(1)} %copy-done, bf16[2,1024]{1,0:T(2,128)(2,1)S(1)} %copy-done.3, f32[1,512]{1,0:T(1,128)S(1)} %get-tuple-element.16.dual_ref, f32[1,512]{1,0:T(1,128)S(1)} %collective-permute-done.3.back_ref), custom_call_target="tpu_custom_call" | custom-call | tf_op jit(solution)/shard_map/primal/pallas_call | solution.py:378
  (5 shorter events, 0.1 us)
Async XLA Ops:
  0.6 1.5 %copy-start.3 = (bf16[2,1024]{1,0:T(2,128)(2,1)S(1)}, bf16[2,1024]{1,0:T(2,128)(2,1)}, u32[]{:S(2)}) copy-start(bf16[2,1024]{1,0:T(2,128)(2,1)} %d_ref.5) | copy-start | bytes 12292
  0.6 11.7 %copy-start = (bf16[2,512,1024]{2,1,0:T(8,128)(2,1)S(1)}, bf16[2,512,1024]{2,1,0:T(8,128)(2,1)}, u32[]{:S(2)}) copy-start(bf16[2,512,1024]{2,1,0:T(8,128)(2,1)} %w_ref.1) | copy-start | bytes 6291460
  3.6 10.5 %collective-permute-start = (f32[8,160,128]{2,1,0:T(8,128)S(1)}, f32[8,160,128]{2,1,0:T(8,128)S(1)}, u32[]{:S(2)}, u32[]{:S(2)}) collective-permute-start(f32[8,160,128]{2,1,0:T(8,128)S(1)} %gram1.1), channel_id=1, source_target_pairs={{0,8},{8,0},{16,24},{24,16},{32,40},{40,32},{48,56},{56,48},{64,72... | collective-permute-start | bytes 1966088 | tf_op jit(solution)/shard_map/ppermute | solution.py:416
  12.5 1.6 %copy-start.4 = (s32[64]{0:T(128)S(1)}, s32[64]{0:T(128)}, u32[]{:S(2)}) copy-start(s32[64]{0:T(128)} %tallies_ref.3) | copy-start | bytes 772
  21.5 4.8 %copy-start.7 = (bf16[2,512]{1,0:T(2,128)(2,1)S(1)}, bf16[2,512]{1,0:T(2,128)(2,1)}, u32[]{:S(2)}) copy-start(bf16[2,512]{1,0:T(2,128)(2,1)} %param.10) | copy-start | bytes 6148
  21.5 4.8 %copy-start.8 = (bf16[2,512]{1,0:T(2,128)(2,1)S(1)}, bf16[2,512]{1,0:T(2,128)(2,1)}, u32[]{:S(2)}) copy-start(bf16[2,512]{1,0:T(2,128)(2,1)} %param.12) | copy-start | bytes 6148
  21.5 20.5 %all-to-all-start = ((f32[8,160,128]{2,1,0:T(8,128)}), f32[8,160,128]{2,1,0:T(8,128)S(1)}, u32[]{:S(2)}, u32[]{:S(2)}) async-start(f32[8,160,128]{2,1,0:T(8,128)} %choose.1), calls=%async_computation | async-start | bytes 1310720 | tf_op jit(solution)/shard_map/all_to_all | solution.py:435
  28.5 20.5 %collective-permute-start.1 = (bf16[514,512]{1,0:T(8,128)(2,1)}, bf16[514,512]{1,0:T(8,128)(2,1)}, u32[]{:S(2)}, u32[]{:S(2)}) collective-permute-start(bf16[514,512]{1,0:T(8,128)(2,1)} %pad_maximum_fusion), channel_id=1, source_target_pairs={{0,8},{8,0},{16,24},{24,16},{32,40},{40,32},{48,56},{56,48},{64,72... | collective-permute-start | bytes 1579016 | tf_op jit(solution)/shard_map/ppermute | solution.py:413
  43.0 20.7 %all-to-all-start.1 = ((f32[8,160,128]{2,1,0:T(8,128)}), f32[8,160,128]{2,1,0:T(8,128)S(1)}, u32[]{:S(2)}, u32[]{:S(2)}) async-start(f32[8,160,128]{2,1,0:T(8,128)} %spread.1), calls=%async_computation.1 | async-start | bytes 1310720 | tf_op jit(solution)/shard_map/all_to_all | solution.py:436
  71.0 1.0 copy-start.1
  71.9 56.0 %copy-start.5 = (f32[512]{0:T(512)S(1)}, f32[512]{0:T(512)}, u32[]{:S(2)}) copy-start(f32[512]{0:T(512)} %param.13) | copy-start | bytes 6148
  72.0 56.0 %copy-start.6 = (f32[512]{0:T(512)S(1)}, f32[512]{0:T(512)}, u32[]{:S(2)}) copy-start(f32[512]{0:T(512)} %param.14) | copy-start | bytes 6148
  93.0 34.9 %copy-start.2 = (f32[512,512]{1,0:T(8,128)S(1)}, f32[512,512]{1,0:T(8,128)}, u32[]{:S(2)}) copy-start(f32[512,512]{1,0:T(8,128)} %copy-done.1) | copy-start | bytes 3145732
  120.9 7.0 %collective-permute-start.2 = (f32[32,8,4,128]{3,2,1,0:T(4,128)S(1)}, f32[32,8,4,128]{3,2,1,0:T(4,128)S(1)}, u32[]{:S(2)}, u32[]{:S(2)}) collective-permute-start(f32[32,8,4,128]{3,2,1,0:T(4,128)S(1)} %all_to_all.27.mine_ref), channel_id=1, source_target_pairs={{0,8},{8,0},{16,24},{24,16},{32,40},{40,32},{48,56},{56,48},{64,72... | collective-permute-start | bytes 1572872 | tf_op jit(solution)/shard_map/ppermute | solution.py:444
  139.4 3.1 %collective-permute-start.3 = (f32[1,512]{1,0:T(1,128)S(1)}, f32[1,512]{1,0:T(1,128)S(1)}, u32[]{:S(2)}, u32[]{:S(2)}) collective-permute-start(f32[1,512]{1,0:T(1,128)S(1)} %get-tuple-element.16.dual_ref), channel_id=1, source_target_pairs={{0,8},{8,0},{16,24},{24,16},{32,40},{40,32},{48,56},{56,48},{64,72... | collective-permute-start | bytes 6152 | tf_op jit(solution)/shard_map/ppermute | solution.py:447

commit v5 on v3

--- a/solution.py
+++ b/solution.py
@@ -9,10 +9,14 @@
 
 F32 = jnp.float32
 BF16 = jnp.bfloat16
+F16 = jnp.float16
 B = 128
 TOL2 = 1e-11
 MAX_STEPS = 4096
 VMEM = 20 * 2**20
+WIDE_VMEM = 50 * 2**20
+SLABS = 16
+STAGGER_NS = 4000
 
 
 def blocks_of(rows):
@@ -38,21 +42,16 @@
     )
 
 
-def gram_kernel(slot, parts, w_hbm, d_hbm, out_ref, w_ref, d_ref, scaled_ref, g_ref, sem):
+def gram_kernel(slot, parts, w_ref, d_ref, out_ref, scaled_ref, g_ref):
+    if slot == 0:
+        @pl.when(lax.rem(lax.axis_index("scen"), 2) == 1)
+        def _():
+            pl.delay(STAGGER_NS)
+
     rows = w_ref.shape[0]
     tiles = [slice(i * B, (i + 1) * B) for i in range(rows // B)]
-    scale_copy = pltpu.make_async_copy(d_hbm, d_ref, sem.at[len(tiles)])
-    copies = [
-        pltpu.make_async_copy(w_hbm.at[slot, at, :], w_ref.at[at, :], sem.at[i])
-        for i, at in enumerate(tiles)
-    ]
-    scale_copy.start()
-    for copy in copies:
-        copy.start()
-    scale_copy.wait()
     scale = d_ref[...].astype(F32)[slot : slot + 1]
-    for at, copy in zip(tiles, copies):
-        copy.wait()
+    for at in tiles:
         scaled_ref[at, :] = (w_ref[at, :].astype(F32) * scale).astype(BF16)
     for at in tiles:
         g_ref[at, :] = lax.dot_general(
@@ -67,23 +66,16 @@
             out_ref[z, b * step : (b + 1) * step, :] = blk[z * step : (z + 1) * step, :]
 
 
-def gram(slot, parts, matrices, ratios):
-    _, rows, cols = matrices.shape
+def gram(slot, parts, matrix, ratios):
+    rows, cols = matrix.shape
     height = len(blocks_of(rows)) * B // parts
     return pl.pallas_call(
         functools.partial(gram_kernel, slot, parts),
-        in_specs=[pl.BlockSpec(memory_space=pl.ANY)] * 2,
         out_shape=jax.ShapeDtypeStruct((parts, height, B), F32),
-        scratch_shapes=[
-            pltpu.VMEM((rows, cols), BF16),
-            pltpu.VMEM(ratios.shape, BF16),
-            pltpu.VMEM((rows, cols), BF16),
-            pltpu.VMEM((rows, rows), F32),
-            pltpu.SemaphoreType.DMA((rows // B + 1,)),
-        ],
+        scratch_shapes=[pltpu.VMEM((rows, cols), BF16), pltpu.VMEM((rows, rows), F32)],
         compiler_params=pltpu.CompilerParams(vmem_limit_bytes=VMEM),
         name=f"gram{slot}",
-    )(matrices, ratios)
+    )(matrix, ratios)
 
 
 def ratio(a, b):
@@ -143,8 +135,8 @@
 
 
 def solve_kernel(
-    recv_ref, reg_ref, rhs_ref, link_ref, g_ref, out_ref,
-    hi_ref, mid_ref, x_ref, r_ref, p_ref, s_ref, rb_ref, sc_ref,
+    recv_ref, reg_ref, rhs_ref, link_ref, g_hbm, out_ref,
+    g_ref, hi_ref, mid_ref, x_ref, r_ref, p_ref, s_ref, rb_ref, sc_ref, sem,
 ):
     parts = recv_ref.shape[0]
     rows = g_ref.shape[0]
@@ -163,6 +155,8 @@
         if i != j:
             g_ref[rj, ri] = other
             hi_ref[rj, ri], mid_ref[rj, ri] = split3(other)[:2]
+    keep = pltpu.make_async_copy(g_ref, g_hbm.at[0], sem)
+    keep.start()
     r_ref[...] = rhs_ref[...].astype(F32)
     cg_block((hi_ref, mid_ref), x_ref, r_ref, p_ref, s_ref, rb_ref, sc_ref)
     n = x_ref.shape[1]
@@ -184,6 +178,7 @@
             at = t * B + c * quarter
             up = pltpu.roll(x_ref[at + half : at + half + quarter, :], half, 1)
             out_ref[c, :, t, :] = jnp.where(low, x_ref[at : at + quarter, :], up)
+    keep.wait()
 
 
 def n0_blocks(rows):
@@ -195,13 +190,20 @@
     return pl.pallas_call(
         solve_kernel,
         out_shape=(
-            jax.ShapeDtypeStruct((rows, rows), F32),
+            jax.ShapeDtypeStruct((SLABS, rows, rows), F32),
             jax.ShapeDtypeStruct((2, B // 4, rows // B, B), F32),
         ),
-        scratch_shapes=[pltpu.VMEM((rows, rows), BF16)] * 2
+        in_specs=[pl.BlockSpec(memory_space=pltpu.VMEM)] * 4,
+        out_specs=(
+            pl.BlockSpec(memory_space=pl.ANY),
+            pl.BlockSpec(memory_space=pltpu.VMEM),
+        ),
+        scratch_shapes=[pltpu.VMEM((rows, rows), F32)]
+        + [pltpu.VMEM((rows, rows), BF16)] * 2
         + [pltpu.VMEM((rows, width), F32)] * 4
-        + [pltpu.VMEM((rows, width), BF16), pltpu.VMEM((8, width), F32)],
-        compiler_params=pltpu.CompilerParams(vmem_limit_bytes=VMEM),
+        + [pltpu.VMEM((rows, width), BF16), pltpu.VMEM((8, width), F32)]
+        + [pltpu.SemaphoreType.DMA],
+        compiler_params=pltpu.CompilerParams(vmem_limit_bytes=WIDE_VMEM),
         name="solve",
     )(received, reg_row, rhs, link)
 
@@ -272,9 +274,11 @@
 
 
 def main_kernel(
-    mine_ref, other_ref, q_ref, c_ref, g_ref, link_ref, b_ref, first_ref, dual_ref,
-    m_ref, x_ref, r_ref, p_ref, s_ref, sc_ref,
+    mine_ref, other_ref, q_ref, c_ref, g_hbm, link_ref, b_ref, first_ref, dual_ref,
+    m_ref, g_ref, x_ref, r_ref, p_ref, s_ref, sc_ref, sem,
 ):
+    load = pltpu.make_async_copy(g_hbm.at[0], g_ref, sem)
+    load.start()
     quarter, shards, tiles, _ = mine_ref.shape
     half = 2 * quarter
     eye = eye_mask()
@@ -314,6 +318,7 @@
     first = cg_row(m_ref, rhs, *refs, eye)
     first_ref[...] = first
     pushed = b_ref[...] + times_row(link_ref, first, eye)
+    load.wait()
     dual_ref[...] = cg_row(g_ref, pushed, *refs, eye)
 
 
@@ -325,10 +330,13 @@
             jax.ShapeDtypeStruct((1, n0), F32),
             jax.ShapeDtypeStruct((1, rows), F32),
         ),
-        scratch_shapes=[pltpu.VMEM((n0, n0), F32)]
+        in_specs=[pl.BlockSpec(memory_space=pltpu.VMEM)] * 4
+        + [pl.BlockSpec(memory_space=pl.ANY)]
+        + [pl.BlockSpec(memory_space=pltpu.VMEM)] * 2,
+        scratch_shapes=[pltpu.VMEM((n0, n0), F32), pltpu.VMEM((rows, rows), F32)]
         + [pltpu.VMEM((1, n0), F32)] * 4
-        + [pltpu.VMEM((8, B), F32)],
-        compiler_params=pltpu.CompilerParams(vmem_limit_bytes=VMEM),
+        + [pltpu.VMEM((8, B), F32), pltpu.SemaphoreType.DMA],
+        compiler_params=pltpu.CompilerParams(vmem_limit_bytes=WIDE_VMEM),
         name="main_solve",
     )(mine, other, q_row, c_row, g, link, b_row)
 
@@ -382,9 +390,10 @@
         for k in range(2)
     ]
     side_moved = lax.ppermute(sides[1], "scen", partner)
-    gram1 = gram(1, n_z, matrices, ratios)
+    gram1 = gram(1, n_z, matrices[1], ratios)
+    later, gram1 = lax.optimization_barrier((matrices, gram1))
     gram_moved = lax.ppermute(gram1, "scen", partner)
-    gram0 = gram(0, n_z, matrices, ratios)
+    gram0 = gram(0, n_z, later[0], ratios)
     side = jnp.where(own, sides[0], side_moved)
     link = side[:rows]
     reg_row = side[rows : rows + 1].astype(F32)
@@ -401,9 +410,10 @@
     )
     rhs = jnp.where(live, rhs, jnp.zeros_like(rhs))
 
-    partial = jnp.where(own, gram0, gram_moved)
-    shard = jnp.sum(lax.all_to_all(partial, "col", 0, 0), axis=0)
-    g, terms = solve(everyone(shard, "col", n_z), reg_row, rhs, link)
+    partial = jnp.where(own, gram0, gram_moved).astype(F16)
+    received = lax.all_to_all(partial, "col", 0, 0).astype(F32)
+    whole = everyone(jnp.sum(received, axis=0).astype(F16), "col", n_z)
+    g, terms = solve(whole.astype(F32), reg_row, rhs, link)
 
     count = n_s // 2
     same = [[2 * i + k for i in range(count)] for k in range(2)]

time: 150 us -> 138 us (0.920)
  waiting for transfers between devices: 35.8 us -> 22.1 us
  Pallas kernels: 23.8 us -> 28.5 us
  blocking collectives: 48.9 us -> 47.4 us
    all_to_all x1, waiting for transfers between devices: 15.3 us -> 8 us  [local(): received = lax.all_to_all(partial, 'col', 0, 0).astype(F32)]
    all_to_all x1, waiting for transfers between devices: 18.1 us -> 11.8 us  [everyone(): lax.all_to_all(jnp.broadcast_to(x[None], (count,) + x.shape), axis, 0, 0,...]
    pallas_call x3, Pallas kernels: 10.9 us -> 14.8 us  [the longest x1 7.78 us: solve(): pl.pallas_call(solve_kernel, out_shape=(jax.ShapeDtypeStruct((SLABS, rows...]
    unnamed x22 -> x18, local copies, waits for them, and re-layouts: 3.29 us -> 0.04 us
    convert_element_type x0 -> x3, other arithmetic: none -> 1.83 us  [the longest x1 1.02 us: local(): g, terms = solve(whole.astype(F32), reg_row, rhs, link)]
    squeeze x0 -> x2, local copies, waits for them, and re-layouts: none -> 1.51 us  [the longest x1 1.44 us: local(): gram1 = gram(1, n_z, matrices[1], ratios)]
  transfers between devices with their start and end apart: 6 -> 6, of which waited for: 4 -> 4; matrix products, arithmetic and copies ran while one was open for 4% -> 5% of each run, Pallas kernels for 1% -> 4%
where the time goes in v5:
time: 138 us; the launch traced here: 137 us
  blocking collectives  47.4 us (34%)
  Pallas kernels  28.5 us (21%)
  starting transfers between devices  27.2 us (20%)
  waiting for transfers between devices  22.1 us (16%)
  local copies, waits for them, and re-layouts  5.7 us (4%)
  other arithmetic  4.06 us (3%)
  between operations  2.24 us (2%)
    all_to_all x2, blocking collectives, everyone(): lax.all_to_all(jnp.broadcast_to(x[None], (count,) + x.shape), axis, 0, 0,...  27.6 us
    all_to_all x1, blocking collectives, local(): lax.all_to_all(terms, 'scen', 0, 0, axis_index_groups=[same[0] + same[1]])  19.8 us
    pallas_call x1, Pallas kernels, main_solve(): pl.pallas_call(main_kernel, out_shape=(jax.ShapeDtypeStruct((1, n0), F32)...  12.1 us
    all_to_all x1, waiting for transfers between devices, everyone(): lax.all_to_all(jnp.broadcast_to(x[None], (count,) + x.shape), axis, 0, 0,...  11.8 us
    ppermute x1, starting transfers between devices, local(): gram_moved = lax.ppermute(gram1, 'scen', partner)  8.75 us
    all_to_all x1, waiting for transfers between devices, local(): received = lax.all_to_all(partial, 'col', 0, 0).astype(F32)  8 us
    pallas_call x1, Pallas kernels, solve(): pl.pallas_call(solve_kernel, out_shape=(jax.ShapeDtypeStruct((SLABS, rows...  7.78 us
    pallas_call x2, Pallas kernels, gram(): pl.pallas_call(functools.partial(gram_kernel, slot, parts), out_shape=jax...  7.02 us
  transfers between devices with their start and end apart: 6, of which 4 were waited for; matrix products, arithmetic and copies ran while one was open for 5% of the time, Pallas kernels for 4%

profile of v5, /device:TPU:1, one launch (start us, length us, event | category | flops | bytes accessed | tf_op | source)
XLA Modules:
  0.0 137.2 jit_solution(15923730255993833407)
XLA Ops:
  0.6 0.0 copy-start.1
  0.6 0.0 copy-start
  0.6 1.4 %slice_bitcast_fusion.1.w_ref = bf16[512,1024]{1,0:T(8,128)(2,1)S(1)} fusion(bf16[2,512,1024]{2,1,0:T(8,128)(2,1)} %w_ref.1), kind=kLoop, calls=%fused_computation.1 | loop fusion | bytes 2097152 | tf_op jit(solution)/shard_map/squeeze | solution.py:393
  2.1 0.0 copy-done.1
  2.1 1.5 %gram1.1 = f32[8,160,128]{2,1,0:T(8,128)S(1)} custom-call(bf16[512,1024]{1,0:T(8,128)(2,1)S(1)} %slice_bitcast_fusion.1.w_ref, bf16[2,1024]{1,0:T(2,128)(2,1)S(1)} %copy-done.1), custom_call_target="tpu_custom_call" | custom-call | tf_op jit(solution)/shard_map/gram1/pallas_call | solution.py:72
  3.6 8.7 %collective-permute-start = (f32[8,160,128]{2,1,0:T(8,128)S(1)}, f32[8,160,128]{2,1,0:T(8,128)}, u32[]{:S(2)}, u32[]{:S(2)}) collective-permute-start(f32[8,160,128]{2,1,0:T(8,128)S(1)} %gram1.1), channel_id=1, source_target_pairs={{0,8},{8,0},{16,24},{24,16},{32,40},{40,32},{48,56},{56,48},{64,72... | collective-permute-start | bytes 1966088 | tf_op jit(solution)/shard_map/ppermute | solution.py:395
  12.4 0.0 copy-done
  12.4 0.1 slice_bitcast_fusion.w_ref
  12.5 0.0 copy-start.2
  12.5 5.5 %gram0.1 = f32[8,160,128]{2,1,0:T(8,128)S(1)} custom-call(bf16[512,1024]{1,0:T(8,128)(2,1)S(1)} %slice_bitcast_fusion.w_ref, bf16[2,1024]{1,0:T(2,128)(2,1)S(1)} %copy-done.1), custom_call_target="tpu_custom_call" | custom-call | tf_op jit(solution)/shard_map/gram0/pallas_call | solution.py:72
  18.0 0.0 copy-done.2
  18.0 0.6 fusion.2
  19.3 2.2 %slice_bitcast_fusion.3 = (bf16[512,512]{1,0:T(8,128)(2,1)}, bf16[512,512]{1,0:T(8,128)(2,1)}) fusion(bf16[2,512,512]{2,1,0:T(8,128)(2,1)} %param.11), kind=kLoop, calls=%fused_computation.7 | loop fusion | bytes 2097152 | tf_op jit(solution)/shard_map/squeeze | solution.py:389
  21.5 0.0 collective-permute-done
  21.5 0.0 copy-start.7
  21.5 0.0 copy-start.8
  21.5 0.0 copy-start.6
  21.5 0.8 select_convert_fusion
  22.3 4.7 %all-to-all-start = ((f16[8,160,128]{2,1,0:T(8,128)(2,1)}), f16[8,160,128]{2,1,0:T(8,128)(2,1)}, u32[]{:S(2)}, u32[]{:S(2)}) async-start(f16[8,160,128]{2,1,0:T(8,128)(2,1)} %select_convert_fusion), calls=%async_computation | async-start | bytes 655360 | tf_op jit(solution)/shard_map/all_to_all | solution.py:414
  27.0 0.0 copy-done.7
  27.0 0.0 copy-done.8
  27.1 0.0 copy-done.6
  27.1 0.0 copy-start.5
  27.1 0.8 pad_maximum_fusion
  27.9 1.9 %collective-permute-start.1 = (bf16[514,512]{1,0:T(8,128)(2,1)}, bf16[514,512]{1,0:T(8,128)(2,1)}, u32[]{:S(2)}, u32[]{:S(2)}) collective-permute-start(bf16[514,512]{1,0:T(8,128)(2,1)} %pad_maximum_fusion), channel_id=1, source_target_pairs={{0,8},{8,0},{16,24},{24,16},{32,40},{40,32},{48,56},{56,48},{64,72... | collective-permute-start | bytes 1579016 | tf_op jit(solution)/shard_map/ppermute | solution.py:392
  30.5 0.1 pad.2.clone
  30.6 8.0 %all-to-all-done = f16[8,160,128]{2,1,0:T(8,128)(2,1)} async-done(((f16[8,160,128]{2,1,0:T(8,128)(2,1)}), f16[8,160,128]{2,1,0:T(8,128)(2,1)}, u32[]{:S(2)}, u32[]{:S(2)}) %all-to-all-start) | async-done | bytes 327712 | tf_op jit(solution)/shard_map/all_to_all | solution.py:414
  38.6 1.0 convert_reduce_fusion
  39.6 0.8 broadcast_in_dim.14
  40.4 4.1 %all-to-all-start.1 = ((f16[8,160,128]{2,1,0:T(8,128)(2,1)}), f16[8,160,128]{2,1,0:T(8,128)(2,1)}, u32[]{:S(2)}, u32[]{:S(2)}) async-start(f16[8,160,128]{2,1,0:T(8,128)(2,1)} %broadcast_in_dim.14), calls=%async_computation.1 | async-start | bytes 655360 | tf_op jit(solution)/shard_map/all_to_all | solution.py:384
  44.5 0.0 collective-permute-done.1
  44.5 0.0 copy-done.5
  44.5 0.2 maximum_select_fusion
  44.7 0.2 copy.11
  44.9 0.1 constant_dynamic-slice_fusion
  45.0 0.1 maximum_select_fusion.1.rhs_ref
  45.2 11.8 %all-to-all-done.1 = f16[8,160,128]{2,1,0:T(8,128)(2,1)} async-done(((f16[8,160,128]{2,1,0:T(8,128)(2,1)}), f16[8,160,128]{2,1,0:T(8,128)(2,1)}, u32[]{:S(2)}, u32[]{:S(2)}) %all-to-all-start.1) | async-done | bytes 327712 | tf_op jit(solution)/shard_map/all_to_all | solution.py:384
  56.9 1.0 convert_element_type.25.recv_ref
  58.0 7.8 %solve.1 = (f32[16,512,512]{2,1,0:T(8,128)}, f32[2,32,4,128]{3,2,1,0:T(4,128)S(1)}) custom-call(f32[8,160,128]{2,1,0:T(8,128)S(1)} %convert_element_type.25.recv_ref, f32[1,512]{1,0:T(1,128)S(1)} %get-tuple-element.23.reg_ref, bf16[512,128]{1,0:T(8,128)(2,1)S(1)} %maximum_select_fusion.1.rhs_ref, bf16[512,512]{1,0:T(8,128)(2,1)S(1)} %slice.46.link_ref), custom_call_target="tpu_custom_call" | custom-call | tf_op jit(solution)/shard_map/solve/pallas_call | solution.py:190
  65.7 0.0 copy-start.3
  65.7 0.0 copy-start.4
  65.8 19.8 %all_to_all.25 = f32[64,4,128]{2,1,0:T(4,128)S(1)} all-to-all(f32[64,4,128]{2,1,0:T(4,128)S(1)} %bitcast.16), channel_id=1, replica_groups={{0,16,32,48,64,80,96,112,128,144,160,176,192,208,224,240,256,272,288,30..., dimensions={0} | all-to-all | bytes 262144 | tf_op jit(solution)/shard_map/all_to_all | solution.py:421
  85.6 0.1 reduce_sum.19
  85.7 9.0 %all_to_all.26 = f32[8,4,128]{2,1,0:T(4,128)S(1)} all-to-all(f32[8,4,128]{2,1,0:T(4,128)S(1)} %broadcast_in_dim.33), channel_id=1, replica_groups=mesh['scen'=64,'col'=8] {'col'}, dimensions={0} | all-to-all | bytes 32768 | tf_op jit(solution)/shard_map/all_to_all | solution.py:384
  94.7 0.1 broadcast_in_dim.34
  94.8 18.6 %all_to_all.27.mine_ref = f32[32,8,4,128]{3,2,1,0:T(4,128)S(1)} all-to-all(f32[32,8,4,128]{3,2,1,0:T(4,128)S(1)} %broadcast_in_dim.34), channel_id=1, replica_groups={{0,16,32,48,64,80,96,112,128,144,160,176,192,208,224,240,256,272,288,30..., dimensions={0} | all-to-all | bytes 1048576 | tf_op jit(solution)/shard_map/all_to_all | solution.py:384
  113.4 5.5 %collective-permute-start.2 = (f32[32,8,4,128]{3,2,1,0:T(4,128)S(1)}, f32[32,8,4,128]{3,2,1,0:T(4,128)S(1)}, u32[]{:S(2)}, u32[]{:S(2)}) collective-permute-start(f32[32,8,4,128]{3,2,1,0:T(4,128)S(1)} %all_to_all.27.mine_ref), channel_id=1, source_target_pairs={{0,8},{8,0},{16,24},{24,16},{32,40},{40,32},{48,56},{56,48},{64,72... | collective-permute-start | bytes 1572872 | tf_op jit(solution)/shard_map/ppermute | solution.py:424
  118.9 1.5 %collective-permute-done.2.other_ref = f32[32,8,4,128]{3,2,1,0:T(4,128)S(1)} collective-permute-done((f32[32,8,4,128]{3,2,1,0:T(4,128)S(1)}, f32[32,8,4,128]{3,2,1,0:T(4,128)S(1)}, u32[]{:S(2)}, u32[]{:S(2)}) %collective-permute-start.2) | collective-permute-done | bytes 524320 | tf_op jit(solution)/shard_map/ppermute | solution.py:424
  120.4 0.0 copy-done.3
  120.4 0.0 copy-done.4
  120.4 12.1 %main_solve.1 = (f32[1,512]{1,0:T(1,128)}, f32[1,512]{1,0:T(1,128)S(1)}) custom-call(f32[32,8,4,128]{3,2,1,0:T(4,128)S(1)} %all_to_all.27.mine_ref, f32[32,8,4,128]{3,2,1,0:T(4,128)S(1)} %collective-permute-done.2.other_ref, f32[1,512]{1,0:T(1,128)S(1)} %bitcast.17, f32[1,512]{1,0:T(1,128)S(1)} %bitcast.18, f32[16,512,512]{2,1,0:T(8,128)} %get-tuple-element.14.g_hbm, ...), custom_call_target="tpu_custom_call" | custom-call | tf_op jit(solution)/shard_map/main_solve/pallas_call | solution.py:327
  132.6 2.3 %collective-permute-start.3 = (f32[1,512]{1,0:T(1,128)S(1)}, f32[1,512]{1,0:T(1,128)S(1)}, u32[]{:S(2)}, u32[]{:S(2)}) collective-permute-start(f32[1,512]{1,0:T(1,128)S(1)} %get-tuple-element.16.dual_ref), channel_id=1, source_target_pairs={{0,8},{8,0},{16,24},{24,16},{32,40},{40,32},{48,56},{56,48},{64,72... | collective-permute-start | bytes 6152 | tf_op jit(solution)/shard_map/ppermute | solution.py:427
  134.9 0.8 collective-permute-done.3.back_ref
  135.7 1.5 %primal.1 = (f32[2,512]{1,0:T(2,128)}, f32[2,1024]{1,0:T(2,128)}) custom-call(s32[64]{0:T(128)S(1)} %copy-done.2, bf16[2,512,1024]{2,1,0:T(8,128)(2,1)S(1)} %copy-done, bf16[2,1024]{1,0:T(2,128)(2,1)S(1)} %copy-done.1, f32[1,512]{1,0:T(1,128)S(1)} %get-tuple-element.16.dual_ref, f32[1,512]{1,0:T(1,128)S(1)} %collective-permute-done.3.back_ref), custom_call_target="tpu_custom_call" | custom-call | tf_op jit(solution)/shard_map/primal/pallas_call | solution.py:357
  (6 shorter events, 0.1 us)
Async XLA Ops:
  0.6 1.5 %copy-start.1 = (bf16[2,1024]{1,0:T(2,128)(2,1)S(1)}, bf16[2,1024]{1,0:T(2,128)(2,1)}, u32[]{:S(2)}) copy-start(bf16[2,1024]{1,0:T(2,128)(2,1)} %d_ref.5) | copy-start | bytes 12292
  0.6 11.7 %copy-start = (bf16[2,512,1024]{2,1,0:T(8,128)(2,1)S(1)}, bf16[2,512,1024]{2,1,0:T(8,128)(2,1)}, u32[]{:S(2)}) copy-start(bf16[2,512,1024]{2,1,0:T(8,128)(2,1)} %w_ref.1) | copy-start | bytes 6291460
  3.6 17.9 %collective-permute-start = (f32[8,160,128]{2,1,0:T(8,128)S(1)}, f32[8,160,128]{2,1,0:T(8,128)}, u32[]{:S(2)}, u32[]{:S(2)}) collective-permute-start(f32[8,160,128]{2,1,0:T(8,128)S(1)} %gram1.1), channel_id=1, source_target_pairs={{0,8},{8,0},{16,24},{24,16},{32,40},{40,32},{48,56},{56,48},{64,72... | collective-permute-start | bytes 1966088 | tf_op jit(solution)/shard_map/ppermute | solution.py:395
  12.5 5.5 %copy-start.2 = (s32[64]{0:T(128)S(1)}, s32[64]{0:T(128)}, u32[]{:S(2)}) copy-start(s32[64]{0:T(128)} %tallies_ref.1) | copy-start | bytes 772
  21.5 5.5 %copy-start.7 = (bf16[2,512]{1,0:T(2,128)(2,1)S(1)}, bf16[2,512]{1,0:T(2,128)(2,1)}, u32[]{:S(2)}) copy-start(bf16[2,512]{1,0:T(2,128)(2,1)} %param.10) | copy-start | bytes 6148
  21.5 5.5 %copy-start.8 = (bf16[2,512]{1,0:T(2,128)(2,1)S(1)}, bf16[2,512]{1,0:T(2,128)(2,1)}, u32[]{:S(2)}) copy-start(bf16[2,512]{1,0:T(2,128)(2,1)} %param.12) | copy-start | bytes 6148
  21.5 5.5 %copy-start.6 = (bf16[512,512]{1,0:T(8,128)(2,1)S(1)}, bf16[512,512]{1,0:T(8,128)(2,1)}, u32[]{:S(2)}) copy-start(bf16[512,512]{1,0:T(8,128)(2,1)} %get-tuple-element.20) | copy-start | bytes 1572868
  22.3 16.2 %all-to-all-start = ((f16[8,160,128]{2,1,0:T(8,128)(2,1)}), f16[8,160,128]{2,1,0:T(8,128)(2,1)}, u32[]{:S(2)}, u32[]{:S(2)}) async-start(f16[8,160,128]{2,1,0:T(8,128)(2,1)} %select_convert_fusion), calls=%async_computation | async-start | bytes 655360 | tf_op jit(solution)/shard_map/all_to_all | solution.py:414
  27.1 17.4 %copy-start.5 = (bf16[512,512]{1,0:T(8,128)(2,1)S(1)}, bf16[512,512]{1,0:T(8,128)(2,1)}, u32[]{:S(2)}) copy-start(bf16[512,512]{1,0:T(8,128)(2,1)} %get-tuple-element.19) | copy-start | bytes 1572868
  27.9 16.6 %collective-permute-start.1 = (bf16[514,512]{1,0:T(8,128)(2,1)}, bf16[514,512]{1,0:T(8,128)(2,1)}, u32[]{:S(2)}, u32[]{:S(2)}) collective-permute-start(bf16[514,512]{1,0:T(8,128)(2,1)} %pad_maximum_fusion), channel_id=1, source_target_pairs={{0,8},{8,0},{16,24},{24,16},{32,40},{40,32},{48,56},{56,48},{64,72... | collective-permute-start | bytes 1579016 | tf_op jit(solution)/shard_map/ppermute | solution.py:392
  40.4 16.5 %all-to-all-start.1 = ((f16[8,160,128]{2,1,0:T(8,128)(2,1)}), f16[8,160,128]{2,1,0:T(8,128)(2,1)}, u32[]{:S(2)}, u32[]{:S(2)}) async-start(f16[8,160,128]{2,1,0:T(8,128)(2,1)} %broadcast_in_dim.14), calls=%async_computation.1 | async-start | bytes 655360 | tf_op jit(solution)/shard_map/all_to_all | solution.py:384
  65.7 54.7 %copy-start.3 = (f32[512]{0:T(512)S(1)}, f32[512]{0:T(512)}, u32[]{:S(2)}) copy-start(f32[512]{0:T(512)} %param.13) | copy-start | bytes 6148
  65.7 54.7 %copy-start.4 = (f32[512]{0:T(512)S(1)}, f32[512]{0:T(512)}, u32[]{:S(2)}) copy-start(f32[512]{0:T(512)} %param.14) | copy-start | bytes 6148
  113.4 7.0 %collective-permute-start.2 = (f32[32,8,4,128]{3,2,1,0:T(4,128)S(1)}, f32[32,8,4,128]{3,2,1,0:T(4,128)S(1)}, u32[]{:S(2)}, u32[]{:S(2)}) collective-permute-start(f32[32,8,4,128]{3,2,1,0:T(4,128)S(1)} %all_to_all.27.mine_ref), channel_id=1, source_target_pairs={{0,8},{8,0},{16,24},{24,16},{32,40},{40,32},{48,56},{56,48},{64,72... | collective-permute-start | bytes 1572872 | tf_op jit(solution)/shard_map/ppermute | solution.py:424
  132.6 3.1 %collective-permute-start.3 = (f32[1,512]{1,0:T(1,128)S(1)}, f32[1,512]{1,0:T(1,128)S(1)}, u32[]{:S(2)}, u32[]{:S(2)}) collective-permute-start(f32[1,512]{1,0:T(1,128)S(1)} %get-tuple-element.16.dual_ref), channel_id=1, source_target_pairs={{0,8},{8,0},{16,24},{24,16},{32,40},{40,32},{48,56},{56,48},{64,72... | collective-permute-start | bytes 6152 | tf_op jit(solution)/shard_map/ppermute | solution.py:427

commit v6 on v5

--- a/solution.py
+++ b/solution.py
@@ -16,7 +16,8 @@
 VMEM = 20 * 2**20
 WIDE_VMEM = 50 * 2**20
 SLABS = 16
-STAGGER_NS = 4000
+RHO_SCALE = 0.25
+STAGGER_NS = 2500
 
 
 def blocks_of(rows):
@@ -171,7 +172,7 @@
     lane = lax.broadcasted_iota(jnp.int32, y.shape, 1)
     start = after * half
     here = (row >= start) & (row < start + half) & (lane == 0)
-    x_ref[...] = jnp.where(here, pltpu.roll(y, half, 1), y)
+    x_ref[...] = jnp.where(here, pltpu.roll(y, half, 1) * RHO_SCALE, y)
     low = low_lanes((quarter, B))
     for t in range(rows // B):
         for c in range(2):
@@ -313,7 +314,7 @@
             eye, q_ref[:, at], 0.0
         )
         m_ref[at, before] = jnp.where((row < half) & (lane == half), give, far)
-    rhs = c_ref[...] - jnp.concatenate(rho, axis=1)
+    rhs = c_ref[...] - jnp.concatenate(rho, axis=1) * (1.0 / RHO_SCALE)
     refs = (x_ref, r_ref, p_ref, s_ref, sc_ref)
     first = cg_row(m_ref, rhs, *refs, eye)
     first_ref[...] = first
@@ -385,15 +386,19 @@
             jnp.broadcast_to(x[None], (count,) + x.shape), axis, 0, 0, **kw
         )
 
+    gram1 = gram(1, n_z, matrices[1], ratios)
+    later, gram1 = lax.optimization_barrier((matrices, gram1))
+    gram_moved = lax.ppermute(gram1, "scen", partner)
+    gram0 = gram(0, n_z, later[0], ratios)
+    partial = jnp.where(own, gram0, gram_moved).astype(F16)
+    partial, coupler, damping, bounds = lax.optimization_barrier(
+        (partial, coupler, damping, bounds)
+    )
     sides = [
         jnp.concatenate([coupler[k], damping[k : k + 1], bounds[k : k + 1]], axis=0)
         for k in range(2)
     ]
     side_moved = lax.ppermute(sides[1], "scen", partner)
-    gram1 = gram(1, n_z, matrices[1], ratios)
-    later, gram1 = lax.optimization_barrier((matrices, gram1))
-    gram_moved = lax.ppermute(gram1, "scen", partner)
-    gram0 = gram(0, n_z, later[0], ratios)
     side = jnp.where(own, sides[0], side_moved)
     link = side[:rows]
     reg_row = side[rows : rows + 1].astype(F32)
@@ -410,7 +415,6 @@
     )
     rhs = jnp.where(live, rhs, jnp.zeros_like(rhs))
 
-    partial = jnp.where(own, gram0, gram_moved).astype(F16)
     received = lax.all_to_all(partial, "col", 0, 0).astype(F32)
     whole = everyone(jnp.sum(received, axis=0).astype(F16), "col", n_z)
     g, terms = solve(whole.astype(F32), reg_row, rhs, link)
@@ -420,9 +424,9 @@
     terms = terms.reshape((n_s,) + terms.shape[2:])
     mine = lax.all_to_all(terms, "scen", 0, 0, axis_index_groups=[same[0] + same[1]])
     wide = everyone(jnp.sum(mine, axis=0), "col", n_z)
-    half = everyone(wide, "scen", count, axis_index_groups=same)
+    half = everyone(wide.astype(F16), "scen", count, axis_index_groups=same)
     other = lax.ppermute(half, "scen", partner)
-    first, dual = main_solve(half, other, q_diag[None], c_vec[None], g, link, b_row)
+    first, dual = main_solve(half.astype(F32), other.astype(F32), q_diag[None], c_vec[None], g, link, b_row)
 
     returned = lax.ppermute(dual, "scen", partner)
     duals, primals = primal(tallies, matrices, ratios, dual, returned)

time: 138 us -> 132 us (0.957)
  blocking collectives: 47.4 us -> 42 us
  Pallas kernels: 28.5 us -> 26.1 us
    all_to_all x2, blocking collectives: 27.6 us -> 22.8 us  [everyone(): lax.all_to_all(jnp.broadcast_to(x[None], (count,) + x.shape), axis, 0, 0,...]
    pallas_call x2, Pallas kernels: 7.02 us -> 5.52 us  [gram(): pl.pallas_call(functools.partial(gram_kernel, slot, parts), out_shape=jax...]
  transfers between devices with their start and end apart: 6 -> 6, of which waited for: 4 -> 4; matrix products, arithmetic and copies ran while one was open for 5% -> 4% of each run, Pallas kernels for 4% -> 3%
where the time goes in v6:
time: 132 us; the launch traced here: 130 us
  blocking collectives  42 us (32%)
  starting transfers between devices  27.4 us (21%)
  Pallas kernels  26.1 us (20%)
  waiting for transfers between devices  23.2 us (18%)
  local copies, waits for them, and re-layouts  4.7 us (4%)
  other arithmetic  4.4 us (3%)
  between operations  2.26 us (2%)
    all_to_all x2, blocking collectives, everyone(): lax.all_to_all(jnp.broadcast_to(x[None], (count,) + x.shape), axis, 0, 0,...  22.8 us
    all_to_all x1, blocking collectives, local(): lax.all_to_all(terms, 'scen', 0, 0, axis_index_groups=[same[0] + same[1]])  19.1 us
    all_to_all x1, waiting for transfers between devices, everyone(): lax.all_to_all(jnp.broadcast_to(x[None], (count,) + x.shape), axis, 0, 0,...  13.1 us
    pallas_call x1, Pallas kernels, main_solve(): pl.pallas_call(main_kernel, out_shape=(jax.ShapeDtypeStruct((1, n0), F32)...  11.8 us
    ppermute x1, starting transfers between devices, local(): gram_moved = lax.ppermute(gram1, 'scen', partner)  8.75 us
    all_to_all x1, waiting for transfers between devices, local(): received = lax.all_to_all(partial, 'col', 0, 0).astype(F32)  8.3 us
    pallas_call x1, Pallas kernels, solve(): pl.pallas_call(solve_kernel, out_shape=(jax.ShapeDtypeStruct((SLABS, rows...  7.26 us
    ppermute x1, starting transfers between devices, local(): other = lax.ppermute(half, 'scen', partner)  5.65 us
  transfers between devices with their start and end apart: 6, of which 4 were waited for; matrix products, arithmetic and copies ran while one was open for 4% of the time, Pallas kernels for 3%

profile of v6, /device:TPU:1, one launch (start us, length us, event | category | flops | bytes accessed | tf_op | source)
XLA Modules:
  0.0 130.0 jit_solution(6907218955231939484)
XLA Ops:
  0.6 0.0 copy-start.1
  0.6 0.0 copy-start
  0.6 1.4 %slice_bitcast_fusion.1.w_ref = bf16[512,1024]{1,0:T(8,128)(2,1)S(1)} fusion(bf16[2,512,1024]{2,1,0:T(8,128)(2,1)} %w_ref.1), kind=kLoop, calls=%fused_computation.1 | loop fusion | bytes 2097152 | tf_op jit(solution)/shard_map/squeeze | solution.py:389
  2.1 0.0 copy-done.1
  2.1 1.5 %gram1.1 = f32[8,160,128]{2,1,0:T(8,128)S(1)} custom-call(bf16[512,1024]{1,0:T(8,128)(2,1)S(1)} %slice_bitcast_fusion.1.w_ref, bf16[2,1024]{1,0:T(2,128)(2,1)S(1)} %copy-done.1), custom_call_target="tpu_custom_call" | custom-call | tf_op jit(solution)/shard_map/gram1/pallas_call | solution.py:73
  3.6 8.7 %collective-permute-start = (f32[8,160,128]{2,1,0:T(8,128)S(1)}, f32[8,160,128]{2,1,0:T(8,128)}, u32[]{:S(2)}, u32[]{:S(2)}) collective-permute-start(f32[8,160,128]{2,1,0:T(8,128)S(1)} %gram1.1), channel_id=1, source_target_pairs={{0,8},{8,0},{16,24},{24,16},{32,40},{40,32},{48,56},{56,48},{64,72... | collective-permute-start | bytes 1966088 | tf_op jit(solution)/shard_map/ppermute | solution.py:391
  12.4 0.0 copy-done
  12.4 0.1 slice_bitcast_fusion.w_ref
  12.5 0.0 copy-start.2
  12.5 4.0 %gram0.1 = f32[8,160,128]{2,1,0:T(8,128)S(1)} custom-call(bf16[512,1024]{1,0:T(8,128)(2,1)S(1)} %slice_bitcast_fusion.w_ref, bf16[2,1024]{1,0:T(2,128)(2,1)S(1)} %copy-done.1), custom_call_target="tpu_custom_call" | custom-call | tf_op jit(solution)/shard_map/gram0/pallas_call | solution.py:73
  16.5 0.0 copy-done.2
  16.5 0.6 fusion.2
  17.8 0.0 collective-permute-done
  17.8 0.9 select_convert_fusion
  18.7 4.7 %all-to-all-start = ((f16[8,160,128]{2,1,0:T(8,128)(2,1)}), f16[8,160,128]{2,1,0:T(8,128)(2,1)}, u32[]{:S(2)}, u32[]{:S(2)}) async-start(f16[8,160,128]{2,1,0:T(8,128)(2,1)} %select_convert_fusion), calls=%async_computation | async-start | bytes 655360 | tf_op jit(solution)/shard_map/all_to_all | solution.py:418
  23.4 0.0 copy-start.5
  23.4 0.0 copy-start.6
  23.4 1.3 slice_bitcast_fusion.3
  24.7 0.0 copy-done.5
  24.7 0.0 copy-done.6
  24.7 0.8 pad_maximum_fusion
  25.5 1.9 %collective-permute-start.1 = (bf16[514,512]{1,0:T(8,128)(2,1)}, bf16[514,512]{1,0:T(8,128)(2,1)S(1)}, u32[]{:S(2)}, u32[]{:S(2)}) collective-permute-start(bf16[514,512]{1,0:T(8,128)(2,1)} %pad_maximum_fusion), channel_id=1, source_target_pairs={{0,8},{8,0},{16,24},{24,16},{32,40},{40,32},{48,56},{56,48},{64,72... | collective-permute-start | bytes 1579016 | tf_op jit(solution)/shard_map/ppermute | solution.py:401
  28.1 0.1 pad.2.clone
  28.2 8.3 %all-to-all-done = f16[8,160,128]{2,1,0:T(8,128)(2,1)} async-done(((f16[8,160,128]{2,1,0:T(8,128)(2,1)}), f16[8,160,128]{2,1,0:T(8,128)(2,1)}, u32[]{:S(2)}, u32[]{:S(2)}) %all-to-all-start) | async-done | bytes 327712 | tf_op jit(solution)/shard_map/all_to_all | solution.py:418
  36.5 1.0 convert_reduce_fusion
  37.5 0.8 broadcast_in_dim.14
  38.3 4.1 %all-to-all-start.1 = ((f16[8,160,128]{2,1,0:T(8,128)(2,1)}), f16[8,160,128]{2,1,0:T(8,128)(2,1)}, u32[]{:S(2)}, u32[]{:S(2)}) async-start(f16[8,160,128]{2,1,0:T(8,128)(2,1)} %broadcast_in_dim.14), calls=%async_computation.1 | async-start | bytes 655360 | tf_op jit(solution)/shard_map/all_to_all | solution.py:385
  42.4 0.0 collective-permute-done.1
  42.4 0.1 maximum_select_fusion
  42.6 0.2 copy.11
  42.8 0.1 constant_dynamic-slice_fusion
  42.9 0.1 maximum_select_fusion.1.rhs_ref
  43.1 13.1 %all-to-all-done.1 = f16[8,160,128]{2,1,0:T(8,128)(2,1)} async-done(((f16[8,160,128]{2,1,0:T(8,128)(2,1)}), f16[8,160,128]{2,1,0:T(8,128)(2,1)}, u32[]{:S(2)}, u32[]{:S(2)}) %all-to-all-start.1) | async-done | bytes 327712 | tf_op jit(solution)/shard_map/all_to_all | solution.py:385
  56.1 1.0 convert_element_type.34.recv_ref
  57.2 7.3 %solve.1 = (f32[16,512,512]{2,1,0:T(8,128)}, f32[2,32,4,128]{3,2,1,0:T(4,128)S(1)}) custom-call(f32[8,160,128]{2,1,0:T(8,128)S(1)} %convert_element_type.34.recv_ref, f32[1,512]{1,0:T(1,128)S(1)} %get-tuple-element.31.reg_ref, bf16[512,128]{1,0:T(8,128)(2,1)S(1)} %maximum_select_fusion.1.rhs_ref, bf16[512,512]{1,0:T(8,128)(2,1)S(1)} %slice.46.link_ref), custom_call_target="tpu_custom_call" | custom-call | tf_op jit(solution)/shard_map/solve/pallas_call | solution.py:191
  64.4 19.1 %all_to_all.25 = f32[64,4,128]{2,1,0:T(4,128)S(1)} all-to-all(f32[64,4,128]{2,1,0:T(4,128)S(1)} %bitcast.16), channel_id=1, replica_groups={{0,16,32,48,64,80,96,112,128,144,160,176,192,208,224,240,256,272,288,30..., dimensions={0} | all-to-all | bytes 262144 | tf_op jit(solution)/shard_map/all_to_all | solution.py:425
  83.6 0.1 reduce_sum.19
  83.7 9.0 %all_to_all.26 = f32[8,4,128]{2,1,0:T(4,128)S(1)} all-to-all(f32[8,4,128]{2,1,0:T(4,128)S(1)} %broadcast_in_dim.33), channel_id=1, replica_groups=mesh['scen'=64,'col'=8] {'col'}, dimensions={0} | all-to-all | bytes 32768 | tf_op jit(solution)/shard_map/all_to_all | solution.py:385
  92.6 0.1 broadcast_in_dim.34
  92.7 0.0 copy-start.3
  92.7 0.0 copy-start.4
  92.7 13.8 %all_to_all.27 = f16[32,8,4,128]{3,2,1,0:T(4,128)(2,1)S(1)} all-to-all(f16[32,8,4,128]{3,2,1,0:T(4,128)(2,1)S(1)} %broadcast_in_dim.34), channel_id=1, replica_groups={{0,16,32,48,64,80,96,112,128,144,160,176,192,208,224,240,256,272,288,30..., dimensions={0} | all-to-all | bytes 524288 | tf_op jit(solution)/shard_map/all_to_all | solution.py:385
  106.6 5.7 %collective-permute-start.2 = (f16[32,8,4,128]{3,2,1,0:T(4,128)(2,1)S(1)}, f16[32,8,4,128]{3,2,1,0:T(4,128)(2,1)S(1)}, u32[]{:S(2)}, u32[]{:S(2)}) collective-permute-start(f16[32,8,4,128]{3,2,1,0:T(4,128)(2,1)S(1)} %all_to_all.27), channel_id=1, source_target_pairs={{0,8},{8,0},{16,24},{24,16},{32,40},{40,32},{48,56},{56,48},{64,72... | collective-permute-start | bytes 786440 | tf_op jit(solution)/shard_map/ppermute | solution.py:428
  112.3 0.1 convert_element_type.37.mine_ref
  112.4 1.0 collective-permute-done.2
  113.4 0.1 convert_element_type.38.other_ref
  113.5 0.0 copy-done.3
  113.5 0.0 copy-done.4
  113.6 11.8 %main_solve.1 = (f32[1,512]{1,0:T(1,128)}, f32[1,512]{1,0:T(1,128)S(1)}) custom-call(f32[32,8,4,128]{3,2,1,0:T(4,128)S(1)} %convert_element_type.37.mine_ref, f32[32,8,4,128]{3,2,1,0:T(4,128)S(1)} %convert_element_type.38.other_ref, f32[1,512]{1,0:T(1,128)S(1)} %bitcast.17, f32[1,512]{1,0:T(1,128)S(1)} %bitcast.18, f32[16,512,512]{2,1,0:T(8,128)} %get-tuple-element.22.g_hbm, ...), custom_call_target="tpu_custom_call" | custom-call | tf_op jit(solution)/shard_map/main_solve/pallas_call | solution.py:328
  125.4 2.3 %collective-permute-start.3 = (f32[1,512]{1,0:T(1,128)S(1)}, f32[1,512]{1,0:T(1,128)S(1)}, u32[]{:S(2)}, u32[]{:S(2)}) collective-permute-start(f32[1,512]{1,0:T(1,128)S(1)} %get-tuple-element.24.dual_ref), channel_id=1, source_target_pairs={{0,8},{8,0},{16,24},{24,16},{32,40},{40,32},{48,56},{56,48},{64,72... | collective-permute-start | bytes 6152 | tf_op jit(solution)/shard_map/ppermute | solution.py:431
  127.7 0.8 collective-permute-done.3.back_ref
  128.5 1.5 %primal.1 = (f32[2,512]{1,0:T(2,128)}, f32[2,1024]{1,0:T(2,128)}) custom-call(s32[64]{0:T(128)S(1)} %copy-done.2, bf16[2,512,1024]{2,1,0:T(8,128)(2,1)S(1)} %copy-done, bf16[2,1024]{1,0:T(2,128)(2,1)S(1)} %copy-done.1, f32[1,512]{1,0:T(1,128)S(1)} %get-tuple-element.24.dual_ref, f32[1,512]{1,0:T(1,128)S(1)} %collective-permute-done.3.back_ref), custom_call_target="tpu_custom_call" | custom-call | tf_op jit(solution)/shard_map/primal/pallas_call | solution.py:358
  (7 shorter events, 0.1 us)
Async XLA Ops:
  0.6 1.5 %copy-start.1 = (bf16[2,1024]{1,0:T(2,128)(2,1)S(1)}, bf16[2,1024]{1,0:T(2,128)(2,1)}, u32[]{:S(2)}) copy-start(bf16[2,1024]{1,0:T(2,128)(2,1)} %d_ref.5) | copy-start | bytes 12292
  0.6 11.7 %copy-start = (bf16[2,512,1024]{2,1,0:T(8,128)(2,1)S(1)}, bf16[2,512,1024]{2,1,0:T(8,128)(2,1)}, u32[]{:S(2)}) copy-start(bf16[2,512,1024]{2,1,0:T(8,128)(2,1)} %w_ref.1) | copy-start | bytes 6291460
  3.6 14.2 %collective-permute-start = (f32[8,160,128]{2,1,0:T(8,128)S(1)}, f32[8,160,128]{2,1,0:T(8,128)}, u32[]{:S(2)}, u32[]{:S(2)}) collective-permute-start(f32[8,160,128]{2,1,0:T(8,128)S(1)} %gram1.1), channel_id=1, source_target_pairs={{0,8},{8,0},{16,24},{24,16},{32,40},{40,32},{48,56},{56,48},{64,72... | collective-permute-start | bytes 1966088 | tf_op jit(solution)/shard_map/ppermute | solution.py:391
  12.5 4.0 %copy-start.2 = (s32[64]{0:T(128)S(1)}, s32[64]{0:T(128)}, u32[]{:S(2)}) copy-start(s32[64]{0:T(128)} %tallies_ref.1) | copy-start | bytes 772
  18.7 17.8 %all-to-all-start = ((f16[8,160,128]{2,1,0:T(8,128)(2,1)}), f16[8,160,128]{2,1,0:T(8,128)(2,1)}, u32[]{:S(2)}, u32[]{:S(2)}) async-start(f16[8,160,128]{2,1,0:T(8,128)(2,1)} %select_convert_fusion), calls=%async_computation | async-start | bytes 655360 | tf_op jit(solution)/shard_map/all_to_all | solution.py:418
  23.4 1.3 %copy-start.5 = (bf16[2,512]{1,0:T(2,128)(2,1)S(1)}, bf16[2,512]{1,0:T(2,128)(2,1)}, u32[]{:S(2)}) copy-start(bf16[2,512]{1,0:T(2,128)(2,1)} %param.10) | copy-start | bytes 6148
  23.4 1.3 %copy-start.6 = (bf16[2,512]{1,0:T(2,128)(2,1)S(1)}, bf16[2,512]{1,0:T(2,128)(2,1)}, u32[]{:S(2)}) copy-start(bf16[2,512]{1,0:T(2,128)(2,1)} %param.12) | copy-start | bytes 6148
  25.5 16.9 %collective-permute-start.1 = (bf16[514,512]{1,0:T(8,128)(2,1)}, bf16[514,512]{1,0:T(8,128)(2,1)S(1)}, u32[]{:S(2)}, u32[]{:S(2)}) collective-permute-start(bf16[514,512]{1,0:T(8,128)(2,1)} %pad_maximum_fusion), channel_id=1, source_target_pairs={{0,8},{8,0},{16,24},{24,16},{32,40},{40,32},{48,56},{56,48},{64,72... | collective-permute-start | bytes 1579016 | tf_op jit(solution)/shard_map/ppermute | solution.py:401
  38.3 17.8 %all-to-all-start.1 = ((f16[8,160,128]{2,1,0:T(8,128)(2,1)}), f16[8,160,128]{2,1,0:T(8,128)(2,1)}, u32[]{:S(2)}, u32[]{:S(2)}) async-start(f16[8,160,128]{2,1,0:T(8,128)(2,1)} %broadcast_in_dim.14), calls=%async_computation.1 | async-start | bytes 655360 | tf_op jit(solution)/shard_map/all_to_all | solution.py:385
  92.7 20.8 %copy-start.3 = (f32[512]{0:T(512)S(1)}, f32[512]{0:T(512)}, u32[]{:S(2)}) copy-start(f32[512]{0:T(512)} %param.13) | copy-start | bytes 6148
  92.7 20.8 %copy-start.4 = (f32[512]{0:T(512)S(1)}, f32[512]{0:T(512)}, u32[]{:S(2)}) copy-start(f32[512]{0:T(512)} %param.14) | copy-start | bytes 6148
  106.6 6.8 %collective-permute-start.2 = (f16[32,8,4,128]{3,2,1,0:T(4,128)(2,1)S(1)}, f16[32,8,4,128]{3,2,1,0:T(4,128)(2,1)S(1)}, u32[]{:S(2)}, u32[]{:S(2)}) collective-permute-start(f16[32,8,4,128]{3,2,1,0:T(4,128)(2,1)S(1)} %all_to_all.27), channel_id=1, source_target_pairs={{0,8},{8,0},{16,24},{24,16},{32,40},{40,32},{48,56},{56,48},{64,72... | collective-permute-start | bytes 786440 | tf_op jit(solution)/shard_map/ppermute | solution.py:428
  125.4 3.1 %collective-permute-start.3 = (f32[1,512]{1,0:T(1,128)S(1)}, f32[1,512]{1,0:T(1,128)S(1)}, u32[]{:S(2)}, u32[]{:S(2)}) collective-permute-start(f32[1,512]{1,0:T(1,128)S(1)} %get-tuple-element.24.dual_ref), channel_id=1, source_target_pairs={{0,8},{8,0},{16,24},{24,16},{32,40},{40,32},{48,56},{56,48},{64,72... | collective-permute-start | bytes 6152 | tf_op jit(solution)/shard_map/ppermute | solution.py:431

commit v7 on v6

--- a/solution.py
+++ b/solution.py
@@ -11,13 +11,13 @@
 BF16 = jnp.bfloat16
 F16 = jnp.float16
 B = 128
-TOL2 = 1e-11
+TOL2 = 1e-10
 MAX_STEPS = 4096
 VMEM = 20 * 2**20
 WIDE_VMEM = 50 * 2**20
 SLABS = 16
 RHO_SCALE = 0.25
-STAGGER_NS = 2500
+STAGGER_NS = 1500
 
 
 def blocks_of(rows):
@@ -77,6 +77,29 @@
         compiler_params=pltpu.CompilerParams(vmem_limit_bytes=VMEM),
         name=f"gram{slot}",
     )(matrix, ratios)
+
+
+def choose_kernel(tallies_ref, own_ref, moved_ref, out_ref):
+    held = tallies_ref[lax.axis_index("scen")]
+
+    @pl.when(held >= 1)
+    def _():
+        out_ref[...] = own_ref[...]
+
+    @pl.when(held < 1)
+    def _():
+        out_ref[...] = moved_ref[...]
+
+
+def choose(tallies, own, moved):
+    return pl.pallas_call(
+        choose_kernel,
+        in_specs=[pl.BlockSpec(memory_space=pltpu.SMEM)]
+        + [pl.BlockSpec(memory_space=pltpu.VMEM)] * 2,
+        out_shape=jax.ShapeDtypeStruct(own.shape, F32),
+        compiler_params=pltpu.CompilerParams(vmem_limit_bytes=VMEM),
+        name="choose",
+    )(tallies, own, moved)
 
 
 def ratio(a, b):
@@ -390,7 +413,7 @@
     later, gram1 = lax.optimization_barrier((matrices, gram1))
     gram_moved = lax.ppermute(gram1, "scen", partner)
     gram0 = gram(0, n_z, later[0], ratios)
-    partial = jnp.where(own, gram0, gram_moved).astype(F16)
+    partial = choose(tallies, gram0, gram_moved).astype(F16)
     partial, coupler, damping, bounds = lax.optimization_barrier(
         (partial, coupler, damping, bounds)
     )

time: 132 us -> 127 us (0.962); the launches traced: 130 us -> 126 us
  blocking collectives: 42 us -> 49.4 us
  Pallas kernels: 26.1 us -> 18.9 us
  other arithmetic: 4.4 us -> 2.34 us
    all_to_all x1, blocking collectives: 19.1 us -> 26.6 us  [local(): lax.all_to_all(terms, 'scen', 0, 0, axis_index_groups=[same[0] + same[1]])]
    pallas_call x1, Pallas kernels: 7.26 us -> 1.4 us  [solve(): pl.pallas_call(solve_kernel, out_shape=(jax.ShapeDtypeStruct((SLABS, rows...]
  transfers between devices with their start and end apart: 6 -> 6, of which waited for: 4 -> 4; matrix products, arithmetic and copies ran while one was open for 4% -> 4% of each run, Pallas kernels for 3% -> 2%
where the time goes in v7:
time: 127 us; the launch traced here: 126 us
  blocking collectives  49.4 us (39%)
  starting transfers between devices  26.7 us (21%)
  waiting for transfers between devices  22.2 us (17%)
  Pallas kernels  18.9 us (15%)
  local copies, waits for them, and re-layouts  4.69 us (4%)
  other arithmetic  2.34 us (2%)
  between operations  2.25 us (2%)
    all_to_all x1, blocking collectives, local(): lax.all_to_all(terms, 'scen', 0, 0, axis_index_groups=[same[0] + same[1]])  26.6 us
    all_to_all x2, blocking collectives, everyone(): lax.all_to_all(jnp.broadcast_to(x[None], (count,) + x.shape), axis, 0, 0,...  22.8 us
    all_to_all x1, waiting for transfers between devices, everyone(): lax.all_to_all(jnp.broadcast_to(x[None], (count,) + x.shape), axis, 0, 0,...  13 us
    pallas_call x1, Pallas kernels, main_solve(): pl.pallas_call(main_kernel, out_shape=(jax.ShapeDtypeStruct((1, n0), F32)...  10.8 us
    ppermute x1, starting transfers between devices, local(): gram_moved = lax.ppermute(gram1, 'scen', partner)  8.75 us
    all_to_all x1, waiting for transfers between devices, local(): received = lax.all_to_all(partial, 'col', 0, 0).astype(F32)  7.4 us
    ppermute x1, starting transfers between devices, local(): other = lax.ppermute(half, 'scen', partner)  5.65 us
    all_to_all x1, starting transfers between devices, local(): received = lax.all_to_all(partial, 'col', 0, 0).astype(F32)  4.69 us
  transfers between devices with their start and end apart: 6, of which 4 were waited for; matrix products, arithmetic and copies ran while one was open for 4% of the time, Pallas kernels for 2%

profile of v7, /device:TPU:1, one launch (start us, length us, event | category | flops | bytes accessed | tf_op | source)
XLA Modules:
  0.0 126.5 jit_solution(7078952190484166480)
XLA Ops:
  0.6 0.0 copy-start.1
  0.6 0.0 copy-start
  0.6 1.4 %slice_bitcast_fusion.1.w_ref = bf16[512,1024]{1,0:T(8,128)(2,1)S(1)} fusion(bf16[2,512,1024]{2,1,0:T(8,128)(2,1)} %w_ref.1), kind=kLoop, calls=%fused_computation.1 | loop fusion | bytes 2097152 | tf_op jit(solution)/shard_map/squeeze | solution.py:412
  2.1 0.0 copy-done.1
  2.1 1.5 %gram1.1 = f32[8,160,128]{2,1,0:T(8,128)S(1)} custom-call(bf16[512,1024]{1,0:T(8,128)(2,1)S(1)} %slice_bitcast_fusion.1.w_ref, bf16[2,1024]{1,0:T(2,128)(2,1)S(1)} %copy-done.1), custom_call_target="tpu_custom_call" | custom-call | tf_op jit(solution)/shard_map/gram1/pallas_call | solution.py:73
  3.6 8.7 %collective-permute-start = (f32[8,160,128]{2,1,0:T(8,128)S(1)}, f32[8,160,128]{2,1,0:T(8,128)S(1)}, u32[]{:S(2)}, u32[]{:S(2)}) collective-permute-start(f32[8,160,128]{2,1,0:T(8,128)S(1)} %gram1.1), channel_id=1, source_target_pairs={{0,8},{8,0},{16,24},{24,16},{32,40},{40,32},{48,56},{56,48},{64,72... | collective-permute-start | bytes 1966088 | tf_op jit(solution)/shard_map/ppermute | solution.py:414
  12.4 0.0 copy-done
  12.4 0.1 slice_bitcast_fusion.w_ref
  12.5 0.0 copy-start.2
  12.5 3.0 %gram0.1.own_ref = f32[8,160,128]{2,1,0:T(8,128)S(1)} custom-call(bf16[512,1024]{1,0:T(8,128)(2,1)S(1)} %slice_bitcast_fusion.w_ref, bf16[2,1024]{1,0:T(2,128)(2,1)S(1)} %copy-done.1), custom_call_target="tpu_custom_call" | custom-call | tf_op jit(solution)/shard_map/gram0/pallas_call | solution.py:73
  15.5 0.0 collective-permute-done.moved_ref
  15.5 0.0 copy-done.2
  15.5 0.6 choose.1
  16.1 0.8 convert_element_type.31
  16.9 4.7 %all-to-all-start = ((f16[8,160,128]{2,1,0:T(8,128)(2,1)}), f16[8,160,128]{2,1,0:T(8,128)(2,1)S(1)}, u32[]{:S(2)}, u32[]{:S(2)}) async-start(f16[8,160,128]{2,1,0:T(8,128)(2,1)} %convert_element_type.31), calls=%async_computation | async-start | bytes 655360 | tf_op jit(solution)/shard_map/all_to_all | solution.py:441
  21.6 0.0 copy-start.5
  21.6 0.0 copy-start.6
  21.6 1.3 %slice_bitcast_fusion.3 = (bf16[512,512]{1,0:T(8,128)(2,1)S(1)}, bf16[512,512]{1,0:T(8,128)(2,1)S(1)}) fusion(bf16[2,512,512]{2,1,0:T(8,128)(2,1)} %param.11), kind=kLoop, calls=%fused_computation.6 | loop fusion | bytes 2097152 | tf_op jit(solution)/shard_map/squeeze | solution.py:421
  22.9 0.0 copy-done.5
  22.9 0.0 copy-done.6
  22.9 0.8 pad_maximum_fusion
  23.8 1.9 %collective-permute-start.1 = (bf16[514,512]{1,0:T(8,128)(2,1)}, bf16[514,512]{1,0:T(8,128)(2,1)S(1)}, u32[]{:S(2)}, u32[]{:S(2)}) collective-permute-start(bf16[514,512]{1,0:T(8,128)(2,1)} %pad_maximum_fusion), channel_id=1, source_target_pairs={{0,8},{8,0},{16,24},{24,16},{32,40},{40,32},{48,56},{56,48},{64,72... | collective-permute-start | bytes 1579016 | tf_op jit(solution)/shard_map/ppermute | solution.py:424
  25.7 0.6 fusion.2
  27.6 0.1 pad.2.clone
  27.7 7.4 %all-to-all-done = f16[8,160,128]{2,1,0:T(8,128)(2,1)S(1)} async-done(((f16[8,160,128]{2,1,0:T(8,128)(2,1)}), f16[8,160,128]{2,1,0:T(8,128)(2,1)S(1)}, u32[]{:S(2)}, u32[]{:S(2)}) %all-to-all-start) | async-done | bytes 327712 | tf_op jit(solution)/shard_map/all_to_all | solution.py:441
  35.1 0.8 broadcast_in_dim.14
  35.9 3.4 %all-to-all-start.1 = ((f16[8,160,128]{2,1,0:T(8,128)(2,1)}), f16[8,160,128]{2,1,0:T(8,128)(2,1)S(1)}, u32[]{:S(2)}, u32[]{:S(2)}) async-start(f16[8,160,128]{2,1,0:T(8,128)(2,1)} %broadcast_in_dim.14), calls=%async_computation.1 | async-start | bytes 655360 | tf_op jit(solution)/shard_map/all_to_all | solution.py:408
  39.4 0.0 collective-permute-done.1
  39.4 0.1 maximum_select_fusion
  39.6 0.2 copy.11
  39.8 0.1 constant_dynamic-slice_fusion
  39.9 0.1 maximum_select_fusion.1.rhs_ref
  40.0 13.0 %all-to-all-done.1 = f16[8,160,128]{2,1,0:T(8,128)(2,1)S(1)} async-done(((f16[8,160,128]{2,1,0:T(8,128)(2,1)}), f16[8,160,128]{2,1,0:T(8,128)(2,1)S(1)}, u32[]{:S(2)}, u32[]{:S(2)}) %all-to-all-start.1) | async-done | bytes 327712 | tf_op jit(solution)/shard_map/all_to_all | solution.py:408
  53.1 1.4 %solve.1 = (f32[16,512,512]{2,1,0:T(8,128)}, f32[2,32,4,128]{3,2,1,0:T(4,128)S(1)}) custom-call(f32[8,160,128]{2,1,0:T(8,128)S(1)} %convert_element_type.34.recv_ref, f32[1,512]{1,0:T(1,128)S(1)} %get-tuple-element.31.reg_ref, bf16[512,128]{1,0:T(8,128)(2,1)S(1)} %maximum_select_fusion.1.rhs_ref, bf16[512,512]{1,0:T(8,128)(2,1)S(1)} %slice.46.link_ref), custom_call_target="tpu_custom_call" | custom-call | tf_op jit(solution)/shard_map/solve/pallas_call | solution.py:214
  54.5 26.6 %all_to_all.25 = f32[64,4,128]{2,1,0:T(4,128)S(1)} all-to-all(f32[64,4,128]{2,1,0:T(4,128)S(1)} %bitcast.16), channel_id=1, replica_groups={{0,16,32,48,64,80,96,112,128,144,160,176,192,208,224,240,256,272,288,30..., dimensions={0} | all-to-all | bytes 262144 | tf_op jit(solution)/shard_map/all_to_all | solution.py:448
  81.1 0.1 reduce_sum.19
  81.1 9.0 %all_to_all.26 = f32[8,4,128]{2,1,0:T(4,128)S(1)} all-to-all(f32[8,4,128]{2,1,0:T(4,128)S(1)} %broadcast_in_dim.33), channel_id=1, replica_groups=mesh['scen'=64,'col'=8] {'col'}, dimensions={0} | all-to-all | bytes 32768 | tf_op jit(solution)/shard_map/all_to_all | solution.py:408
  90.1 0.1 broadcast_in_dim.34
  90.2 0.0 copy-start.3
  90.2 0.0 copy-start.4
  90.2 13.8 %all_to_all.27 = f16[32,8,4,128]{3,2,1,0:T(4,128)(2,1)S(1)} all-to-all(f16[32,8,4,128]{3,2,1,0:T(4,128)(2,1)S(1)} %broadcast_in_dim.34), channel_id=1, replica_groups={{0,16,32,48,64,80,96,112,128,144,160,176,192,208,224,240,256,272,288,30..., dimensions={0} | all-to-all | bytes 524288 | tf_op jit(solution)/shard_map/all_to_all | solution.py:408
  104.1 5.7 %collective-permute-start.2 = (f16[32,8,4,128]{3,2,1,0:T(4,128)(2,1)S(1)}, f16[32,8,4,128]{3,2,1,0:T(4,128)(2,1)S(1)}, u32[]{:S(2)}, u32[]{:S(2)}) collective-permute-start(f16[32,8,4,128]{3,2,1,0:T(4,128)(2,1)S(1)} %all_to_all.27), channel_id=1, source_target_pairs={{0,8},{8,0},{16,24},{24,16},{32,40},{40,32},{48,56},{56,48},{64,72... | collective-permute-start | bytes 786440 | tf_op jit(solution)/shard_map/ppermute | solution.py:451
  109.7 0.1 convert_element_type.37.mine_ref
  109.9 1.0 collective-permute-done.2
  110.9 0.1 convert_element_type.38.other_ref
  111.0 0.0 copy-done.3
  111.0 0.0 copy-done.4
  111.0 10.8 %main_solve.1 = (f32[1,512]{1,0:T(1,128)}, f32[1,512]{1,0:T(1,128)S(1)}) custom-call(f32[32,8,4,128]{3,2,1,0:T(4,128)S(1)} %convert_element_type.37.mine_ref, f32[32,8,4,128]{3,2,1,0:T(4,128)S(1)} %convert_element_type.38.other_ref, f32[1,512]{1,0:T(1,128)S(1)} %bitcast.17, f32[1,512]{1,0:T(1,128)S(1)} %bitcast.18, f32[16,512,512]{2,1,0:T(8,128)} %get-tuple-element.22.g_hbm, ...), custom_call_target="tpu_custom_call" | custom-call | tf_op jit(solution)/shard_map/main_solve/pallas_call | solution.py:351
  121.9 2.3 %collective-permute-start.3 = (f32[1,512]{1,0:T(1,128)S(1)}, f32[1,512]{1,0:T(1,128)S(1)}, u32[]{:S(2)}, u32[]{:S(2)}) collective-permute-start(f32[1,512]{1,0:T(1,128)S(1)} %get-tuple-element.24.dual_ref), channel_id=1, source_target_pairs={{0,8},{8,0},{16,24},{24,16},{32,40},{40,32},{48,56},{56,48},{64,72... | collective-permute-start | bytes 6152 | tf_op jit(solution)/shard_map/ppermute | solution.py:454
  124.1 0.8 collective-permute-done.3.back_ref
  124.9 1.5 %primal.1 = (f32[2,512]{1,0:T(2,128)}, f32[2,1024]{1,0:T(2,128)}) custom-call(s32[64]{0:T(128)S(1)} %copy-done.2, bf16[2,512,1024]{2,1,0:T(8,128)(2,1)S(1)} %copy-done, bf16[2,1024]{1,0:T(2,128)(2,1)S(1)} %copy-done.1, f32[1,512]{1,0:T(1,128)S(1)} %get-tuple-element.24.dual_ref, f32[1,512]{1,0:T(1,128)S(1)} %collective-permute-done.3.back_ref), custom_call_target="tpu_custom_call" | custom-call | tf_op jit(solution)/shard_map/primal/pallas_call | solution.py:381
  (9 shorter events, 0.2 us)
Async XLA Ops:
  0.6 1.5 %copy-start.1 = (bf16[2,1024]{1,0:T(2,128)(2,1)S(1)}, bf16[2,1024]{1,0:T(2,128)(2,1)}, u32[]{:S(2)}) copy-start(bf16[2,1024]{1,0:T(2,128)(2,1)} %d_ref.5) | copy-start | bytes 12292
  0.6 11.7 %copy-start = (bf16[2,512,1024]{2,1,0:T(8,128)(2,1)S(1)}, bf16[2,512,1024]{2,1,0:T(8,128)(2,1)}, u32[]{:S(2)}) copy-start(bf16[2,512,1024]{2,1,0:T(8,128)(2,1)} %w_ref.1) | copy-start | bytes 6291460
  3.6 11.9 %collective-permute-start = (f32[8,160,128]{2,1,0:T(8,128)S(1)}, f32[8,160,128]{2,1,0:T(8,128)S(1)}, u32[]{:S(2)}, u32[]{:S(2)}) collective-permute-start(f32[8,160,128]{2,1,0:T(8,128)S(1)} %gram1.1), channel_id=1, source_target_pairs={{0,8},{8,0},{16,24},{24,16},{32,40},{40,32},{48,56},{56,48},{64,72... | collective-permute-start | bytes 1966088 | tf_op jit(solution)/shard_map/ppermute | solution.py:414
  12.5 3.1 %copy-start.2 = (s32[64]{0:T(128)S(1)}, s32[64]{0:T(128)}, u32[]{:S(2)}) copy-start(s32[64]{0:T(128)} %tallies_ref.3) | copy-start | bytes 772
  16.9 18.2 %all-to-all-start = ((f16[8,160,128]{2,1,0:T(8,128)(2,1)}), f16[8,160,128]{2,1,0:T(8,128)(2,1)S(1)}, u32[]{:S(2)}, u32[]{:S(2)}) async-start(f16[8,160,128]{2,1,0:T(8,128)(2,1)} %convert_element_type.31), calls=%async_computation | async-start | bytes 655360 | tf_op jit(solution)/shard_map/all_to_all | solution.py:441
  21.6 1.3 %copy-start.5 = (bf16[2,512]{1,0:T(2,128)(2,1)S(1)}, bf16[2,512]{1,0:T(2,128)(2,1)}, u32[]{:S(2)}) copy-start(bf16[2,512]{1,0:T(2,128)(2,1)} %param.10) | copy-start | bytes 6148
  21.6 1.3 %copy-start.6 = (bf16[2,512]{1,0:T(2,128)(2,1)S(1)}, bf16[2,512]{1,0:T(2,128)(2,1)}, u32[]{:S(2)}) copy-start(bf16[2,512]{1,0:T(2,128)(2,1)} %param.12) | copy-start | bytes 6148
  23.8 15.6 %collective-permute-start.1 = (bf16[514,512]{1,0:T(8,128)(2,1)}, bf16[514,512]{1,0:T(8,128)(2,1)S(1)}, u32[]{:S(2)}, u32[]{:S(2)}) collective-permute-start(bf16[514,512]{1,0:T(8,128)(2,1)} %pad_maximum_fusion), channel_id=1, source_target_pairs={{0,8},{8,0},{16,24},{24,16},{32,40},{40,32},{48,56},{56,48},{64,72... | collective-permute-start | bytes 1579016 | tf_op jit(solution)/shard_map/ppermute | solution.py:424
  35.9 17.1 %all-to-all-start.1 = ((f16[8,160,128]{2,1,0:T(8,128)(2,1)}), f16[8,160,128]{2,1,0:T(8,128)(2,1)S(1)}, u32[]{:S(2)}, u32[]{:S(2)}) async-start(f16[8,160,128]{2,1,0:T(8,128)(2,1)} %broadcast_in_dim.14), calls=%async_computation.1 | async-start | bytes 655360 | tf_op jit(solution)/shard_map/all_to_all | solution.py:408
  90.2 20.8 %copy-start.3 = (f32[512]{0:T(512)S(1)}, f32[512]{0:T(512)}, u32[]{:S(2)}) copy-start(f32[512]{0:T(512)} %param.13) | copy-start | bytes 6148
  90.2 20.8 %copy-start.4 = (f32[512]{0:T(512)S(1)}, f32[512]{0:T(512)}, u32[]{:S(2)}) copy-start(f32[512]{0:T(512)} %param.14) | copy-start | bytes 6148
  104.1 6.8 %collective-permute-start.2 = (f16[32,8,4,128]{3,2,1,0:T(4,128)(2,1)S(1)}, f16[32,8,4,128]{3,2,1,0:T(4,128)(2,1)S(1)}, u32[]{:S(2)}, u32[]{:S(2)}) collective-permute-start(f16[32,8,4,128]{3,2,1,0:T(4,128)(2,1)S(1)} %all_to_all.27), channel_id=1, source_target_pairs={{0,8},{8,0},{16,24},{24,16},{32,40},{40,32},{48,56},{56,48},{64,72... | collective-permute-start | bytes 786440 | tf_op jit(solution)/shard_map/ppermute | solution.py:451
  121.9 3.1 %collective-permute-start.3 = (f32[1,512]{1,0:T(1,128)S(1)}, f32[1,512]{1,0:T(1,128)S(1)}, u32[]{:S(2)}, u32[]{:S(2)}) collective-permute-start(f32[1,512]{1,0:T(1,128)S(1)} %get-tuple-element.24.dual_ref), channel_id=1, source_target_pairs={{0,8},{8,0},{16,24},{24,16},{32,40},{40,32},{48,56},{56,48},{64,72... | collective-permute-start | bytes 6152 | tf_op jit(solution)/shard_map/ppermute | solution.py:454

commit v8 on v7

--- a/solution.py
+++ b/solution.py
@@ -17,7 +17,6 @@
 WIDE_VMEM = 50 * 2**20
 SLABS = 16
 RHO_SCALE = 0.25
-STAGGER_NS = 1500
 
 
 def blocks_of(rows):
@@ -44,11 +43,6 @@
 
 
 def gram_kernel(slot, parts, w_ref, d_ref, out_ref, scaled_ref, g_ref):
-    if slot == 0:
-        @pl.when(lax.rem(lax.axis_index("scen"), 2) == 1)
-        def _():
-            pl.delay(STAGGER_NS)
-
     rows = w_ref.shape[0]
     tiles = [slice(i * B, (i + 1) * B) for i in range(rows // B)]
     scale = d_ref[...].astype(F32)[slot : slot + 1]
@@ -446,8 +440,11 @@
     same = [[2 * i + k for i in range(count)] for k in range(2)]
     terms = terms.reshape((n_s,) + terms.shape[2:])
     mine = lax.all_to_all(terms, "scen", 0, 0, axis_index_groups=[same[0] + same[1]])
-    wide = everyone(jnp.sum(mine, axis=0), "col", n_z)
-    half = everyone(wide.astype(F16), "scen", count, axis_index_groups=same)
+    rows_of = [[k * n_z + z for k in group for z in range(n_z)] for group in same]
+    half = everyone(
+        jnp.sum(mine, axis=0).astype(F16), ("scen", "col"), count * n_z, axis_index_groups=rows_of
+    )
+    half = half.reshape((count, n_z) + half.shape[1:])
     other = lax.ppermute(half, "scen", partner)
     first, dual = main_solve(half.astype(F32), other.astype(F32), q_diag[None], c_vec[None], g, link, b_row)
 

time: 127 us -> 124 us (0.976)
  blocking collectives: 49.4 us -> 44.9 us
  Pallas kernels: 18.9 us -> 22.7 us
  starting transfers between devices: 26.7 us -> 24.7 us
    all_to_all x1, blocking collectives: 26.6 us -> 21.1 us  [local(): lax.all_to_all(terms, 'scen', 0, 0, axis_index_groups=[same[0] + same[1]])]
    pallas_call x1, Pallas kernels: 1.4 us -> 6.75 us  [solve(): pl.pallas_call(solve_kernel, out_shape=(jax.ShapeDtypeStruct((SLABS, rows...]
    ppermute x1, starting transfers between devices: 5.65 us -> 2.98 us  [local(): other = lax.ppermute(half, 'scen', partner)]
    pallas_call x2, Pallas kernels: 4.53 us -> 3.01 us  [gram(): pl.pallas_call(functools.partial(gram_kernel, slot, parts), out_shape=jax...]
    all_to_all x2 -> x1, blocking collectives: 22.8 us -> 23.8 us  [everyone(): lax.all_to_all(jnp.broadcast_to(x[None], (count,) + x.shape), axis, 0, 0,...]
  transfers between devices with their start and end apart: 6 -> 6, of which waited for: 4 -> 5; matrix products, arithmetic and copies ran while one was open for 4% -> 4% of each run, Pallas kernels for 2% -> 1%
where the time goes in v8:
time: 124 us; the launch traced here: 123 us
  blocking collectives  44.9 us (36%)
  starting transfers between devices  24.7 us (20%)
  Pallas kernels  22.7 us (18%)
  waiting for transfers between devices  21.7 us (18%)
  local copies, waits for them, and re-layouts  4.69 us (4%)
  other arithmetic  2.34 us (2%)
  between operations  2.24 us (2%)
    all_to_all x1, blocking collectives, everyone(): lax.all_to_all(jnp.broadcast_to(x[None], (count,) + x.shape), axis, 0, 0,...  23.8 us
    all_to_all x1, blocking collectives, local(): lax.all_to_all(terms, 'scen', 0, 0, axis_index_groups=[same[0] + same[1]])  21.1 us
    all_to_all x1, waiting for transfers between devices, everyone(): lax.all_to_all(jnp.broadcast_to(x[None], (count,) + x.shape), axis, 0, 0,...  12.9 us
    pallas_call x1, Pallas kernels, main_solve(): pl.pallas_call(main_kernel, out_shape=(jax.ShapeDtypeStruct((1, n0), F32)...  10.8 us
    ppermute x1, starting transfers between devices, local(): gram_moved = lax.ppermute(gram1, 'scen', partner)  8.75 us
    all_to_all x1, waiting for transfers between devices, local(): received = lax.all_to_all(partial, 'col', 0, 0).astype(F32)  6.88 us
    pallas_call x1, Pallas kernels, solve(): pl.pallas_call(solve_kernel, out_shape=(jax.ShapeDtypeStruct((SLABS, rows...  6.75 us
    all_to_all x1, starting transfers between devices, local(): received = lax.all_to_all(partial, 'col', 0, 0).astype(F32)  4.69 us
  transfers between devices with their start and end apart: 6, of which 5 were waited for; matrix products, arithmetic and copies ran while one was open for 4% of the time, Pallas kernels for 1%

profile of v8, /device:TPU:1, one launch (start us, length us, event | category | flops | bytes accessed | tf_op | source)
XLA Modules:
  0.0 123.2 jit_solution(18177655779197380172)
XLA Ops:
  0.6 0.0 copy-start.1
  0.6 0.0 copy-start
  0.6 1.4 %slice_bitcast_fusion.1.w_ref = bf16[512,1024]{1,0:T(8,128)(2,1)S(1)} fusion(bf16[2,512,1024]{2,1,0:T(8,128)(2,1)} %w_ref.1), kind=kLoop, calls=%fused_computation.1 | loop fusion | bytes 2097152 | tf_op jit(solution)/shard_map/squeeze | solution.py:406
  2.1 0.0 copy-done.1
  2.1 1.5 %gram1.1 = f32[8,160,128]{2,1,0:T(8,128)S(1)} custom-call(bf16[512,1024]{1,0:T(8,128)(2,1)S(1)} %slice_bitcast_fusion.1.w_ref, bf16[2,1024]{1,0:T(2,128)(2,1)S(1)} %copy-done.1), custom_call_target="tpu_custom_call" | custom-call | tf_op jit(solution)/shard_map/gram1/pallas_call | solution.py:67
  3.6 8.7 %collective-permute-start = (f32[8,160,128]{2,1,0:T(8,128)S(1)}, f32[8,160,128]{2,1,0:T(8,128)S(1)}, u32[]{:S(2)}, u32[]{:S(2)}) collective-permute-start(f32[8,160,128]{2,1,0:T(8,128)S(1)} %gram1.1), channel_id=1, source_target_pairs={{0,8},{8,0},{16,24},{24,16},{32,40},{40,32},{48,56},{56,48},{64,72... | collective-permute-start | bytes 1966088 | tf_op jit(solution)/shard_map/ppermute | solution.py:408
  12.4 0.0 copy-done
  12.4 0.1 slice_bitcast_fusion.w_ref
  12.5 0.0 copy-start.2
  12.5 1.5 %gram0.1.own_ref = f32[8,160,128]{2,1,0:T(8,128)S(1)} custom-call(bf16[512,1024]{1,0:T(8,128)(2,1)S(1)} %slice_bitcast_fusion.w_ref, bf16[2,1024]{1,0:T(2,128)(2,1)S(1)} %copy-done.1), custom_call_target="tpu_custom_call" | custom-call | tf_op jit(solution)/shard_map/gram0/pallas_call | solution.py:67
  14.0 0.1 collective-permute-done.moved_ref
  14.1 0.0 copy-done.2
  14.1 0.6 choose.1
  14.7 0.8 convert_element_type.35
  15.5 4.7 %all-to-all-start = ((f16[8,160,128]{2,1,0:T(8,128)(2,1)}), f16[8,160,128]{2,1,0:T(8,128)(2,1)S(1)}, u32[]{:S(2)}, u32[]{:S(2)}) async-start(f16[8,160,128]{2,1,0:T(8,128)(2,1)} %convert_element_type.35), calls=%async_computation | async-start | bytes 655360 | tf_op jit(solution)/shard_map/all_to_all | solution.py:435
  20.2 0.0 copy-start.5
  20.2 0.0 copy-start.6
  20.2 1.3 %slice_bitcast_fusion.3 = (bf16[512,512]{1,0:T(8,128)(2,1)S(1)}, bf16[512,512]{1,0:T(8,128)(2,1)S(1)}) fusion(bf16[2,512,512]{2,1,0:T(8,128)(2,1)} %param.11), kind=kLoop, calls=%fused_computation.6 | loop fusion | bytes 2097152 | tf_op jit(solution)/shard_map/squeeze | solution.py:415
  21.5 0.0 copy-done.5
  21.5 0.0 copy-done.6
  21.5 0.8 pad_maximum_fusion
  22.3 2.5 %collective-permute-start.1 = (bf16[514,512]{1,0:T(8,128)(2,1)}, bf16[514,512]{1,0:T(8,128)(2,1)S(1)}, u32[]{:S(2)}, u32[]{:S(2)}) collective-permute-start(bf16[514,512]{1,0:T(8,128)(2,1)} %pad_maximum_fusion), channel_id=1, source_target_pairs={{0,8},{8,0},{16,24},{24,16},{32,40},{40,32},{48,56},{56,48},{64,72... | collective-permute-start | bytes 1579016 | tf_op jit(solution)/shard_map/ppermute | solution.py:418
  24.9 0.6 fusion.2
  26.8 0.1 pad.2.clone
  26.9 6.9 %all-to-all-done = f16[8,160,128]{2,1,0:T(8,128)(2,1)S(1)} async-done(((f16[8,160,128]{2,1,0:T(8,128)(2,1)}), f16[8,160,128]{2,1,0:T(8,128)(2,1)S(1)}, u32[]{:S(2)}, u32[]{:S(2)}) %all-to-all-start) | async-done | bytes 327712 | tf_op jit(solution)/shard_map/all_to_all | solution.py:435
  33.8 0.8 broadcast_in_dim.24
  34.6 3.4 %all-to-all-start.1 = ((f16[8,160,128]{2,1,0:T(8,128)(2,1)}), f16[8,160,128]{2,1,0:T(8,128)(2,1)S(1)}, u32[]{:S(2)}, u32[]{:S(2)}) async-start(f16[8,160,128]{2,1,0:T(8,128)(2,1)} %broadcast_in_dim.24), calls=%async_computation.1 | async-start | bytes 655360 | tf_op jit(solution)/shard_map/all_to_all | solution.py:402
  38.0 0.0 collective-permute-done.1
  38.0 0.1 maximum_select_fusion
  38.3 0.2 copy.11
  38.4 0.1 constant_dynamic-slice_fusion
  38.6 0.1 maximum_select_fusion.1.rhs_ref
  38.7 12.9 %all-to-all-done.1 = f16[8,160,128]{2,1,0:T(8,128)(2,1)S(1)} async-done(((f16[8,160,128]{2,1,0:T(8,128)(2,1)}), f16[8,160,128]{2,1,0:T(8,128)(2,1)S(1)}, u32[]{:S(2)}, u32[]{:S(2)}) %all-to-all-start.1) | async-done | bytes 327712 | tf_op jit(solution)/shard_map/all_to_all | solution.py:402
  51.6 6.7 %solve.1 = (f32[16,512,512]{2,1,0:T(8,128)}, f32[2,32,4,128]{3,2,1,0:T(4,128)S(1)}) custom-call(f32[8,160,128]{2,1,0:T(8,128)S(1)} %convert_element_type.38.recv_ref, f32[1,512]{1,0:T(1,128)S(1)} %get-tuple-element.31.reg_ref, bf16[512,128]{1,0:T(8,128)(2,1)S(1)} %maximum_select_fusion.1.rhs_ref, bf16[512,512]{1,0:T(8,128)(2,1)S(1)} %slice.46.link_ref), custom_call_target="tpu_custom_call" | custom-call | tf_op jit(solution)/shard_map/solve/pallas_call | solution.py:208
  58.4 21.1 %all_to_all.20 = f32[64,4,128]{2,1,0:T(4,128)S(1)} all-to-all(f32[64,4,128]{2,1,0:T(4,128)S(1)} %bitcast.17), channel_id=1, replica_groups={{0,16,32,48,64,80,96,112,128,144,160,176,192,208,224,240,256,272,288,30..., dimensions={0} | all-to-all | bytes 262144 | tf_op jit(solution)/shard_map/all_to_all | solution.py:442
  79.5 0.1 reduce_sum.19
  79.6 0.1 broadcast_in_dim.27
  79.6 0.0 copy-start.3
  79.7 0.0 copy-start.4
  79.7 23.8 %all_to_all.21 = f16[256,4,128]{2,1,0:T(4,128)(2,1)S(1)} all-to-all(f16[256,4,128]{2,1,0:T(4,128)(2,1)S(1)} %broadcast_in_dim.27), channel_id=1, replica_groups={{0,1,2,3,4,5,6,7,16,17,18,19,20,21,22,23,32,33,34,35,36,37,38,39,48,49,..., dimensions={0} | all-to-all | bytes 524288 | tf_op jit(solution)/shard_map/all_to_all | solution.py:402
  103.5 3.0 %collective-permute-start.2 = (f16[32,8,4,128]{3,2,1,0:T(4,128)(2,1)S(1)}, f16[32,8,4,128]{3,2,1,0:T(4,128)(2,1)S(1)}, u32[]{:S(2)}, u32[]{:S(2)}) collective-permute-start(f16[32,8,4,128]{3,2,1,0:T(4,128)(2,1)S(1)} %bitcast.20), channel_id=1, source_target_pairs={{0,8},{8,0},{16,24},{24,16},{32,40},{40,32},{48,56},{56,48},{64,72... | collective-permute-start | bytes 786440 | tf_op jit(solution)/shard_map/ppermute | solution.py:448
  106.5 0.1 convert_element_type.41.mine_ref
  106.6 1.0 collective-permute-done.2
  107.6 0.1 convert_element_type.42.other_ref
  107.7 0.0 copy-done.3
  107.7 0.0 copy-done.4
  107.8 10.8 %main_solve.1 = (f32[1,512]{1,0:T(1,128)}, f32[1,512]{1,0:T(1,128)S(1)}) custom-call(f32[32,8,4,128]{3,2,1,0:T(4,128)S(1)} %convert_element_type.41.mine_ref, f32[32,8,4,128]{3,2,1,0:T(4,128)S(1)} %convert_element_type.42.other_ref, f32[1,512]{1,0:T(1,128)S(1)} %bitcast.18, f32[1,512]{1,0:T(1,128)S(1)} %bitcast.19, f32[16,512,512]{2,1,0:T(8,128)} %get-tuple-element.22.g_hbm, ...), custom_call_target="tpu_custom_call" | custom-call | tf_op jit(solution)/shard_map/main_solve/pallas_call | solution.py:345
  118.6 2.3 %collective-permute-start.3 = (f32[1,512]{1,0:T(1,128)S(1)}, f32[1,512]{1,0:T(1,128)S(1)}, u32[]{:S(2)}, u32[]{:S(2)}) collective-permute-start(f32[1,512]{1,0:T(1,128)S(1)} %get-tuple-element.24.dual_ref), channel_id=1, source_target_pairs={{0,8},{8,0},{16,24},{24,16},{32,40},{40,32},{48,56},{56,48},{64,72... | collective-permute-start | bytes 6152 | tf_op jit(solution)/shard_map/ppermute | solution.py:451
  120.9 0.8 collective-permute-done.3.back_ref
  121.7 1.5 %primal.1 = (f32[2,512]{1,0:T(2,128)}, f32[2,1024]{1,0:T(2,128)}) custom-call(s32[64]{0:T(128)S(1)} %copy-done.2, bf16[2,512,1024]{2,1,0:T(8,128)(2,1)S(1)} %copy-done, bf16[2,1024]{1,0:T(2,128)(2,1)S(1)} %copy-done.1, f32[1,512]{1,0:T(1,128)S(1)} %get-tuple-element.24.dual_ref, f32[1,512]{1,0:T(1,128)S(1)} %collective-permute-done.3.back_ref), custom_call_target="tpu_custom_call" | custom-call | tf_op jit(solution)/shard_map/primal/pallas_call | solution.py:375
  (8 shorter events, 0.2 us)
Async XLA Ops:
  0.6 1.5 %copy-start.1 = (bf16[2,1024]{1,0:T(2,128)(2,1)S(1)}, bf16[2,1024]{1,0:T(2,128)(2,1)}, u32[]{:S(2)}) copy-start(bf16[2,1024]{1,0:T(2,128)(2,1)} %d_ref.5) | copy-start | bytes 12292
  0.6 11.7 %copy-start = (bf16[2,512,1024]{2,1,0:T(8,128)(2,1)S(1)}, bf16[2,512,1024]{2,1,0:T(8,128)(2,1)}, u32[]{:S(2)}) copy-start(bf16[2,512,1024]{2,1,0:T(8,128)(2,1)} %w_ref.1) | copy-start | bytes 6291460
  3.6 10.5 %collective-permute-start = (f32[8,160,128]{2,1,0:T(8,128)S(1)}, f32[8,160,128]{2,1,0:T(8,128)S(1)}, u32[]{:S(2)}, u32[]{:S(2)}) collective-permute-start(f32[8,160,128]{2,1,0:T(8,128)S(1)} %gram1.1), channel_id=1, source_target_pairs={{0,8},{8,0},{16,24},{24,16},{32,40},{40,32},{48,56},{56,48},{64,72... | collective-permute-start | bytes 1966088 | tf_op jit(solution)/shard_map/ppermute | solution.py:408
  12.5 1.6 %copy-start.2 = (s32[64]{0:T(128)S(1)}, s32[64]{0:T(128)}, u32[]{:S(2)}) copy-start(s32[64]{0:T(128)} %tallies_ref.3) | copy-start | bytes 772
  15.5 18.3 %all-to-all-start = ((f16[8,160,128]{2,1,0:T(8,128)(2,1)}), f16[8,160,128]{2,1,0:T(8,128)(2,1)S(1)}, u32[]{:S(2)}, u32[]{:S(2)}) async-start(f16[8,160,128]{2,1,0:T(8,128)(2,1)} %convert_element_type.35), calls=%async_computation | async-start | bytes 655360 | tf_op jit(solution)/shard_map/all_to_all | solution.py:435
  20.2 1.3 %copy-start.5 = (bf16[2,512]{1,0:T(2,128)(2,1)S(1)}, bf16[2,512]{1,0:T(2,128)(2,1)}, u32[]{:S(2)}) copy-start(bf16[2,512]{1,0:T(2,128)(2,1)} %param.10) | copy-start | bytes 6148
  20.2 1.3 %copy-start.6 = (bf16[2,512]{1,0:T(2,128)(2,1)S(1)}, bf16[2,512]{1,0:T(2,128)(2,1)}, u32[]{:S(2)}) copy-start(bf16[2,512]{1,0:T(2,128)(2,1)} %param.12) | copy-start | bytes 6148
  22.3 15.7 %collective-permute-start.1 = (bf16[514,512]{1,0:T(8,128)(2,1)}, bf16[514,512]{1,0:T(8,128)(2,1)S(1)}, u32[]{:S(2)}, u32[]{:S(2)}) collective-permute-start(bf16[514,512]{1,0:T(8,128)(2,1)} %pad_maximum_fusion), channel_id=1, source_target_pairs={{0,8},{8,0},{16,24},{24,16},{32,40},{40,32},{48,56},{56,48},{64,72... | collective-permute-start | bytes 1579016 | tf_op jit(solution)/shard_map/ppermute | solution.py:418
  34.6 17.0 %all-to-all-start.1 = ((f16[8,160,128]{2,1,0:T(8,128)(2,1)}), f16[8,160,128]{2,1,0:T(8,128)(2,1)S(1)}, u32[]{:S(2)}, u32[]{:S(2)}) async-start(f16[8,160,128]{2,1,0:T(8,128)(2,1)} %broadcast_in_dim.24), calls=%async_computation.1 | async-start | bytes 655360 | tf_op jit(solution)/shard_map/all_to_all | solution.py:402
  79.6 28.1 %copy-start.3 = (f32[512]{0:T(512)S(1)}, f32[512]{0:T(512)}, u32[]{:S(2)}) copy-start(f32[512]{0:T(512)} %param.13) | copy-start | bytes 6148
  79.7 28.1 %copy-start.4 = (f32[512]{0:T(512)S(1)}, f32[512]{0:T(512)}, u32[]{:S(2)}) copy-start(f32[512]{0:T(512)} %param.14) | copy-start | bytes 6148
  103.5 4.1 %collective-permute-start.2 = (f16[32,8,4,128]{3,2,1,0:T(4,128)(2,1)S(1)}, f16[32,8,4,128]{3,2,1,0:T(4,128)(2,1)S(1)}, u32[]{:S(2)}, u32[]{:S(2)}) collective-permute-start(f16[32,8,4,128]{3,2,1,0:T(4,128)(2,1)S(1)} %bitcast.20), channel_id=1, source_target_pairs={{0,8},{8,0},{16,24},{24,16},{32,40},{40,32},{48,56},{56,48},{64,72... | collective-permute-start | bytes 786440 | tf_op jit(solution)/shard_map/ppermute | solution.py:448
  118.6 3.1 %collective-permute-start.3 = (f32[1,512]{1,0:T(1,128)S(1)}, f32[1,512]{1,0:T(1,128)S(1)}, u32[]{:S(2)}, u32[]{:S(2)}) collective-permute-start(f32[1,512]{1,0:T(1,128)S(1)} %get-tuple-element.24.dual_ref), channel_id=1, source_target_pairs={{0,8},{8,0},{16,24},{24,16},{32,40},{40,32},{48,56},{56,48},{64,72... | collective-permute-start | bytes 6152 | tf_op jit(solution)/shard_map/ppermute | solution.py:451

commit v9 on v8

--- a/solution.py
+++ b/solution.py
@@ -363,12 +363,17 @@
     held = tallies_ref[lax.axis_index("scen")]
     scale = d_ref[...].astype(F32)
     for slot, source in enumerate((dual_ref, back_ref)):
-        dual = source[...]
-        dual = jnp.where(held > slot, dual, jnp.zeros_like(dual))
-        y_ref[slot : slot + 1, :] = dual
-        out_ref[slot : slot + 1, :] = scale[slot : slot + 1] * mm(
-            dual.astype(BF16), w_ref[slot]
-        )
+        at = slice(slot, slot + 1)
+
+        @pl.when(held > slot)
+        def _(slot=slot, source=source, at=at):
+            y_ref[at, :] = source[...]
+            out_ref[at, :] = scale[at] * mm(source[...].astype(BF16), w_ref[slot])
+
+        @pl.when(held <= slot)
+        def _(at=at):
+            y_ref[at, :] = jnp.zeros((1, y_ref.shape[1]), F32)
+            out_ref[at, :] = jnp.zeros((1, out_ref.shape[1]), F32)
 
 
 def primal(tallies, matrices, ratios, dual, back):

time: 124 us -> 124 us (level)
  no operation moved by 1% of the time
where the time goes in v9:
time: 124 us; the launch traced here: 123 us
  blocking collectives  44.4 us (36%)
  starting transfers between devices  24.7 us (20%)
  Pallas kernels  23.2 us (19%)
  waiting for transfers between devices  21.7 us (18%)
  local copies, waits for them, and re-layouts  4.69 us (4%)
  other arithmetic  2.34 us (2%)
  between operations  2.24 us (2%)
    all_to_all x1, blocking collectives, everyone(): lax.all_to_all(jnp.broadcast_to(x[None], (count,) + x.shape), axis, 0, 0,...  23.8 us
    all_to_all x1, blocking collectives, local(): lax.all_to_all(terms, 'scen', 0, 0, axis_index_groups=[same[0] + same[1]])  20.6 us
    all_to_all x1, waiting for transfers between devices, everyone(): lax.all_to_all(jnp.broadcast_to(x[None], (count,) + x.shape), axis, 0, 0,...  12.9 us
    pallas_call x1, Pallas kernels, main_solve(): pl.pallas_call(main_kernel, out_shape=(jax.ShapeDtypeStruct((1, n0), F32)...  11.2 us
    ppermute x1, starting transfers between devices, local(): gram_moved = lax.ppermute(gram1, 'scen', partner)  8.75 us
    pallas_call x1, Pallas kernels, solve(): pl.pallas_call(solve_kernel, out_shape=(jax.ShapeDtypeStruct((SLABS, rows...  7.26 us
    all_to_all x1, waiting for transfers between devices, local(): received = lax.all_to_all(partial, 'col', 0, 0).astype(F32)  6.88 us
    all_to_all x1, starting transfers between devices, local(): received = lax.all_to_all(partial, 'col', 0, 0).astype(F32)  4.69 us
  transfers between devices with their start and end apart: 6, of which 5 were waited for; matrix products, arithmetic and copies ran while one was open for 4% of the time, Pallas kernels for 1%

profile of v9, /device:TPU:1, one launch (start us, length us, event | category | flops | bytes accessed | tf_op | source)
XLA Modules:
  0.0 123.2 jit_solution(20814396485764582)
XLA Ops:
  0.6 0.0 copy-start.1
  0.6 0.0 copy-start
  0.6 1.4 %slice_bitcast_fusion.1.w_ref = bf16[512,1024]{1,0:T(8,128)(2,1)S(1)} fusion(bf16[2,512,1024]{2,1,0:T(8,128)(2,1)} %w_ref.1), kind=kLoop, calls=%fused_computation.1 | loop fusion | bytes 2097152 | tf_op jit(solution)/shard_map/squeeze | solution.py:411
  2.1 0.0 copy-done.1
  2.1 1.5 %gram1.1 = f32[8,160,128]{2,1,0:T(8,128)S(1)} custom-call(bf16[512,1024]{1,0:T(8,128)(2,1)S(1)} %slice_bitcast_fusion.1.w_ref, bf16[2,1024]{1,0:T(2,128)(2,1)S(1)} %copy-done.1), custom_call_target="tpu_custom_call" | custom-call | tf_op jit(solution)/shard_map/gram1/pallas_call | solution.py:67
  3.6 8.7 %collective-permute-start = (f32[8,160,128]{2,1,0:T(8,128)S(1)}, f32[8,160,128]{2,1,0:T(8,128)S(1)}, u32[]{:S(2)}, u32[]{:S(2)}) collective-permute-start(f32[8,160,128]{2,1,0:T(8,128)S(1)} %gram1.1), channel_id=1, source_target_pairs={{0,8},{8,0},{16,24},{24,16},{32,40},{40,32},{48,56},{56,48},{64,72... | collective-permute-start | bytes 1966088 | tf_op jit(solution)/shard_map/ppermute | solution.py:413
  12.4 0.0 copy-done
  12.4 0.1 slice_bitcast_fusion.w_ref
  12.5 0.0 copy-start.2
  12.5 1.5 %gram0.1.own_ref = f32[8,160,128]{2,1,0:T(8,128)S(1)} custom-call(bf16[512,1024]{1,0:T(8,128)(2,1)S(1)} %slice_bitcast_fusion.w_ref, bf16[2,1024]{1,0:T(2,128)(2,1)S(1)} %copy-done.1), custom_call_target="tpu_custom_call" | custom-call | tf_op jit(solution)/shard_map/gram0/pallas_call | solution.py:67
  14.0 0.1 collective-permute-done.moved_ref
  14.1 0.0 copy-done.2
  14.1 0.6 choose.1
  14.7 0.8 convert_element_type.35
  15.5 4.7 %all-to-all-start = ((f16[8,160,128]{2,1,0:T(8,128)(2,1)}), f16[8,160,128]{2,1,0:T(8,128)(2,1)S(1)}, u32[]{:S(2)}, u32[]{:S(2)}) async-start(f16[8,160,128]{2,1,0:T(8,128)(2,1)} %convert_element_type.35), calls=%async_computation | async-start | bytes 655360 | tf_op jit(solution)/shard_map/all_to_all | solution.py:440
  20.2 0.0 copy-start.5
  20.2 0.0 copy-start.6
  20.2 1.3 %slice_bitcast_fusion.3 = (bf16[512,512]{1,0:T(8,128)(2,1)S(1)}, bf16[512,512]{1,0:T(8,128)(2,1)S(1)}) fusion(bf16[2,512,512]{2,1,0:T(8,128)(2,1)} %param.11), kind=kLoop, calls=%fused_computation.6 | loop fusion | bytes 2097152 | tf_op jit(solution)/shard_map/squeeze | solution.py:420
  21.5 0.0 copy-done.5
  21.5 0.0 copy-done.6
  21.5 0.8 pad_maximum_fusion
  22.3 2.5 %collective-permute-start.1 = (bf16[514,512]{1,0:T(8,128)(2,1)}, bf16[514,512]{1,0:T(8,128)(2,1)S(1)}, u32[]{:S(2)}, u32[]{:S(2)}) collective-permute-start(bf16[514,512]{1,0:T(8,128)(2,1)} %pad_maximum_fusion), channel_id=1, source_target_pairs={{0,8},{8,0},{16,24},{24,16},{32,40},{40,32},{48,56},{56,48},{64,72... | collective-permute-start | bytes 1579016 | tf_op jit(solution)/shard_map/ppermute | solution.py:423
  24.9 0.6 fusion.2
  26.8 0.1 pad.2.clone
  26.9 6.9 %all-to-all-done = f16[8,160,128]{2,1,0:T(8,128)(2,1)S(1)} async-done(((f16[8,160,128]{2,1,0:T(8,128)(2,1)}), f16[8,160,128]{2,1,0:T(8,128)(2,1)S(1)}, u32[]{:S(2)}, u32[]{:S(2)}) %all-to-all-start) | async-done | bytes 327712 | tf_op jit(solution)/shard_map/all_to_all | solution.py:440
  33.8 0.8 broadcast_in_dim.24
  34.6 3.4 %all-to-all-start.1 = ((f16[8,160,128]{2,1,0:T(8,128)(2,1)}), f16[8,160,128]{2,1,0:T(8,128)(2,1)S(1)}, u32[]{:S(2)}, u32[]{:S(2)}) async-start(f16[8,160,128]{2,1,0:T(8,128)(2,1)} %broadcast_in_dim.24), calls=%async_computation.1 | async-start | bytes 655360 | tf_op jit(solution)/shard_map/all_to_all | solution.py:407
  38.0 0.0 collective-permute-done.1
  38.0 0.1 maximum_select_fusion
  38.3 0.2 copy.11
  38.4 0.1 constant_dynamic-slice_fusion
  38.6 0.1 maximum_select_fusion.1.rhs_ref
  38.7 12.9 %all-to-all-done.1 = f16[8,160,128]{2,1,0:T(8,128)(2,1)S(1)} async-done(((f16[8,160,128]{2,1,0:T(8,128)(2,1)}), f16[8,160,128]{2,1,0:T(8,128)(2,1)S(1)}, u32[]{:S(2)}, u32[]{:S(2)}) %all-to-all-start.1) | async-done | bytes 327712 | tf_op jit(solution)/shard_map/all_to_all | solution.py:407
  51.6 7.3 %solve.1 = (f32[16,512,512]{2,1,0:T(8,128)}, f32[2,32,4,128]{3,2,1,0:T(4,128)S(1)}) custom-call(f32[8,160,128]{2,1,0:T(8,128)S(1)} %convert_element_type.38.recv_ref, f32[1,512]{1,0:T(1,128)S(1)} %get-tuple-element.31.reg_ref, bf16[512,128]{1,0:T(8,128)(2,1)S(1)} %maximum_select_fusion.1.rhs_ref, bf16[512,512]{1,0:T(8,128)(2,1)S(1)} %slice.46.link_ref), custom_call_target="tpu_custom_call" | custom-call | tf_op jit(solution)/shard_map/solve/pallas_call | solution.py:208
  58.9 20.6 %all_to_all.20 = f32[64,4,128]{2,1,0:T(4,128)S(1)} all-to-all(f32[64,4,128]{2,1,0:T(4,128)S(1)} %bitcast.17), channel_id=1, replica_groups={{0,16,32,48,64,80,96,112,128,144,160,176,192,208,224,240,256,272,288,30..., dimensions={0} | all-to-all | bytes 262144 | tf_op jit(solution)/shard_map/all_to_all | solution.py:447
  79.5 0.1 reduce_sum.19
  79.6 0.1 broadcast_in_dim.27
  79.6 0.0 copy-start.3
  79.7 0.0 copy-start.4
  79.7 23.8 %all_to_all.21 = f16[256,4,128]{2,1,0:T(4,128)(2,1)S(1)} all-to-all(f16[256,4,128]{2,1,0:T(4,128)(2,1)S(1)} %broadcast_in_dim.27), channel_id=1, replica_groups={{0,1,2,3,4,5,6,7,16,17,18,19,20,21,22,23,32,33,34,35,36,37,38,39,48,49,..., dimensions={0} | all-to-all | bytes 524288 | tf_op jit(solution)/shard_map/all_to_all | solution.py:407
  103.5 3.0 %collective-permute-start.2 = (f16[32,8,4,128]{3,2,1,0:T(4,128)(2,1)S(1)}, f16[32,8,4,128]{3,2,1,0:T(4,128)(2,1)S(1)}, u32[]{:S(2)}, u32[]{:S(2)}) collective-permute-start(f16[32,8,4,128]{3,2,1,0:T(4,128)(2,1)S(1)} %bitcast.20), channel_id=1, source_target_pairs={{0,8},{8,0},{16,24},{24,16},{32,40},{40,32},{48,56},{56,48},{64,72... | collective-permute-start | bytes 786440 | tf_op jit(solution)/shard_map/ppermute | solution.py:453
  106.5 0.1 convert_element_type.41.mine_ref
  106.6 1.0 collective-permute-done.2
  107.6 0.1 convert_element_type.42.other_ref
  107.7 0.0 copy-done.3
  107.7 0.0 copy-done.4
  107.8 11.2 %main_solve.1 = (f32[1,512]{1,0:T(1,128)}, f32[1,512]{1,0:T(1,128)S(1)}) custom-call(f32[32,8,4,128]{3,2,1,0:T(4,128)S(1)} %convert_element_type.41.mine_ref, f32[32,8,4,128]{3,2,1,0:T(4,128)S(1)} %convert_element_type.42.other_ref, f32[1,512]{1,0:T(1,128)S(1)} %bitcast.18, f32[1,512]{1,0:T(1,128)S(1)} %bitcast.19, f32[16,512,512]{2,1,0:T(8,128)} %get-tuple-element.22.g_hbm, ...), custom_call_target="tpu_custom_call" | custom-call | tf_op jit(solution)/shard_map/main_solve/pallas_call | solution.py:345
  118.9 2.3 %collective-permute-start.3 = (f32[1,512]{1,0:T(1,128)S(1)}, f32[1,512]{1,0:T(1,128)S(1)}, u32[]{:S(2)}, u32[]{:S(2)}) collective-permute-start(f32[1,512]{1,0:T(1,128)S(1)} %get-tuple-element.24.dual_ref), channel_id=1, source_target_pairs={{0,8},{8,0},{16,24},{24,16},{32,40},{40,32},{48,56},{56,48},{64,72... | collective-permute-start | bytes 6152 | tf_op jit(solution)/shard_map/ppermute | solution.py:456
  121.2 0.8 collective-permute-done.3.back_ref
  122.0 1.2 primal.1
  (8 shorter events, 0.2 us)
Async XLA Ops:
  0.6 1.5 %copy-start.1 = (bf16[2,1024]{1,0:T(2,128)(2,1)S(1)}, bf16[2,1024]{1,0:T(2,128)(2,1)}, u32[]{:S(2)}) copy-start(bf16[2,1024]{1,0:T(2,128)(2,1)} %d_ref.5) | copy-start | bytes 12292
  0.6 11.7 %copy-start = (bf16[2,512,1024]{2,1,0:T(8,128)(2,1)S(1)}, bf16[2,512,1024]{2,1,0:T(8,128)(2,1)}, u32[]{:S(2)}) copy-start(bf16[2,512,1024]{2,1,0:T(8,128)(2,1)} %w_ref.1) | copy-start | bytes 6291460
  3.6 10.5 %collective-permute-start = (f32[8,160,128]{2,1,0:T(8,128)S(1)}, f32[8,160,128]{2,1,0:T(8,128)S(1)}, u32[]{:S(2)}, u32[]{:S(2)}) collective-permute-start(f32[8,160,128]{2,1,0:T(8,128)S(1)} %gram1.1), channel_id=1, source_target_pairs={{0,8},{8,0},{16,24},{24,16},{32,40},{40,32},{48,56},{56,48},{64,72... | collective-permute-start | bytes 1966088 | tf_op jit(solution)/shard_map/ppermute | solution.py:413
  12.5 1.6 %copy-start.2 = (s32[64]{0:T(128)S(1)}, s32[64]{0:T(128)}, u32[]{:S(2)}) copy-start(s32[64]{0:T(128)} %tallies_ref.3) | copy-start | bytes 772
  15.5 18.3 %all-to-all-start = ((f16[8,160,128]{2,1,0:T(8,128)(2,1)}), f16[8,160,128]{2,1,0:T(8,128)(2,1)S(1)}, u32[]{:S(2)}, u32[]{:S(2)}) async-start(f16[8,160,128]{2,1,0:T(8,128)(2,1)} %convert_element_type.35), calls=%async_computation | async-start | bytes 655360 | tf_op jit(solution)/shard_map/all_to_all | solution.py:440
  20.2 1.3 %copy-start.5 = (bf16[2,512]{1,0:T(2,128)(2,1)S(1)}, bf16[2,512]{1,0:T(2,128)(2,1)}, u32[]{:S(2)}) copy-start(bf16[2,512]{1,0:T(2,128)(2,1)} %param.10) | copy-start | bytes 6148
  20.2 1.3 %copy-start.6 = (bf16[2,512]{1,0:T(2,128)(2,1)S(1)}, bf16[2,512]{1,0:T(2,128)(2,1)}, u32[]{:S(2)}) copy-start(bf16[2,512]{1,0:T(2,128)(2,1)} %param.12) | copy-start | bytes 6148
  22.3 15.7 %collective-permute-start.1 = (bf16[514,512]{1,0:T(8,128)(2,1)}, bf16[514,512]{1,0:T(8,128)(2,1)S(1)}, u32[]{:S(2)}, u32[]{:S(2)}) collective-permute-start(bf16[514,512]{1,0:T(8,128)(2,1)} %pad_maximum_fusion), channel_id=1, source_target_pairs={{0,8},{8,0},{16,24},{24,16},{32,40},{40,32},{48,56},{56,48},{64,72... | collective-permute-start | bytes 1579016 | tf_op jit(solution)/shard_map/ppermute | solution.py:423
  34.6 17.0 %all-to-all-start.1 = ((f16[8,160,128]{2,1,0:T(8,128)(2,1)}), f16[8,160,128]{2,1,0:T(8,128)(2,1)S(1)}, u32[]{:S(2)}, u32[]{:S(2)}) async-start(f16[8,160,128]{2,1,0:T(8,128)(2,1)} %broadcast_in_dim.24), calls=%async_computation.1 | async-start | bytes 655360 | tf_op jit(solution)/shard_map/all_to_all | solution.py:407
  79.6 28.1 %copy-start.3 = (f32[512]{0:T(512)S(1)}, f32[512]{0:T(512)}, u32[]{:S(2)}) copy-start(f32[512]{0:T(512)} %param.13) | copy-start | bytes 6148
  79.7 28.1 %copy-start.4 = (f32[512]{0:T(512)S(1)}, f32[512]{0:T(512)}, u32[]{:S(2)}) copy-start(f32[512]{0:T(512)} %param.14) | copy-start | bytes 6148
  103.5 4.1 %collective-permute-start.2 = (f16[32,8,4,128]{3,2,1,0:T(4,128)(2,1)S(1)}, f16[32,8,4,128]{3,2,1,0:T(4,128)(2,1)S(1)}, u32[]{:S(2)}, u32[]{:S(2)}) collective-permute-start(f16[32,8,4,128]{3,2,1,0:T(4,128)(2,1)S(1)} %bitcast.20), channel_id=1, source_target_pairs={{0,8},{8,0},{16,24},{24,16},{32,40},{40,32},{48,56},{56,48},{64,72... | collective-permute-start | bytes 786440 | tf_op jit(solution)/shard_map/ppermute | solution.py:453
  118.9 3.1 %collective-permute-start.3 = (f32[1,512]{1,0:T(1,128)S(1)}, f32[1,512]{1,0:T(1,128)S(1)}, u32[]{:S(2)}, u32[]{:S(2)}) collective-permute-start(f32[1,512]{1,0:T(1,128)S(1)} %get-tuple-element.24.dual_ref), channel_id=1, source_target_pairs={{0,8},{8,0},{16,24},{24,16},{32,40},{40,32},{48,56},{56,48},{64,72... | collective-permute-start | bytes 6152 | tf_op jit(solution)/shard_map/ppermute | solution.py:456
